TPU v7x, 32 devices: a whole 2x2x4 slice. The times are simulated.
32 devices in a mesh: groups: 2 (over x), seq: 16 (over z, y, core).
Axes of the slice: x: 2, y: 2, z: 4, core: 2. Of those that a mesh axis runs over, the one named last changes fastest.
Arguments:
- grad_out: bfloat16 [4096, 4096], P(None, ('groups', 'seq')), parts along dimension 1, may hold values from -6 to 6
- query: bfloat16 [4096, 4096], P(None, ('groups', 'seq')), parts along dimension 1, may hold values from -6 to 6
- key: bfloat16 [4096, 4096], P(None, ('groups', 'seq')), parts along dimension 1, may hold values from -6 to 6
- value: bfloat16 [4096, 4096], P(None, ('groups', 'seq')), parts along dimension 1, may hold values from -6 to 6
- conv_out: bfloat16 [4096, 4096], P(None, ('groups', 'seq')), parts along dimension 1, may hold values from -6 to 6
- channel_filter: int32 [4096], replicated, may hold values from 0 to 127, as said below
- decay_rate: float32 [128, 16], replicated, may hold values from 0.01 to 68
- twist: float32 [128, 16], replicated, may hold values from -3 to 3
- residues: float32 [2, 128, 16], replicated, may hold values from -1.5 to 1.5
Outputs:
- grad_query: bfloat16 [4096, 4096], P(None, ('groups', 'seq')), parts along dimension 1
- grad_key: bfloat16 [4096, 4096], P(None, ('groups', 'seq')), parts along dimension 1
- grad_value: bfloat16 [4096, 4096], P(None, ('groups', 'seq')), parts along dimension 1
- grad_log_rate: float32 [256, 16], P('groups'), parts along dimension 0
- grad_twist: float32 [256, 16], P('groups'), parts along dimension 0
- grad_residues: float32 [4, 128, 16], P('groups'), parts along dimension 0
There are 2 independent parts, one for each index of `groups`. A program takes and returns all parts, laid end to end along the dimension named above; an argument that names none is the same for every part. Nothing has to cross between parts.
Inputs may be any that keep to these rules, and one draw needn't show every extreme that they name: `channel_filter`: each of the 128 filters is used by exactly 32 channels.
All inputs are finite; a program needn't handle non-finite values.
Results may differ from a plain program's by a relative error of at most 0.0051.
Values sent between devices are 32-bit elements; how exact they have to be, the bound alone decides.
No kernel may reach another device: no remote copies, remote signals or barrier semaphores. Data moves between devices by JAX's collectives and lax.ppermute only.
A program may use at most 384 MiB of HBM per device.

v0:
```python
import jax
import jax.numpy as jnp
from jax import lax
from jax.sharding import PartitionSpec as P


def prefix(value, axis, join, neutral):
    count, mine = (lax.axis_size(axis), lax.axis_index(axis))
    pieces = jax.tree.map(lambda part: lax.all_gather(part, axis), value)
    pieces = jax.tree.map(lambda part: part[::-1], pieces)
    mine = count - 1 - mine
    total = jax.tree.map(
        lambda part, zero: jnp.full_like(part, 0) + jnp.asarray(zero, part.dtype), value, neutral
    )

    def turn(position, total):
        longer = join(total, jax.tree.map(lambda part: part[position], pieces))
        return jax.tree.map(lambda new, old: jnp.where(position < mine, new, old), longer, total)

    return lax.fori_loop(0, count - 1, turn, total)


def complex_product(a_real, a_imag, b_real, b_imag):
    return (a_real * b_real - a_imag * b_imag, a_real * b_imag + a_imag * b_real)


def mode_tables(decay_rate, twist, residues, length):
    rho = decay_rate / length
    angle = twist * rho
    scale = jnp.sqrt(1.0 - jnp.exp(-2.0 * rho))
    return (rho, angle, residues[0] * scale, residues[1] * scale)


def param_grads(decay_rate, twist, residues, length, a_real, a_imag, w_real, w_imag):
    rho_fixed, angle_fixed, res_real, res_imag = mode_tables(decay_rate, twist, residues, length)
    rw_real, rw_imag = complex_product(res_real, res_imag, w_real, w_imag)

    def objective(log_rate, twist_val, residue_val):
        rho, angle, rr_val, ri_val = mode_tables(jnp.exp(log_rate), twist_val, residue_val, length)
        magnitude = jnp.exp(-rho)
        first = jnp.sum(rr_val * a_real - ri_val * a_imag)
        second = jnp.sum(
            rw_real * magnitude * jnp.cos(angle) - rw_imag * magnitude * jnp.sin(angle)
        )
        return first + second

    return jax.grad(objective, argnums=(0, 1, 2))(jnp.log(decay_rate), twist, residues)


def power_table(rho, angle, steps):
    magnitude = jnp.exp(-rho[:, :, None] * steps[None, None, :])
    phase = angle[:, :, None] * steps[None, None, :]
    return (magnitude * jnp.cos(phase), magnitude * jnp.sin(phase))


def widen(values, states):
    return jnp.repeat(values, states.shape[1] // values.shape[1], axis=1)


def backward_full_combine(earlier, later):
    pe_real, pe_imag, qe_real, qe_imag, ye_real, ye_imag, ve_real, ve_imag = earlier
    pl_real, pl_imag, ql_real, ql_imag, yl_real, yl_imag, vl_real, vl_imag = later
    p_real, p_imag = complex_product(pl_real, pl_imag, pe_real, pe_imag)
    q1_real, q1_imag = complex_product(pl_real, pl_imag, qe_real, qe_imag)
    q2_real, q2_imag = complex_product(ql_real, ql_imag, pe_real, pe_imag)
    wide_p_real, wide_p_imag = (widen(pl_real, ye_real), widen(pl_imag, ye_real))
    wide_q_real, wide_q_imag = (widen(ql_real, ye_real), widen(ql_imag, ye_real))
    py_real, py_imag = complex_product(wide_p_real, wide_p_imag, ye_real, ye_imag)
    qy_real, qy_imag = complex_product(wide_q_real, wide_q_imag, ye_real, ye_imag)
    pv_real, pv_imag = complex_product(wide_p_real, wide_p_imag, ve_real, ve_imag)
    return (
        p_real,
        p_imag,
        q1_real + q2_real,
        q1_imag + q2_imag,
        yl_real + py_real,
        yl_imag + py_imag,
        vl_real + qy_real + pv_real,
        vl_imag + qy_imag + pv_imag,
    )


def mode_sum(table_real, table_imag, data):
    highest = lax.Precision.HIGHEST
    out_real = jnp.einsum("fmt,fst->sfm", data, table_real, precision=highest)
    out_imag = jnp.einsum("fmt,fst->sfm", data, table_imag, precision=highest)
    return (out_real.reshape(out_real.shape[0], -1), out_imag.reshape(out_imag.shape[0], -1))


def body(grad_out, query, key, value, conv_out, channel_filter, decay_rate, twist, residues):
    highest = lax.Precision.HIGHEST
    channels, positions = grad_out.shape
    filters, modes_count = decay_rate.shape
    members = channels // filters
    length = positions * lax.axis_size("seq")
    grad_query = (grad_out.astype(jnp.float32) * conv_out.astype(jnp.float32)).astype(jnp.bfloat16)
    mixed = (key.astype(jnp.float32) * value.astype(jnp.float32)).astype(jnp.bfloat16)
    gate_grad = (grad_out.astype(jnp.float32) * query.astype(jnp.float32)).astype(jnp.bfloat16)
    order = jnp.argsort(channel_filter, stable=True)
    mixed_grouped = mixed[order].reshape(filters, members, positions)
    gate_grouped = gate_grad[order].reshape(filters, members, positions)
    mixed_wide = mixed_grouped.astype(jnp.float32)
    gate_wide = gate_grouped.astype(jnp.float32)
    rho, angle, res_real, res_imag = mode_tables(decay_rate, twist, residues, length)
    steps = jnp.arange(positions, dtype=jnp.float32)
    head_real, head_imag = power_table(rho, angle, steps)
    shift_real, shift_imag = power_table(rho, angle, steps - 1.0)
    der_real = steps * shift_real
    der_imag = steps * shift_imag
    reverse_steps = positions - 1.0 - steps
    back_real, back_imag = power_table(rho, angle, reverse_steps)
    rshift_real, rshift_imag = power_table(rho, angle, reverse_steps - 1.0)
    span = float(positions)
    block_mag = jnp.exp(-rho * span)
    block_real = (block_mag * jnp.cos(angle * span)).T
    block_imag = (block_mag * jnp.sin(angle * span)).T
    slope_mag = span * jnp.exp(-rho * (span - 1.0))
    slope_real = (slope_mag * jnp.cos(angle * (span - 1.0))).T
    slope_imag = (slope_mag * jnp.sin(angle * (span - 1.0))).T
    filt = jnp.sum(res_real[:, :, None] * head_real - res_imag[:, :, None] * head_imag, axis=1)
    rows = jnp.arange(positions, dtype=jnp.int32)
    lag_index = rows[:, None] - rows[None, :]
    causal = lag_index >= 0
    toeplitz = jnp.where(causal[None], jnp.take(filt, jnp.maximum(lag_index, 0), axis=1), 0.0)
    grad_local = jnp.einsum("ftj,fmt->fmj", toeplitz, gate_wide, precision=highest)
    y_real, y_imag = mode_sum(head_real, head_imag, gate_wide)
    v_real, v_imag = mode_sum(der_real, der_imag, gate_wide)
    x_real, x_imag = mode_sum(back_real, back_imag, mixed_wide)
    w_real, w_imag = mode_sum(reverse_steps * rshift_real, reverse_steps * rshift_imag, mixed_wide)
    corr = jnp.einsum(
        "fmt,fmj->ftj", gate_grouped, mixed_grouped, preferred_element_type=jnp.float32
    )
    lower = jnp.where(causal[None], corr, 0.0)
    grow = jnp.exp(rho[:, :, None] * steps[None, None, :])
    inv_real = grow * jnp.cos(angle[:, :, None] * steps[None, None, :])
    inv_imag = -grow * jnp.sin(angle[:, :, None] * steps[None, None, :])
    table = jnp.concatenate([inv_real, inv_imag, steps * inv_real, steps * inv_imag], axis=1)
    inner = jnp.einsum("ftj,fkj->fkt", lower, table, precision=highest)
    ia_real = inner[:, :modes_count]
    ia_imag = inner[:, modes_count : 2 * modes_count]
    ib_real = inner[:, 2 * modes_count : 3 * modes_count]
    ib_imag = inner[:, 3 * modes_count :]
    la_real, la_imag = complex_product(head_real, head_imag, ia_real, ia_imag)
    local_a_real = jnp.sum(la_real, axis=2)
    local_a_imag = jnp.sum(la_imag, axis=2)
    lw_real, lw_imag = complex_product(
        shift_real, shift_imag, steps * ia_real - ib_real, steps * ia_imag - ib_imag
    )
    local_w_real = jnp.sum(lw_real, axis=2)
    local_w_imag = jnp.sum(lw_imag, axis=2)
    pole_real = widen(head_real[:, :, 1].T, y_real)
    pole_imag = widen(head_imag[:, :, 1].T, y_real)
    zeros_modes = jnp.zeros_like(block_real)
    ones_modes = jnp.ones_like(block_real)
    zeros_states = jnp.zeros_like(y_real)
    back = prefix(
        (block_real, block_imag, slope_real, slope_imag, y_real, y_imag, v_real, v_imag),
        "seq",
        backward_full_combine,
        (
            ones_modes,
            zeros_modes,
            zeros_modes,
            zeros_modes,
            zeros_states,
            zeros_states,
            zeros_states,
            zeros_states,
        ),
    )
    yin_real, yin_imag, vin_real, vin_imag = (back[4], back[5], back[6], back[7])
    px_real, px_imag = complex_product(pole_real, pole_imag, x_real, x_imag)
    ca_real, ca_imag = complex_product(px_real, px_imag, yin_real, yin_imag)
    pw_real, pw_imag = complex_product(pole_real, pole_imag, w_real, w_imag)
    c1_real, c1_imag = complex_product(pw_real + x_real, pw_imag + x_imag, yin_real, yin_imag)
    c2_real, c2_imag = complex_product(px_real, px_imag, vin_real, vin_imag)
    cw_real, cw_imag = (c1_real + c2_real, c1_imag + c2_imag)
    tail_real, tail_imag = power_table(rho, angle, span - steps)
    coef_real, coef_imag = complex_product(
        res_real[:, :, None], res_imag[:, :, None], tail_real, tail_imag
    )
    yin_real_g = yin_real.reshape(modes_count, filters, members)
    yin_imag_g = yin_imag.reshape(modes_count, filters, members)
    grad_cross = jnp.einsum("sfm,fsj->fmj", yin_real_g, coef_real, precision=highest) - jnp.einsum(
        "sfm,fsj->fmj", yin_imag_g, coef_imag, precision=highest
    )
    grad_grouped = (grad_local + grad_cross).reshape(channels, positions)
    conv_grad = jnp.zeros((channels, positions), jnp.float32).at[order].set(grad_grouped)
    grad_key = (conv_grad * value.astype(jnp.float32)).astype(jnp.bfloat16)
    grad_value = (conv_grad * key.astype(jnp.float32)).astype(jnp.bfloat16)

    def fold_members(values):
        return jnp.sum(values.reshape(modes_count, filters, members), axis=2).T

    part_a_real = local_a_real + fold_members(ca_real)
    part_a_imag = local_a_imag + fold_members(ca_imag)
    part_w_real = local_w_real + fold_members(cw_real)
    part_w_imag = local_w_imag + fold_members(cw_imag)
    total_a_real, total_a_imag, total_w_real, total_w_imag = lax.psum(
        (part_a_real, part_a_imag, part_w_real, part_w_imag), "seq"
    )
    grad_log_rate, grad_twist, grad_residues = param_grads(
        decay_rate, twist, residues, length, total_a_real, total_a_imag, total_w_real, total_w_imag
    )
    return (grad_query, grad_key, grad_value, grad_log_rate, grad_twist, grad_residues)


def solution(mesh):
    placed = (
        P(None, ("groups", "seq")),
        P(None, ("groups", "seq")),
        P(None, ("groups", "seq")),
        P(None, ("groups", "seq")),
        P(None, ("groups", "seq")),
        P(),
        P(),
        P(),
        P(),
    )
    return jax.shard_map(
        body,
        mesh=mesh,
        in_specs=placed,
        out_specs=(
            P(None, ("groups", "seq")),
            P(None, ("groups", "seq")),
            P(None, ("groups", "seq")),
            P("groups", None),
            P("groups", None),
            P("groups", None, None),
        ),
        check_vma=False,
    )
```

profile of v0, /device:TPU:0, one launch (start us, length us, event | category | flops | bytes accessed | tf_op | source)
XLA Modules:
  0.0 564.3 jit_solution(12893681685276480238)
XLA Ops:
  9.1 6.5 %sort.17 = (s32[4096]{0:T(1024)}, s32[4096]{0:T(1024)S(1)}) sort(s32[4096]{0:T(1024)} %param.16, s32[4096]{0:T(1024)S(1)} %iota.65), dimensions={0}, to_apply=%region_0.0 | sort | flops 49152 | bytes 65536 | tf_op jit(solution)/shard_map/jit(argsort)/sort | solution.py:99
  16.2 3.3 fusion.18
  19.5 12.1 %gather_fusion = bf16[4096,128]{1,0:T(8,128)(2,1)S(1)} fusion(bf16[4096,128]{1,0:T(8,128)(2,1)S(1)} %get-tuple-element.367, s32[4096]{0:T(1024)S(1)} %get-tuple-element.383), kind=kCustom, calls=%fused_computation | custom fusion | bytes 2113536 | tf_op jit(solution)/shard_map/gather | solution.py:101
  31.6 5.0 convolution_bitcast_fusion.5
  38.4 5.0 convolution_bitcast_fusion.4
  45.0 6.3 %convolution_bitcast_fusion.7 = f32[16,128,32]{2,0,1:T(8,128)S(1)} fusion(bf16[128,32,128]{2,1,0:T(8,128)(2,1)S(1)} %bitcast.129, f32[128,16]{1,0:T(8,128)S(1)} %copy.142, f32[128,16]{1,0:T(8,128)S(1)} %copy.141), kind=kOutput, calls=%fused_computation.56 | convolution fusion | flops 101449728 | bytes 1327104 | tf_op jit(solution)/shard_map/fmt,fst->sfm/dot_general | solution.py:85
  53.0 6.3 %convolution_bitcast_fusion.6 = f32[16,128,32]{2,0,1:T(8,128)S(1)} fusion(bf16[128,32,128]{2,1,0:T(8,128)(2,1)S(1)} %bitcast.130, f32[128,16]{1,0:T(8,128)S(1)} %copy.142, f32[128,16]{1,0:T(8,128)S(1)} %copy.141), kind=kOutput, calls=%fused_computation.55 | convolution fusion | flops 101449728 | bytes 1327104 | tf_op jit(solution)/shard_map/fmt,fst->sfm/dot_general | solution.py:86
  60.9 23.9 %all-gather = f32[256,128]{1,0:T(8,128)S(1)} all-gather(f32[16,128]{1,0:T(8,128)S(1)} %get-tuple-element.382), channel_id=2, replica_groups=mesh['groups'=2,'seq'=16] {'seq'}, dimensions={0}, use_global_device_ids=true | all-gather | bytes 139264 | tf_op jit(solution)/shard_map/all_gather | solution.py:9
  85.5 17.8 %all-gather.1 = f32[256,128]{1,0:T(8,128)S(1)} all-gather(f32[16,128]{1,0:T(8,128)S(1)} %get-tuple-element.381), channel_id=3, replica_groups=mesh['groups'=2,'seq'=16] {'seq'}, dimensions={0}, use_global_device_ids=true | all-gather | bytes 139264 | tf_op jit(solution)/shard_map/all_gather | solution.py:9
  104.1 19.1 %all-gather.2 = f32[256,128]{1,0:T(8,128)S(1)} all-gather(f32[16,128]{1,0:T(8,128)S(1)} %get-tuple-element.380), channel_id=4, replica_groups=mesh['groups'=2,'seq'=16] {'seq'}, dimensions={0}, use_global_device_ids=true | all-gather | bytes 139264 | tf_op jit(solution)/shard_map/all_gather | solution.py:9
  123.8 18.4 %all-gather.3 = f32[256,128]{1,0:T(8,128)S(1)} all-gather(f32[16,128]{1,0:T(8,128)S(1)} %get-tuple-element.353), channel_id=5, replica_groups=mesh['groups'=2,'seq'=16] {'seq'}, dimensions={0}, use_global_device_ids=true | all-gather | bytes 139264 | tf_op jit(solution)/shard_map/all_gather | solution.py:9
  142.9 1.9 fusion.21
  144.8 15.0 %gather_fusion.2 = bf16[4096,128]{1,0:T(8,128)(2,1)} fusion(bf16[4096,128]{1,0:T(8,128)(2,1)S(1)} %fusion.21, s32[4096]{0:T(1024)S(1)} %get-tuple-element.383), kind=kCustom, calls=%fused_computation.2 | custom fusion | bytes 2113536 | tf_op jit(solution)/shard_map/gather | solution.py:100
  160.7 4.5 fusion.39
  166.6 16.8 %fusion.6 = f32[128,64,128]{2,1,0:T(8,128)S(1)} fusion(f32[128,128,128]{2,1,0:T(8,128)S(1)} %fusion.117, f32[128,16,128]{2,1,0:T(8,128)S(1)} %get-tuple-element.372, f32[128,16,128]{2,1,0:T(8,128)S(1)} %get-tuple-element.373, f32[128,16,128]{2,1,0:T(8,128)S(1)} %get-tuple-element.374, f32[128,16,128]{2,1,0:T(8,128)S(1)} %get-tuple-element.371, ...), kind=kOutput, calls=%fused_computation.19 | convolution fusion | flops 1615855616 | bytes 16793600 | tf_op jit(solution)/shard_map/ftj,fkj->fkt/dot_general | solution.py:138
  183.4 12.1 %subtract_reduce_fusion.1 = (f32[128,16]{1,0:T(8,128)}, f32[128,16]{1,0:T(8,128)}, f32[128,16]{1,0:T(8,128)}, f32[128,16]{1,0:T(8,128)}, f32[128,128]{1,0:T(8,12...) fusion(f32[128]{0:T(128)S(1)} %copy-done.27, f32[128,16]{1,0:T(8,128)S(1)} %copy.142, f32[128,16]{1,0:T(8,128)S(1)} %copy.141, ...), kind=kLoop, calls=%fused_computation.74 | loop fusion | flops 8364032 | bytes 6423040 | tf_op jit(solution)/shard_map/reduce_sum | solution.py:149
  196.8 1.6 copy.153
  199.8 1.7 reshape.158
  201.5 2.5 slice.47
  204.0 2.3 copy.155
  206.3 2.0 broadcast_in_dim.129
  208.3 2.4 reshape.160
  211.7 5.0 convolution_bitcast_fusion.1
  218.0 2.4 reshape.162
  220.4 5.8 %convolution_bitcast_fusion = f32[16,128,32]{2,0,1:T(8,128)S(1)} fusion(bf16[128,32,128]{2,1,0:T(8,128)(2,1)S(1)} %bitcast.135, f32[128]{0:T(128)} %copy-done.28, f32[128,16]{1,0:T(8,128)S(1)} %copy.142, f32[128,16]{1,0:T(8,128)S(1)} %copy.141), kind=kOutput, calls=%fused_computation.49 | convolution fusion | flops 101449728 | bytes 1327616 | tf_op jit(solution)/shard_map/fmt,fst->sfm/dot_general | solution.py:86
  227.5 2.4 reshape.163
  229.9 1.5 copy.161
  231.4 5.6 convolution_bitcast_fusion.3
  238.3 2.4 reshape.159
  240.8 6.1 %convolution_bitcast_fusion.2 = f32[16,128,32]{2,0,1:T(8,128)S(1)} fusion(bf16[128,32,128]{2,1,0:T(8,128)(2,1)S(1)} %bitcast.137, f32[128]{0:T(128)} %get-tuple-element.391, f32[128]{0:T(128)} %copy-done.28, f32[128,16]{1,0:T(8,128)S(1)} %copy.142, f32[128,16]{1,0:T(8,128)S(1)} %copy.141), kind=kOutput, calls=%fused_computation.51 | convolution fusion | flops 101711872 | bytes 1328128 | tf_op jit(solution)/shard_map/fmt,fst->sfm/dot_general | solution.py:86
  248.4 1.5 copy.160
  249.9 1.5 copy.159
  251.4 1.5 copy.162
  253.9 54.8 %gather_fusion.1 = f32[16384,128]{1,0:T(8,128)} fusion(f32[128,128]{0,1:T(8,128)S(1)} %copy.144, s32[16384]{0:T(1024)S(1)} %bitcast_clamp_fusion), kind=kCustom, calls=%fused_computation.1 | custom fusion | bytes 16842752 | tf_op jit(solution)/shard_map/jit(_take)/gather | solution.py:124
  308.7 7.6 %select_bitcast_fusion = f32[128,128,128]{0,2,1:T(8,128)} fusion(f32[128,128,128]{2,1,0:T(8,128)} %bitcast.126, pred[128,128]{1,0:T(8,128)(4,1)S(1)} %get-tuple-element.390, pred[128,128]{1,0:T(8,128)(4,1)S(1)} %copy-done.19), kind=kLoop, calls=%fused_computation.18 | loop fusion | flops 4194304 | bytes 16809984 | tf_op jit(solution)/shard_map/jit(_where)/select_n | solution.py:124
  316.3 9.4 %copy.145 = f32[128,128,128]{2,1,0:T(8,128)} copy(f32[128,128,128]{0,2,1:T(8,128)} %select_bitcast_fusion) | data formatting | bytes 16777216 | tf_op jit(solution)/shard_map/jit(_where)/select_n | solution.py:124
  326.2 7.3 %fusion.116 = f32[128,32,128]{2,1,0:T(8,128)} fusion(bf16[128,32,128]{2,1,0:T(8,128)(2,1)S(1)} %bitcast.132, f32[128,128,128]{2,1,0:T(8,128)} %copy.145), kind=kOutput, calls=%fused_computation.199 | convolution fusion | flops 805306368 | bytes 11534336 | tf_op jit(solution)/shard_map/ftj,fmt->fmj/dot_general | solution.py:125
  333.6 4.6 rev.28
  338.2 4.6 rev.31
  342.8 4.6 rev.24
  347.4 4.6 rev.27
  352.0 94.2 %while.20 = (s32[]{:T(128)}, f32[16,4096]{1,0:T(8,128)S(1)}, f32[16,4096]{1,0:T(8,128)S(1)}, f32[16,4096]{1,0:T(8,128)S(1)}, f32[16,4096]{1,0:T(8,128)S(1)}, /*i...) while((s32[]{:T(128)}, f32[16,4096]{1,0:T(8,128)S(1)}, ...), condition=%wide.region_3.4_spmd.clone, body=%wide.region_2.3_spmd.clone.sunk | while | flops 2097156 | bytes 7438517 | solution.py:20
  356.7 1.5 fusion.131
  363.0 1.5 fusion.131
  369.3 1.5 fusion.131
  375.5 1.5 fusion.131
  381.8 1.5 fusion.131
  388.1 1.5 fusion.131
  394.3 1.5 fusion.131
  400.6 1.5 fusion.131
  406.9 1.5 fusion.131
  413.1 1.5 fusion.131
  419.4 1.5 fusion.131
  425.7 1.5 fusion.131
  438.2 1.5 fusion.131
  444.5 1.5 fusion.131
  448.8 2.0 multiply_add_fusion
  452.2 2.1 subtract_add_fusion.1
  456.3 2.0 add_add_fusion
  461.4 10.5 %fusion.37 = f32[128,32,128]{2,1,0:T(8,128)S(1)} fusion(f32[16,128,32]{2,1,0:T(8,128)} %reshape.154, f32[128]{0:T(128)} %iota_subtract_fusion.3, f32[128,16]{1,0:T(8,128)} %copy-done.10, f32[128,16]{1,0:T(8,128)S(1)} %copy.142, f32[128,16]{1,0:T(8,128)S(1)} %copy.141, f32[128,16]{1,0:T(8,128)} %copy-done.8), kind=kOutput, calls=%fused_computation.70 | convolution fusion | flops 102498304 | bytes 2392576 | tf_op jit(solution)/shard_map/sfm,fsj->fmj/dot_general | solution.py:184
  472.0 10.3 %subtract_add_fusion = f32[128,32,128]{2,1,0:T(8,128)} fusion(f32[128,32,128]{2,1,0:T(8,128)S(1)} %copy-done, f32[128,32,128]{2,1,0:T(8,128)S(1)} %fusion.37, f32[16,128,32]{2,1,0:T(8,128)S(1)} %copy-done.3, f32[128]{0:T(128)S(1)} %copy-done.25, f32[128,16]{1,0:T(8,128)S(1)} %copy-done.11, f32[128,16]{1,0:T(8,128)S(1)} %copy.142, f32[128,16]{1,0:T(8,128)S(1)} %copy.141, ...), kind=kOutput, calls=%fused_computation.40 | convolution fusion | flops 103546880 | bytes 6586880 | tf_op jit(solution)/shard_map/sfm,fsj->fmj/dot_general | solution.py:184
  482.4 11.4 %scatter_custom_fusion = f32[4096,128]{1,0:T(8,128)S(1)} fusion(s32[4096]{0:T(1024)} %get-tuple-element.384, f32[4096,128]{1,0:T(8,128)} %bitcast.138, f32[]{:T(128)} %constant.65.clone.1), kind=kCustom, calls=%fused_computation.102 | custom fusion | bytes 2097664 | tf_op jit(solution)/shard_map/scatter | solution.py:188
  493.8 2.9 fusion.20
  496.9 58.7 %all-reduce.2 = (f32[128,16]{0,1:T(8,128)S(1)}, f32[128,16]{0,1:T(8,128)S(1)}, f32[128,16]{0,1:T(8,128)S(1)}, f32[128,16]{0,1:T(8,128)S(1)}) all-reduce(f32[128,16]{0,1:T(8,128)S(1)} %bitcast_add_fusion.4, f32[128,16]{0,1:T(8,128)S(1)} %bitcast_add_fusion.7, ...), channel_id=1, replica_groups=mesh['groups'=2,'seq'=16] {'seq'}, use_global_device_ids=true, to_apply=%region_16.17 | all-reduce | flops 8192 | bytes 65536 | tf_op jit(solution)/shard_map/psum | solution.py:199
  (277 shorter events, 107.9 us)
Async XLA Ops:
  7.2 326.4 %all-gather.13.cloned.1.call-start = ((), (), s32[]{:S(2)}) async-start(), calls=%async_computation.2 | async-start | bytes 4456448 | tf_op jit(solution)/shard_map/all_gather | solution.py:9
  7.2 31.2 %copy-start.26 = (f32[128]{0:T(128)}, f32[128]{0:T(128)S(1)}, u32[]{:S(2)}) copy-start(f32[128]{0:T(128)S(1)} %iota_add_fusion) | copy-start | bytes 1540
  8.9 150.9 %copy-start.15 = (f32[128,16]{0,1:T(8,128)}, f32[128,16]{0,1:T(8,128)S(1)}, u32[]{:S(2)}) copy-start(f32[128,16]{0,1:T(8,128)S(1)} %get-tuple-element.387) | copy-start | bytes 24580
  8.9 151.0 %copy-start.13 = (f32[128,16]{0,1:T(8,128)}, f32[128,16]{0,1:T(8,128)S(1)}, u32[]{:S(2)}) copy-start(f32[128,16]{0,1:T(8,128)S(1)} %get-tuple-element.386) | copy-start | bytes 24580
  38.1 300.0 %all-gather.15.cloned.1.call-start = ((), (), s32[]{:S(2)}) async-start(), calls=%async_computation.3 | async-start | bytes 4456448 | tf_op jit(solution)/shard_map/all_gather | solution.py:9
  45.0 297.8 %all-gather.9.cloned.1.call-start = ((), (), s32[]{:S(2)}) async-start(), calls=%async_computation | async-start | bytes 4456448 | tf_op jit(solution)/shard_map/all_gather | solution.py:9
  52.9 294.5 %all-gather.11.cloned.1.call-start = ((), (), s32[]{:S(2)}) async-start(), calls=%async_computation.1 | async-start | bytes 4456448 | tf_op jit(solution)/shard_map/all_gather | solution.py:9
  159.8 5.4 copy-start.1
  159.9 23.4 %copy-start.8 = (f32[128,16]{1,0:T(8,128)}, f32[128,16]{1,0:T(8,128)S(1)}, u32[]{:S(2)}) copy-start(f32[128,16]{1,0:T(8,128)S(1)} %copy.140) | copy-start | bytes 24580
  160.1 23.3 %copy-start.10 = (f32[128,16]{1,0:T(8,128)}, f32[128,16]{1,0:T(8,128)S(1)}, u32[]{:S(2)}) copy-start(f32[128,16]{1,0:T(8,128)S(1)} %copy.143) | copy-start | bytes 24580
  166.6 16.8 %copy-start.27 = (f32[128]{0:T(128)S(1)}, f32[128]{0:T(128)}, u32[]{:S(2)}) copy-start(f32[128]{0:T(128)} %copy-done.26) | copy-start | bytes 1540
  211.2 0.5 copy-start.28
  253.8 54.8 %copy-start.19 = (pred[128,128]{1,0:T(8,128)(4,1)S(1)}, pred[128,128]{1,0:T(8,128)(4,1)}, u32[]{:S(2)}) copy-start(pred[128,128]{1,0:T(8,128)(4,1)} %get-tuple-element.389) | copy-start | bytes 49156
  446.2 6.0 %copy-start.4 = (f32[16,4096]{1,0:T(8,128)S(1)}, f32[16,4096]{1,0:T(8,128)}, u32[]{:S(2)}) copy-start(f32[16,4096]{1,0:T(8,128)} %reshape.160) | copy-start | bytes 786436
  446.2 6.0 %copy-start.5 = (f32[16,4096]{1,0:T(8,128)S(1)}, f32[16,4096]{1,0:T(8,128)}, u32[]{:S(2)}) copy-start(f32[16,4096]{1,0:T(8,128)} %reshape.162) | copy-start | bytes 786436
  446.2 6.0 %copy-start.6 = (f32[16,4096]{1,0:T(8,128)S(1)}, f32[16,4096]{1,0:T(8,128)}, u32[]{:S(2)}) copy-start(f32[16,4096]{1,0:T(8,128)} %reshape.163) | copy-start | bytes 786436
  450.8 3.5 copy-start.7
  458.3 13.6 %copy-start = (f32[128,32,128]{2,1,0:T(8,128)S(1)}, f32[128,32,128]{2,1,0:T(8,128)}, u32[]{:S(2)}) copy-start(f32[128,32,128]{2,1,0:T(8,128)} %fusion.116) | copy-start | bytes 6291460
  461.0 10.9 %copy-start.9 = (f32[128,16]{1,0:T(8,128)S(1)}, f32[128,16]{1,0:T(8,128)}, u32[]{:S(2)}) copy-start(f32[128,16]{1,0:T(8,128)} %copy-done.8) | copy-start | bytes 24580
  461.0 10.9 %copy-start.11 = (f32[128,16]{1,0:T(8,128)S(1)}, f32[128,16]{1,0:T(8,128)}, u32[]{:S(2)}) copy-start(f32[128,16]{1,0:T(8,128)} %copy-done.10) | copy-start | bytes 24580
  461.1 10.9 %copy-start.25 = (f32[128]{0:T(128)S(1)}, f32[128]{0:T(128)}, u32[]{:S(2)}) copy-start(f32[128]{0:T(128)} %iota_subtract_fusion.3) | copy-start | bytes 1540
  461.4 10.6 %copy-start.3 = (f32[16,128,32]{2,1,0:T(8,128)S(1)}, f32[16,128,32]{2,1,0:T(8,128)}, u32[]{:S(2)}) copy-start(f32[16,128,32]{2,1,0:T(8,128)} %reshape.155) | copy-start | bytes 786436
  472.0 21.8 %copy-start.2 = (bf16[4096,128]{1,0:T(8,128)(2,1)S(1)}, bf16[4096,128]{1,0:T(8,128)(2,1)}, u32[]{:S(2)}) copy-start(bf16[4096,128]{1,0:T(8,128)(2,1)} %param.14) | copy-start | bytes 3145732
  482.3 14.5 %copy-start.21 = (f32[128,16]{0,1:T(8,128)S(1)}, f32[128,16]{0,1:T(8,128)}, u32[]{:S(2)}) copy-start(f32[128,16]{0,1:T(8,128)} %copy.161) | copy-start | bytes 24580
  482.3 14.5 %copy-start.24 = (f32[128,16]{0,1:T(8,128)S(1)}, f32[128,16]{0,1:T(8,128)}, u32[]{:S(2)}) copy-start(f32[128,16]{0,1:T(8,128)} %copy.160) | copy-start | bytes 24580
  482.3 14.5 %copy-start.20 = (f32[16,128]{1,0:T(8,128)S(1)}, f32[16,128]{1,0:T(8,128)}, u32[]{:S(2)}) copy-start(f32[16,128]{1,0:T(8,128)} %reduce_sum.83) | copy-start | bytes 24580
  482.3 14.5 %copy-start.23 = (f32[128,16]{0,1:T(8,128)S(1)}, f32[128,16]{0,1:T(8,128)}, u32[]{:S(2)}) copy-start(f32[128,16]{0,1:T(8,128)} %copy.159) | copy-start | bytes 24580
  482.3 14.5 %copy-start.22 = (f32[128,16]{0,1:T(8,128)S(1)}, f32[128,16]{0,1:T(8,128)}, u32[]{:S(2)}) copy-start(f32[128,16]{0,1:T(8,128)} %copy.162) | copy-start | bytes 24580
  482.4 73.2 %copy-start.12 = (f32[128,16]{0,1:T(8,128)S(1)}, f32[128,16]{0,1:T(8,128)}, u32[]{:S(2)}) copy-start(f32[128,16]{0,1:T(8,128)} %param.17) | copy-start | bytes 24580
  482.4 73.2 %copy-start.14 = (f32[128,16]{0,1:T(8,128)S(1)}, f32[128,16]{0,1:T(8,128)}, u32[]{:S(2)}) copy-start(f32[128,16]{0,1:T(8,128)} %copy-done.13) | copy-start | bytes 24580
  482.4 73.2 %copy-start.16 = (f32[128,16]{0,1:T(8,128)S(1)}, f32[128,16]{0,1:T(8,128)}, u32[]{:S(2)}) copy-start(f32[128,16]{0,1:T(8,128)} %copy-done.15) | copy-start | bytes 24580
  482.4 73.2 %copy-start.17 = (f32[128,16]{0,1:T(8,128)S(1)}, f32[128,16]{0,1:T(8,128)}, u32[]{:S(2)}) copy-start(f32[128,16]{0,1:T(8,128)} %param.18) | copy-start | bytes 24580
  482.4 73.8 %copy-start.18 = (f32[2,128,16]{1,2,0:T(8,128)S(1)}, f32[2,128,16]{1,2,0:T(8,128)}, u32[]{:S(2)}) copy-start(f32[2,128,16]{1,2,0:T(8,128)} %param.19) | copy-start | bytes 49156
Sparse Core Ops, SparseCore 0:
  38.2 53.6 all-gather.12
  94.1 51.3 all-gather.14
  147.7 49.1 all-gather.8
  198.8 49.0 all-gather.10
where the time goes:
time: 575 us; the launch traced here: 564 us
  local copies, waits for them, and re-layouts  244 us (42%)
  blocking collectives  138 us (24%)
  matrix products  91.3 us (16%)
  other arithmetic  75.3 us (13%)
  between operations  14.6 us (3%)
    all_gather x4, blocking collectives, prefix(): pieces = jax.tree.map(lambda part: lax.all_gather(part, axis), value)  79.2 us
    psum x1, blocking collectives, body(): lax.psum((part_a_real, part_a_imag, part_w_real, part_w_imag), 'seq')  58.7 us
    gather x1, local copies, waits for them, and re-layouts, body(): jnp.take(filt, jnp.maximum(lag_index, 0), axis=1)  54.8 us
    reshape x62, local copies, waits for them, and re-layouts, widen(): return jnp.repeat(values, states.shape[1] // values.shape[1], axis=1)  33.8 us
    dot_general x4, matrix products, mode_sum(): out_imag = jnp.einsum('fmt,fst->sfm', data, table_imag, precision=highest)  23.2 us
    broadcast_in_dim x62, local copies, waits for them, and re-layouts, widen(): return jnp.repeat(values, states.shape[1] // values.shape[1], axis=1)  22.8 us
    select_n x15, other arithmetic, turn(): jnp.where(position < mine, new, old)  22.4 us
    dot_general x4, matrix products, mode_sum(): out_real = jnp.einsum('fmt,fst->sfm', data, table_real, precision=highest)  21.9 us
  transfers between devices with their start and end apart: 4, of which 0 were waited for; matrix products, arithmetic and copies ran while one was open for 41% of the time, Pallas kernels for 0%

commit v1 on v0

v1 whole, which is shorter than its diff:
```python
import functools

import jax
import jax.numpy as jnp
from jax import lax
from jax.experimental import pallas as pl
from jax.experimental.pallas import tpu as pltpu
from jax.sharding import PartitionSpec as P

F32 = jnp.float32
BF16 = jnp.bfloat16
LANES = 128


def complex_product(a_real, a_imag, b_real, b_imag):
    return (a_real * b_real - a_imag * b_imag, a_real * b_imag + a_imag * b_real)


def split(x):
    hi = x.astype(BF16)
    return hi, (x - hi.astype(F32)).astype(BF16)


def dot(lhs, rhs, contract):
    return lax.dot_general(lhs, rhs, (contract, ((), ())), preferred_element_type=F32)


NN = ((1,), (0,))
NT = ((1,), (1,))
TN = ((0,), (0,))


def place_kernel(per_filter, filter_ref, pos_ref):
    rows = lax.broadcasted_iota(jnp.int32, (LANES, LANES), 0)
    cols = lax.broadcasted_iota(jnp.int32, (LANES, LANES), 1)
    before = (rows < cols).astype(F32).astype(BF16)
    ones = jnp.ones((LANES, LANES), BF16)
    pair = jnp.concatenate([before, ones], axis=1)
    seen = (rows * per_filter).astype(F32)
    for block in range(filter_ref.shape[0]):
        hot = rows == filter_ref[block : block + 1, :]
        counts = dot(hot.astype(F32).astype(BF16), pair, NN)
        place = jnp.where(hot, counts[:, :LANES] + seen, 0.0)
        pos_ref[block : block + 1, :] = jnp.sum(place, axis=0, keepdims=True).astype(jnp.int32)
        seen = seen + counts[:, LANES:]


def powers(re_ref, im_ref, group, backward):
    low = slice(8, 16) if backward else slice(0, 8)
    low_re, low_im = re_ref[group, low, :], im_ref[group, low, :]
    real, imag = [], []
    for a in range(16):
        row = 16 + (15 - a if backward else a)
        high_re, high_im = re_ref[group, row : row + 1, :], im_ref[group, row : row + 1, :]
        r, i = complex_product(high_re, high_im, low_re, low_im)
        real.append(r)
        imag.append(i)
    return jnp.concatenate(real, axis=0), jnp.concatenate(imag, axis=0)


def stacked(real, imag):
    hi, lo = split(jnp.concatenate([real, imag], axis=1))
    return jnp.concatenate([hi, lo], axis=0)


def own_filter(rows, lanes, members, modes):
    row = lax.broadcasted_iota(jnp.int32, (rows, lanes), 0) // members
    lane = (lax.broadcasted_iota(jnp.int32, (rows, lanes), 1) % LANES) // modes
    return row == lane


def mode_sum(data, table, members, modes):
    out = dot(jnp.concatenate([data, data], axis=1), table, NN)
    lane = (lax.broadcasted_iota(jnp.int32, (members, 2 * LANES), 1) % LANES) // modes
    total = jnp.zeros((members, 2 * LANES), F32)
    for f in range(data.shape[0] // members):
        total = jnp.where(lane == f, out[f * members : (f + 1) * members], total)
    return total


def states_kernel(
    members, modes, pos_ref, go_ref, q_ref, k_ref, v_ref, re_ref, im_ref,
    gate_ref, mixed_ref, y_ref, x_ref, natural_g, natural_m, grouped_g, grouped_m,
):
    channels = go_ref.shape[0]
    tile = 256

    @pl.loop(0, channels // tile)
    def _(i):
        at = pl.ds(pl.multiple_of(i * tile, tile), tile)
        gate = (go_ref[at, :].astype(F32) * q_ref[at, :].astype(F32)).astype(BF16)
        mixed = (k_ref[at, :].astype(F32) * v_ref[at, :].astype(F32)).astype(BF16)
        natural_g[at, :] = gate.astype(F32)
        natural_m[at, :] = mixed.astype(F32)

    @pl.loop(0, channels // 16)
    def _(i):
        base = pl.multiple_of(i * 16, 16)
        for u in range(16):
            to = pos_ref[base + u]
            grouped_g[pl.ds(to, 1), :] = natural_g[pl.ds(base + u, 1), :]
            grouped_m[pl.ds(to, 1), :] = natural_m[pl.ds(base + u, 1), :]

    size = (LANES // modes) * members

    @pl.loop(0, channels // size)
    def _(g):
        at = pl.ds(pl.multiple_of(g * size, size), size)
        gate = grouped_g[at, :].astype(BF16)
        mixed = grouped_m[at, :].astype(BF16)
        gate_ref[at, :] = gate
        mixed_ref[at, :] = mixed
        y = mode_sum(gate, stacked(*powers(re_ref, im_ref, g, False)), members, modes)
        x = mode_sum(mixed, stacked(*powers(re_ref, im_ref, g, True)), members, modes)
        y_ref[g, 0], y_ref[g, 1] = y[:, :LANES], y[:, LANES:]
        x_ref[g, 0], x_ref[g, 1] = x[:, :LANES], x[:, LANES:]


def local_kernel(
    members, modes, gate_ref, mixed_ref, re_ref, im_ref, rr_ref, ri_ref,
    conv_ref, v_ref, w_ref, sums_ref, toe, lag,
):
    per = LANES // modes
    head_re, head_im = powers(re_ref, im_ref, 0, False)
    back_re, back_im = powers(re_ref, im_ref, 0, True)
    step = lax.broadcasted_iota(jnp.int32, (LANES, LANES), 0).astype(F32)
    gate, mixed = gate_ref[...], mixed_ref[...]
    der = stacked(step * head_re, step * head_im)
    v = mode_sum(gate, der, members, modes)
    span = float(LANES)
    w = mode_sum(
        mixed, stacked((span - step) * back_re, (span - step) * back_im), members, modes
    )
    v_ref[0, 0], v_ref[0, 1] = v[:, :LANES], v[:, LANES:]
    w_ref[0, 0], w_ref[0, 1] = w[:, :LANES], w[:, LANES:]
    head = stacked(head_re, head_im)
    head_hi, head_lo = head[:LANES], head[LANES:]
    own8 = own_filter(per, 2 * LANES, 1, modes)
    res = jnp.concatenate([rr_ref[0], -ri_ref[0]], axis=1)
    res_hi, res_lo = split(jnp.where(own8, res, 0.0))
    filt = dot(res_hi, head_hi, NT) + dot(res_lo, head_hi, NT) + dot(res_hi, head_lo, NT)
    row = lax.broadcasted_iota(jnp.int32, (LANES, LANES), 0)
    col = lax.broadcasted_iota(jnp.int32, (LANES, LANES), 1)
    causal = col >= row
    mirror = (row + col == LANES - 1).astype(F32).astype(BF16)
    mirrored = dot(mixed, mirror, NN).astype(BF16)
    for f in range(per):
        at = slice(f * members, (f + 1) * members)
        wide = jnp.broadcast_to(filt[f : f + 1, :], (LANES, LANES))
        shifted = pltpu.roll(wide, 0, 1, stride=1, stride_axis=0)
        hi, lo = split(jnp.where(causal, shifted, 0.0))
        gate_f = gate[at]
        conv_ref[at, :] = dot(gate_f, hi, NT) + dot(gate_f, lo, NT)
        corr = jnp.where(row + col >= LANES - 1, dot(mirrored[at], gate_f, TN), 0.0)
        aligned = pltpu.roll(corr, 1, 1, stride=1, stride_axis=0)
        lag[f : f + 1, :] = jnp.sum(aligned, axis=0, keepdims=True)
    lag_hi, lag_lo = split(lag[...])
    for which, table in enumerate((head, der)):
        hi, lo = table[:LANES], table[LANES:]
        out = dot(lag_hi, hi, NN) + dot(lag_lo, hi, NN) + dot(lag_hi, lo, NN)
        out = jnp.sum(jnp.where(own8, out, 0.0), axis=0, keepdims=True)
        sums_ref[0, 2 * which : 2 * which + 1, :] = out[:, :LANES]
        sums_ref[0, 2 * which + 1 : 2 * which + 2, :] = out[:, LANES:]


def sums_kernel(
    x_ref, w_ref, v_ref, yin_ref, xin_ref, pr_ref, pi_ref, local_ref, out_ref
):
    def member_sum(pair):
        return [jnp.sum(part, axis=0, keepdims=True) for part in pair]

    for g in range(x_ref.shape[0]):
        yin = (yin_ref[g, 0], yin_ref[g, 1])
        xin = (xin_ref[g, 0], xin_ref[g, 1])
        a = member_sum(complex_product(x_ref[g, 0], x_ref[g, 1], *yin))
        c1 = member_sum(complex_product(w_ref[g, 0], w_ref[g, 1], *yin))
        c2 = member_sum(complex_product(v_ref[g, 0], v_ref[g, 1], *xin))
        c3 = member_sum(complex_product(*xin, *yin))
        c3 = complex_product(pr_ref[g : g + 1, :], pi_ref[g : g + 1, :], *c3)
        out_ref[0, g : g + 1, :] = local_ref[g, 0:1, :] + a[0]
        out_ref[1, g : g + 1, :] = local_ref[g, 1:2, :] + a[1]
        span = float(LANES)
        out_ref[2, g : g + 1, :] = local_ref[g, 2:3, :] + c1[0] + c2[0] + span * c3[0]
        out_ref[3, g : g + 1, :] = local_ref[g, 3:4, :] + c1[1] + c2[1] + span * c3[1]


def finish_kernel(
    members, modes, pos_ref, conv_ref, yin_ref, re_ref, im_ref, rr_ref, ri_ref, k_ref, v_ref,
    gk_ref, gv_ref, grouped, natural,
):
    channels = conv_ref.shape[0]
    per = LANES // modes
    size = per * members

    @pl.loop(0, channels // size)
    def _(g):
        at = pl.ds(pl.multiple_of(g * size, size), size)
        back_re, back_im = powers(re_ref, im_ref, g, True)
        rr, ri = rr_ref[g], ri_ref[g]
        coef_re, coef_im = complex_product(rr, ri, back_re, back_im)
        coef_hi, coef_lo = split(jnp.concatenate([coef_re, -coef_im], axis=1))
        yin = jnp.concatenate([yin_ref[g, 0], yin_ref[g, 1]], axis=1)
        lane = (lax.broadcasted_iota(jnp.int32, (members, 2 * LANES), 1) % LANES) // modes
        wide = jnp.concatenate([jnp.where(lane == f, yin, 0.0) for f in range(per)], axis=0)
        hi, lo = split(wide)
        cross = dot(hi, coef_hi, NT) + dot(lo, coef_hi, NT) + dot(hi, coef_lo, NT)
        grouped[at, :] = conv_ref[at, :] + cross

    @pl.loop(0, channels // 16)
    def _(i):
        base = pl.multiple_of(i * 16, 16)
        for u in range(16):
            natural[pl.ds(base + u, 1), :] = grouped[pl.ds(pos_ref[base + u], 1), :]

    tile = 256

    @pl.loop(0, channels // tile)
    def _(i):
        at = pl.ds(pl.multiple_of(i * tile, tile), tile)
        conv = natural[at, :]
        gk_ref[at, :] = (conv * v_ref[at, :].astype(F32)).astype(BF16)
        gv_ref[at, :] = (conv * k_ref[at, :].astype(F32)).astype(BF16)


def vmem(n):
    return [pl.BlockSpec(memory_space=pltpu.VMEM)] * n


SMEM = pl.BlockSpec(memory_space=pltpu.SMEM)
PARAMS = pltpu.CompilerParams(vmem_limit_bytes=48 << 20)


def swap(value, bit):
    count = lax.axis_size("seq")
    return lax.ppermute(value, "seq", [(i, i ^ bit) for i in range(count)])


def body(grad_out, query, key, value, conv_out, channel_filter, decay_rate, twist, residues):
    channels, positions = grad_out.shape
    filters, modes = decay_rate.shape
    members = channels // filters
    per = LANES // modes
    groups = filters // per
    count = lax.axis_size("seq")
    me = lax.axis_index("seq")
    length = positions * count
    shape = jax.ShapeDtypeStruct

    pos = pl.pallas_call(
        functools.partial(place_kernel, members),
        out_shape=shape((channels // LANES, LANES), jnp.int32),
        in_specs=vmem(1),
        out_specs=vmem(1)[0],
    )(channel_filter.reshape(channels // LANES, LANES)).reshape(channels)

    small = jnp.stack([decay_rate, twist, residues[0], residues[1]]).reshape(4, groups, LANES)
    rho = small[0] / length
    angle = small[1] * rho
    scale = jnp.sqrt(1.0 - jnp.exp(-2.0 * rho))
    rr, ri = small[2] * scale, small[3] * scale

    def power(steps):
        mag = jnp.exp(-rho[:, None, :] * steps[None, :, None])
        phase = angle[:, None, :] * steps[None, :, None]
        return mag * jnp.cos(phase), mag * jnp.sin(phase)

    low = jnp.arange(8, dtype=F32)
    steps = jnp.concatenate([low, 8.0 - low, 8.0 * jnp.arange(16, dtype=F32)])
    tab_re, tab_im = power(steps)

    state = shape((groups, 2, members, LANES), F32)
    gate, mixed, y, x = pl.pallas_call(
        functools.partial(states_kernel, members, modes),
        out_shape=(
            shape((channels, positions), BF16), shape((channels, positions), BF16), state, state,
        ),
        in_specs=[SMEM] + vmem(6),
        out_specs=tuple(vmem(4)),
        scratch_shapes=[pltpu.VMEM((channels, positions), F32)] * 4,
        compiler_params=PARAMS,
    )(pos, grad_out, query, key, value, tab_re, tab_im)

    rr3, ri3 = rr[:, None, :], ri[:, None, :]
    size = per * members
    rows = pl.BlockSpec((size, positions), lambda g: (g, 0))
    table = pl.BlockSpec((1, 32, LANES), lambda g: (g, 0, 0))
    one = pl.BlockSpec((1, 1, LANES), lambda g: (g, 0, 0))
    stat = pl.BlockSpec((1, 2, members, LANES), lambda g: (g, 0, 0, 0))
    conv, v, w, local = pl.pallas_call(
        functools.partial(local_kernel, members, modes),
        grid=(groups,),
        out_shape=(shape((channels, positions), F32), state, state, shape((groups, 4, LANES), F32)),
        in_specs=[rows, rows, table, table, one, one],
        out_specs=(rows, stat, stat, pl.BlockSpec((1, 4, LANES), lambda g: (g, 0, 0))),
        scratch_shapes=[pltpu.VMEM((8, LANES), F32), pltpu.VMEM((per, LANES), F32)],
        compiler_params=PARAMS,
        cost_estimate=pl.CostEstimate(flops=10**10, bytes_accessed=8 << 20, transcendentals=0),
    )(gate, mixed, tab_re, tab_im, rr3, ri3)
    grad_query = (grad_out.astype(F32) * conv_out.astype(F32)).astype(BF16)

    def decay(blocks):
        blocks = jnp.asarray(blocks).astype(F32) * float(positions)
        mag = jnp.exp(-rho * blocks)
        return mag * jnp.cos(angle * blocks), mag * jnp.sin(angle * blocks)

    def advance(factor, values, start, rows_):
        re, im = factor
        re = lax.dynamic_slice_in_dim(re, start, rows_, 0)[:, None, :]
        im = lax.dynamic_slice_in_dim(im, start, rows_, 0)[:, None, :]
        r, i = complex_product(re, im, values[:, 0], values[:, 1])
        return jnp.stack([r, i], axis=1)

    def half(values, which):
        n = values.shape[0] // 2
        return lax.dynamic_slice_in_dim(values, which * n, n, 0)

    halvings = []
    first = jnp.int32(0)
    level = 0
    while (1 << level) < count and level < 2:
        bit = 1 << level
        upper = (me // bit) % 2
        is_up = upper == 1
        main, side = jnp.where(is_up, x, y), jnp.where(is_up, y, x)
        n = main.shape[0] // 2
        sent = jnp.concatenate([side, half(main, 1 - upper)], axis=0)
        got = swap(sent, bit)
        full, part = got[: 2 * n], got[2 * n :]
        halvings.append((bit, upper, is_up, full, first))
        first = first + upper * n
        factor = decay(bit)
        t_main = half(main, upper) + advance(factor, half(full, upper), first, n)
        t_side = part + advance(factor, half(side, upper), first, n)
        y_next, x_next = jnp.where(is_up, t_side, t_main), jnp.where(is_up, t_main, t_side)
        own = (y, x) if level == 0 else own
        y, x = y_next, x_next
        level += 1

    n = y.shape[0]
    into_y, into_x = jnp.zeros_like(y), jnp.zeros_like(x)
    base = 1 << level
    bit = base
    while bit < count:
        upper = (me // bit) % 2
        is_up = upper == 1
        main, side = jnp.where(is_up, x, y), jnp.where(is_up, y, x)
        last = bit * 2 >= count
        got = swap(side if last else jnp.concatenate([side, main], axis=0), bit)
        got_main = got[:n]
        inside = me % bit // base
        between = jnp.where(is_up, inside, bit // base - 1 - inside) * base
        more = advance(decay(between), got_main, first, n)
        into_y = into_y + jnp.where(is_up, 0.0, more)
        into_x = into_x + jnp.where(is_up, more, 0.0)
        if not last:
            factor = decay(bit)
            t_main = main + advance(factor, got_main, first, n)
            t_side = got[n:] + advance(factor, side, first, n)
            y, x = jnp.where(is_up, t_side, t_main), jnp.where(is_up, t_main, t_side)
        bit *= 2

    for bit, upper, is_up, full, start in reversed(halvings):
        mine = jnp.stack([into_y, into_x])
        other = swap(mine, bit)
        both = jnp.concatenate(
            [jnp.where(is_up, other, mine), jnp.where(is_up, mine, other)], axis=1
        )
        in_y, in_x = both[0], both[1]
        n2 = in_y.shape[0]
        factor = decay(bit)
        into_y = jnp.where(is_up, in_y, full + advance(factor, in_y, start, n2))
        into_x = jnp.where(is_up, full + advance(factor, in_x, start, n2), in_x)

    own_y, own_x = own
    block_re, block_im = decay(1)
    total = pl.pallas_call(
        sums_kernel,
        out_shape=shape((4, groups, LANES), F32),
        in_specs=vmem(8),
        out_specs=vmem(1)[0],
        compiler_params=PARAMS,
    )(own_x, w, v, into_y, into_x, block_re, block_im, local)
    grad_key, grad_value = pl.pallas_call(
        functools.partial(finish_kernel, members, modes),
        out_shape=(shape((channels, positions), BF16), shape((channels, positions), BF16)),
        in_specs=[SMEM] + vmem(8),
        out_specs=tuple(vmem(2)),
        scratch_shapes=[pltpu.VMEM((channels, positions), F32)] * 2,
        compiler_params=PARAMS,
        cost_estimate=pl.CostEstimate(flops=10**10, bytes_accessed=8 << 20, transcendentals=0),
    )(pos, conv, into_y, tab_re, tab_im, rr3, ri3, key, value)

    bit = 1
    while bit < count:
        total = total + swap(total, bit)
        bit *= 2
    a_re, a_im, w_re, w_im = total[0], total[1], total[2], total[3]
    b_re, b_im = complex_product(rr, ri, w_re, w_im)
    plain = small[2] * a_re - small[3] * a_im
    log_rate = plain * (rho * jnp.exp(-2.0 * rho) / scale) - b_re * rho - b_im * angle
    grads = jnp.stack([log_rate, -b_im * rho, scale * a_re, -scale * a_im])
    grads = grads.reshape(4, filters, modes)
    return (grad_query, grad_key, grad_value, grads[0], grads[1], grads[2:])


def solution(mesh):
    wide = P(None, ("groups", "seq"))
    return jax.shard_map(
        body,
        mesh=mesh,
        in_specs=(wide,) * 5 + (P(),) * 4,
        out_specs=(wide, wide, wide, P("groups", None), P("groups", None), P("groups", None, None)),
        check_vma=False,
    )
```

time: 575 us -> 110 us (0.19); the launches traced: 564 us -> 109 us
  local copies, waits for them, and re-layouts: 244 us -> 12.6 us
  blocking collectives: 138 us -> 0 us
  matrix products: 91.3 us -> 0 us
  other arithmetic: 75.3 us -> 6.62 us
  Pallas kernels: 0 us -> 43.1 us
  waiting for transfers between devices: 0.07 us -> 35.2 us
  between operations: 14.6 us -> 1.11 us
  starting transfers between devices: 0.38 us -> 10.7 us
    dot_general x13 -> x0, matrix products: 91.3 us -> none  [the longest x4 23.2 us: mode_sum(): out_imag = jnp.einsum('fmt,fst->sfm', data, table_imag, precision=highest)]
    gather x3 -> x0, local copies, waits for them, and re-layouts: 82 us -> none  [the longest x1 54.8 us: body(): jnp.take(filt, jnp.maximum(lag_index, 0), axis=1)]
    all_gather x4 -> x0, blocking collectives: 79.2 us -> none  [prefix(): pieces = jax.tree.map(lambda part: lax.all_gather(part, axis), value)]
    psum x1 -> x0, blocking collectives: 58.7 us -> none  [body(): lax.psum((part_a_real, part_a_imag, part_w_real, part_w_imag), 'seq')]
    reshape x72 -> x0, local copies, waits for them, and re-layouts: 49.3 us -> none  [the longest x62 33.8 us: widen(): return jnp.repeat(values, states.shape[1] // values.shape[1], axis=1)]
    pallas_call x0 -> x5, Pallas kernels: none -> 43.1 us  [the longest x1 17.3 us: body(): pl.pallas_call(functools.partial(local_kernel, members, modes), grid=(gro...]
    ppermute x0 -> x10, waiting for transfers between devices: none -> 35.2 us  [swap(): return lax.ppermute(value, 'seq', [(i, i ^ bit) for i in range(count)])]
    select_n x16 -> x7, other arithmetic: 30 us -> 0.78 us  [the longest x4 0.32 us: body(): main, side = (jnp.where(is_up, x, y), jnp.where(is_up, y, x))]
  transfers between devices with their start and end apart: 4 -> 10, of which waited for: 0 -> 8; matrix products, arithmetic and copies ran while one was open for 41% -> 2% of each run, Pallas kernels for 0% -> 26%
where the time goes in v1:
time: 110 us; the launch traced here: 109 us
  Pallas kernels  43.1 us (39%)
  waiting for transfers between devices  35.2 us (32%)
  local copies, waits for them, and re-layouts  12.6 us (11%)
  starting transfers between devices  10.7 us (10%)
  other arithmetic  6.62 us (6%)
  between operations  1.11 us (1%)
    ppermute x10, waiting for transfers between devices, swap(): return lax.ppermute(value, 'seq', [(i, i ^ bit) for i in range(count)])  35.2 us
    pallas_call x1, Pallas kernels, body(): pl.pallas_call(functools.partial(local_kernel, members, modes), grid=(gro...  17.3 us
    pallas_call x1, Pallas kernels, body(): pl.pallas_call(functools.partial(states_kernel, members, modes), out_shap...  11.7 us
    pallas_call x1, Pallas kernels, body(): pl.pallas_call(functools.partial(finish_kernel, members, modes), out_shap...  11.6 us
    unnamed x40, local copies, waits for them, and re-layouts  10.8 us
    ppermute x10, starting transfers between devices, swap(): return lax.ppermute(value, 'seq', [(i, i ^ bit) for i in range(count)])  10.7 us
  transfers between devices with their start and end apart: 10, of which 8 were waited for; matrix products, arithmetic and copies ran while one was open for 2% of the time, Pallas kernels for 26%

profile of v1, /device:TPU:0, one launch (start us, length us, event | category | flops | bytes accessed | tf_op | source)
XLA Modules:
  0.0 109.3 jit_solution(7384900737738264881)
XLA Ops:
  0.7 1.3 %multiply_exponential_fusion.6 = (f32[128,16]{0,1:T(8,128)}, f32[128,16]{0,1:T(8,128)S(1)}, f32[128,16]{0,1:T(8,128)S(1)}, f32[128,16]{0,1:T(8,128)S(1)}, f32[128,16]{0,1:T(8,128)}) fusion(f32[128,16]{0,1:T(8,128)} %param.15, f32[128,16]{0,1:T(8,128)} %param.16), kind=kLoop, calls=%fused_computation.101 | loop fusion | flops 10240 | bytes 57344 | tf_op jit(solution)/shard_map/exp | solution.py:259
  2.0 0.1 copy.76
  2.1 0.1 mul.706
  2.2 0.1 copy.75
  2.3 0.1 neg.40
  2.4 2.1 %shard_map.136 = s32[32,128]{1,0:T(8,128)} custom-call(s32[32,128]{1,0:T(8,128)} %bitcast.60), custom_call_target="tpu_custom_call" | custom-call | tf_op jit(solution)/shard_map/pallas_call | solution.py:249
  4.5 0.1 pad_maximum_fusion.10
  4.6 1.0 fusion.6
  5.6 1.2 %copy-done = bf16[4096,128]{1,0:T(8,128)(2,1)S(1)} copy-done((bf16[4096,128]{1,0:T(8,128)(2,1)S(1)}, bf16[4096,128]{1,0:T(8,128)(2,1)}, u32[]{:S(2)}) %copy-start) | copy-done | bytes 1048600
  6.8 1.2 %copy-done.2 = bf16[4096,128]{1,0:T(8,128)(2,1)S(1)} copy-done((bf16[4096,128]{1,0:T(8,128)(2,1)S(1)}, bf16[4096,128]{1,0:T(8,128)(2,1)}, u32[]{:S(2)}) %copy-start.2) | copy-done | bytes 1048600
  8.0 0.7 copy-done.5
  8.8 11.7 %shard_map.137 = (bf16[4096,128]{1,0:T(8,128)(2,1)S(1)}, bf16[4096,128]{1,0:T(8,128)(2,1)S(1)}, f32[16,2,32,128]{3,2,1,0:T(8,128)S(1)}, f32[16,2,32,128]{3,2,1,0:T(8,128)S(1)}) custom-call(s32[4096]{0:T(1024)S(1)} %bitcast.54, bf16[4096,128]{1,0:T(8,128)(2,1)S(1)} %copy-done, bf16[4096,128]{1,0:T(8,128)(2,1)S(1)} %copy-done.2, bf16[4096,128]{1,0:T(8,128)(2,1)} %k_ref.3, ...), custom_call_target="tpu_custom_call" | custom-call | tf_op jit(solution)/shard_map/pallas_call | solution.py:272
  20.5 0.1 copy_select_fusion
  20.6 1.1 %pad_maximum_fusion = f32[24,2,32,128]{3,2,0,1:T(8,128)} fusion(f32[8,2,32,128]{3,2,0,1:T(8,128)S(1)} %constant_dynamic-slice_fusion.12, f32[16,2,32,128]{3,2,0,1:T(8,128)S(1)} %get-tuple-element.51), kind=kLoop, calls=%fused_computation.3 | loop fusion | flops 196608 | bytes 1572864 | tf_op jit(solution)/shard_map/concatenate | solution.py:326
  21.7 0.3 copy-done.9
  22.0 0.4 collective-permute-start
  22.5 0.1 broadcast_multiply_fusion.2
  22.6 2.0 %collective-permute-done = f32[24,2,32,128]{3,2,0,1:T(8,128)S(1)} collective-permute-done((f32[24,2,32,128]{3,2,0,1:T(8,128)}, f32[24,2,32,128]{3,2,0,1:T(8,128)S(1)}, u32[]{:S(2)}, u32[]{:S(2)}) %collective-permute-start) | collective-permute-done | bytes 786464 | tf_op jit(solution)/shard_map/ppermute | solution.py:235
  24.7 0.1 broadcast_select_fusion.6
  24.9 3.0 %collective-permute-start.1 = (f32[12,2,32,128]{3,2,0,1:T(8,128)S(1)}, f32[12,2,32,128]{3,2,0,1:T(8,128)S(1)}, u32[]{:S(2)}, u32[]{:S(2)}) collective-permute-start(f32[12,2,32,128]{3,2,0,1:T(8,128)S(1)} %pad_maximum_fusion.3), channel_id=1, source_target_pairs={{0,2},{1,3},{2,0},{3,1},{4,6},{5,7},{6,4},{7,5},{8,10},{9,11},{10,... | collective-permute-start | bytes 1179656 | tf_op jit(solution)/shard_map/ppermute | solution.py:235
  27.8 9.4 %collective-permute-done.1 = f32[12,2,32,128]{3,2,0,1:T(8,128)S(1)} collective-permute-done((f32[12,2,32,128]{3,2,0,1:T(8,128)S(1)}, f32[12,2,32,128]{3,2,0,1:T(8,128)S(1)}, u32[]{:S(2)}, u32[]{:S(2)}) %collective-permute-start.1) | collective-permute-done | bytes 393248 | tf_op jit(solution)/shard_map/ppermute | solution.py:235
  37.4 1.9 %collective-permute-start.2 = (f32[8,2,32,128]{3,2,0,1:T(8,128)S(1)}, f32[8,2,32,128]{3,2,0,1:T(8,128)S(1)}, u32[]{:S(2)}, u32[]{:S(2)}) collective-permute-start(f32[8,2,32,128]{3,2,0,1:T(8,128)S(1)} %pad_maximum_fusion.5), channel_id=1, source_target_pairs={{0,4},{1,5},{2,6},{3,7},{4,0},{5,1},{6,2},{7,3},{8,12},{9,13},{10,... | collective-permute-start | bytes 786440 | tf_op jit(solution)/shard_map/ppermute | solution.py:235
  39.3 6.0 %collective-permute-done.2 = f32[8,2,32,128]{3,2,0,1:T(8,128)S(1)} collective-permute-done((f32[8,2,32,128]{3,2,0,1:T(8,128)S(1)}, f32[8,2,32,128]{3,2,0,1:T(8,128)S(1)}, u32[]{:S(2)}, u32[]{:S(2)}) %collective-permute-start.2) | collective-permute-done | bytes 262176 | tf_op jit(solution)/shard_map/ppermute | solution.py:235
  45.4 2.6 %collective-permute-start.3 = (f32[4,2,32,128]{3,2,0,1:T(8,128)S(1)}, f32[4,2,32,128]{3,2,0,1:T(8,128)S(1)}, u32[]{:S(2)}, u32[]{:S(2)}) collective-permute-start(f32[4,2,32,128]{3,2,0,1:T(8,128)S(1)} %select_select_fusion), channel_id=1, source_target_pairs={{0,8},{1,9},{2,10},{3,11},{4,12},{5,13},{6,14},{7,15},{8,0},{9,1},... | collective-permute-start | bytes 393224 | tf_op jit(solution)/shard_map/ppermute | solution.py:235
  48.0 5.3 %collective-permute-done.3 = f32[4,2,32,128]{3,2,0,1:T(8,128)S(1)} collective-permute-done((f32[4,2,32,128]{3,2,0,1:T(8,128)S(1)}, f32[4,2,32,128]{3,2,0,1:T(8,128)S(1)}, u32[]{:S(2)}, u32[]{:S(2)}) %collective-permute-start.3) | collective-permute-done | bytes 131104 | tf_op jit(solution)/shard_map/ppermute | solution.py:235
  53.4 1.1 %collective-permute-start.4 = (f32[2,4,2,32,128]{4,3,2,1,0:T(8,128)S(1)}, f32[2,4,2,32,128]{4,3,2,1,0:T(8,128)S(1)}, u32[]{:S(2)}, u32[]{:S(2)}) collective-permute-start(f32[2,4,2,32,128]{4,3,2,1,0:T(8,128)S(1)} %pad_maximum_fusion.6), channel_id=1, source_target_pairs={{0,2},{1,3},{2,0},{3,1},{4,6},{5,7},{6,4},{7,5},{8,10},{9,11},{10,... | collective-permute-start | bytes 786440 | tf_op jit(solution)/shard_map/ppermute | solution.py:235
  54.5 0.1 copy.78
  54.6 0.1 sqrt.42
  54.7 0.1 copy.77
  54.8 0.1 squeeze.22
  54.9 0.1 copy.79
  55.0 0.1 squeeze.23
  55.1 5.8 %collective-permute-done.4 = f32[2,4,2,32,128]{4,3,2,1,0:T(8,128)S(1)} collective-permute-done((f32[2,4,2,32,128]{4,3,2,1,0:T(8,128)S(1)}, f32[2,4,2,32,128]{4,3,2,1,0:T(8,128)S(1)}, u32[]{:S(2)}, u32[]{:S(2)}) %collective-permute-start.4) | collective-permute-done | bytes 262176 | tf_op jit(solution)/shard_map/ppermute | solution.py:235
  61.0 0.1 multiply_subtract_fusion.3
  61.1 0.1 fusion.11
  61.3 0.9 copy-done.8
  62.2 0.3 copy-done.10
  62.5 17.3 %shard_map.138 = (f32[4096,128]{1,0:T(8,128)S(1)}, f32[16,2,32,128]{3,2,1,0:T(8,128)S(1)}, f32[16,2,32,128]{3,2,1,0:T(8,128)S(1)}, f32[16,4,128]{2,1,0:T(4,128)S(1)}) custom-call(bf16[4096,128]{1,0:T(8,128)(2,1)S(1)} %copy-done.8, bf16[4096,128]{1,0:T(8,128)(2,1)S(1)} %copy-done.10, f32[16,32,128]{2,1,0:T(8,128)S(1)} %get-tuple-element.95.re_ref, ...), custom_call_target="tpu_custom_call" | custom-call | flops 10000000000 | bytes 8388608 | tf_op jit(solution)/shard_map/pallas_call | solution.py:289
  79.9 0.1 broadcast_select_fusion
  80.1 1.1 %copy-done.11 = f32[4096,128]{1,0:T(8,128)} copy-done((f32[4096,128]{1,0:T(8,128)}, f32[4096,128]{1,0:T(8,128)S(1)}, u32[]{:S(2)}) %copy-start.11) | copy-done | bytes 2097176
  81.2 0.2 multiply_subtract_fusion
  81.4 0.3 fusion.4
  81.7 0.4 shard_map.140
  82.3 1.2 %collective-permute-done.6 = f32[4,16,128]{2,1,0:T(8,128)S(1)} collective-permute-done((f32[4,16,128]{2,1,0:T(8,128)S(1)}, f32[4,16,128]{2,1,0:T(8,128)S(1)}, u32[]{:S(2)}, u32[]{:S(2)}) %collective-permute-start.6) | collective-permute-done | bytes 32800 | tf_op jit(solution)/shard_map/ppermute | solution.py:235
  83.5 0.3 collective-permute-start.7
  83.8 3.6 %collective-permute-done.7 = f32[4,16,128]{2,1,0:T(8,128)S(1)} collective-permute-done((f32[4,16,128]{2,1,0:T(8,128)S(1)}, f32[4,16,128]{2,1,0:T(8,128)S(1)}, u32[]{:S(2)}, u32[]{:S(2)}) %collective-permute-start.7) | collective-permute-done | bytes 32800 | tf_op jit(solution)/shard_map/ppermute | solution.py:235
  87.4 1.2 %multiply_convert_fusion = bf16[4096,128]{1,0:T(8,128)(2,1)} fusion(bf16[4096,128]{1,0:T(8,128)(2,1)S(1)} %copy-done.13, bf16[4096,128]{1,0:T(8,128)(2,1)S(1)} %copy-done.1), kind=kLoop, calls=%fused_computation | loop fusion | flops 2097152 | bytes 3145728 | tf_op jit(solution)/shard_map/convert_element_type | solution.py:299
  88.7 0.1 squeeze.27
  88.7 0.1 squeeze.29
  88.8 0.1 copy.103
  88.9 0.1 copy.101
  89.0 0.1 div.68
  89.1 0.1 copy.102
  89.2 0.1 exp.76
  89.3 0.1 squeeze.30
  89.4 1.9 %collective-permute-done.8 = f32[4,16,128]{2,1,0:T(8,128)S(1)} collective-permute-done((f32[4,16,128]{2,1,0:T(8,128)S(1)}, f32[4,16,128]{2,1,0:T(8,128)S(1)}, u32[]{:S(2)}, u32[]{:S(2)}) %collective-permute-start.8) | collective-permute-done | bytes 32800 | tf_op jit(solution)/shard_map/ppermute | solution.py:235
  91.3 1.3 %collective-permute-start.9 = (f32[4,16,128]{2,1,0:T(8,128)S(1)}, f32[4,16,128]{2,1,0:T(8,128)S(1)}, u32[]{:S(2)}, u32[]{:S(2)}) collective-permute-start(f32[4,16,128]{2,1,0:T(8,128)S(1)} %add.219), channel_id=1, source_target_pairs={{0,8},{1,9},{2,10},{3,11},{4,12},{5,13},{6,14},{7,15},{8,0},{9,1},... | collective-permute-start | bytes 98312 | tf_op jit(solution)/shard_map/ppermute | solution.py:235
  92.6 1.2 %copy-done.4 = bf16[4096,128]{1,0:T(8,128)(2,1)S(1)} copy-done((bf16[4096,128]{1,0:T(8,128)(2,1)S(1)}, bf16[4096,128]{1,0:T(8,128)(2,1)}, u32[]{:S(2)}) %copy-start.4) | copy-done | bytes 1048600
  93.9 1.6 %copy-done.12 = f32[4096,128]{1,0:T(8,128)S(1)} copy-done((f32[4096,128]{1,0:T(8,128)S(1)}, f32[4096,128]{1,0:T(8,128)}, u32[]{:S(2)}) %copy-start.12) | copy-done | bytes 2097176
  95.4 11.6 %shard_map.139 = (bf16[4096,128]{1,0:T(8,128)(2,1)}, bf16[4096,128]{1,0:T(8,128)(2,1)}) custom-call(s32[4096]{0:T(1024)S(1)} %bitcast.55, f32[4096,128]{1,0:T(8,128)S(1)} %copy-done.12, f32[16,2,32,128]{3,2,1,0:T(8,128)S(1)} %get-tuple-element.63.yin_ref, f32[16,32,128]{2,1,0:T(8,128)S(1)} %get-tuple-element.95.re_ref, ...), custom_call_target="tpu_custom_call" | custom-call | flops 10000000000 | bytes 8388608 | tf_op jit(solution)/shard_map/pallas_call | solution.py:383
  107.0 0.1 slice.175
  107.1 0.7 copy.106
  107.9 0.7 copy.104
  108.7 0.7 copy.105
  (66 shorter events, 1.2 us)
Async XLA Ops:
  5.6 1.2 %copy-start = (bf16[4096,128]{1,0:T(8,128)(2,1)S(1)}, bf16[4096,128]{1,0:T(8,128)(2,1)}, u32[]{:S(2)}) copy-start(bf16[4096,128]{1,0:T(8,128)(2,1)} %go_ref.1) | copy-start | bytes 3145732
  6.8 1.2 %copy-start.2 = (bf16[4096,128]{1,0:T(8,128)(2,1)S(1)}, bf16[4096,128]{1,0:T(8,128)(2,1)}, u32[]{:S(2)}) copy-start(bf16[4096,128]{1,0:T(8,128)(2,1)} %q_ref.1) | copy-start | bytes 3145732
  8.0 0.7 copy-start.5
  20.5 1.3 %copy-start.7 = (bf16[4096,128]{1,0:T(8,128)(2,1)}, bf16[4096,128]{1,0:T(8,128)(2,1)S(1)}, u32[]{:S(2)}) copy-start(bf16[4096,128]{1,0:T(8,128)(2,1)S(1)} %get-tuple-element.16.gate_ref) | copy-start | bytes 3145732
  20.5 1.6 %copy-start.9 = (bf16[4096,128]{1,0:T(8,128)(2,1)}, bf16[4096,128]{1,0:T(8,128)(2,1)S(1)}, u32[]{:S(2)}) copy-start(bf16[4096,128]{1,0:T(8,128)(2,1)S(1)} %get-tuple-element.17.mixed_ref) | copy-start | bytes 3145732
  22.0 2.6 %collective-permute-start = (f32[24,2,32,128]{3,2,0,1:T(8,128)}, f32[24,2,32,128]{3,2,0,1:T(8,128)S(1)}, u32[]{:S(2)}, u32[]{:S(2)}) collective-permute-start(f32[24,2,32,128]{3,2,0,1:T(8,128)} %pad_maximum_fusion), channel_id=1, source_target_pairs={{0,1},{1,0},{2,3},{3,2},{4,5},{5,4},{6,7},{7,6},{8,9},{9,8},{10,11... | collective-permute-start | bytes 2359304 | tf_op jit(solution)/shard_map/ppermute | solution.py:235
  24.8 23.1 %copy-start.17 = (f32[2,128,16]{1,2,0:T(8,128)S(1)}, f32[2,128,16]{1,2,0:T(8,128)}, u32[]{:S(2)}) copy-start(f32[2,128,16]{1,2,0:T(8,128)} %param.17) | copy-start | bytes 49156
  24.9 12.4 %collective-permute-start.1 = (f32[12,2,32,128]{3,2,0,1:T(8,128)S(1)}, f32[12,2,32,128]{3,2,0,1:T(8,128)S(1)}, u32[]{:S(2)}, u32[]{:S(2)}) collective-permute-start(f32[12,2,32,128]{3,2,0,1:T(8,128)S(1)} %pad_maximum_fusion.3), channel_id=1, source_target_pairs={{0,2},{1,3},{2,0},{3,1},{4,6},{5,7},{6,4},{7,5},{8,10},{9,11},{10,... | collective-permute-start | bytes 1179656 | tf_op jit(solution)/shard_map/ppermute | solution.py:235
  37.4 7.9 %collective-permute-start.2 = (f32[8,2,32,128]{3,2,0,1:T(8,128)S(1)}, f32[8,2,32,128]{3,2,0,1:T(8,128)S(1)}, u32[]{:S(2)}, u32[]{:S(2)}) collective-permute-start(f32[8,2,32,128]{3,2,0,1:T(8,128)S(1)} %pad_maximum_fusion.5), channel_id=1, source_target_pairs={{0,4},{1,5},{2,6},{3,7},{4,0},{5,1},{6,2},{7,3},{8,12},{9,13},{10,... | collective-permute-start | bytes 786440 | tf_op jit(solution)/shard_map/ppermute | solution.py:235
  45.4 7.9 %collective-permute-start.3 = (f32[4,2,32,128]{3,2,0,1:T(8,128)S(1)}, f32[4,2,32,128]{3,2,0,1:T(8,128)S(1)}, u32[]{:S(2)}, u32[]{:S(2)}) collective-permute-start(f32[4,2,32,128]{3,2,0,1:T(8,128)S(1)} %select_select_fusion), channel_id=1, source_target_pairs={{0,8},{1,9},{2,10},{3,11},{4,12},{5,13},{6,14},{7,15},{8,0},{9,1},... | collective-permute-start | bytes 393224 | tf_op jit(solution)/shard_map/ppermute | solution.py:235
  53.4 7.5 %collective-permute-start.4 = (f32[2,4,2,32,128]{4,3,2,1,0:T(8,128)S(1)}, f32[2,4,2,32,128]{4,3,2,1,0:T(8,128)S(1)}, u32[]{:S(2)}, u32[]{:S(2)}) collective-permute-start(f32[2,4,2,32,128]{4,3,2,1,0:T(8,128)S(1)} %pad_maximum_fusion.6), channel_id=1, source_target_pairs={{0,2},{1,3},{2,0},{3,1},{4,6},{5,7},{6,4},{7,5},{8,10},{9,11},{10,... | collective-permute-start | bytes 786440 | tf_op jit(solution)/shard_map/ppermute | solution.py:235
  61.0 1.2 %copy-start.8 = (bf16[4096,128]{1,0:T(8,128)(2,1)S(1)}, bf16[4096,128]{1,0:T(8,128)(2,1)}, u32[]{:S(2)}) copy-start(bf16[4096,128]{1,0:T(8,128)(2,1)} %copy-done.7) | copy-start | bytes 3145732
  61.0 1.5 %copy-start.10 = (bf16[4096,128]{1,0:T(8,128)(2,1)S(1)}, bf16[4096,128]{1,0:T(8,128)(2,1)}, u32[]{:S(2)}) copy-start(bf16[4096,128]{1,0:T(8,128)(2,1)} %copy-done.9) | copy-start | bytes 3145732
  61.3 18.6 %collective-permute-start.5 = (f32[2,8,2,32,128]{4,3,2,1,0:T(8,128)S(1)}, f32[2,8,2,32,128]{4,3,2,1,0:T(8,128)S(1)}, u32[]{:S(2)}, u32[]{:S(2)}) collective-permute-start(f32[2,8,2,32,128]{4,3,2,1,0:T(8,128)S(1)} %pad_maximum_fusion.2), channel_id=1, source_target_pairs={{0,1},{1,0},{2,3},{3,2},{4,5},{5,4},{6,7},{7,6},{8,9},{9,8},{10,11... | collective-permute-start | bytes 1572872 | tf_op jit(solution)/shard_map/ppermute | solution.py:235
  79.9 1.4 %copy-start.11 = (f32[4096,128]{1,0:T(8,128)}, f32[4096,128]{1,0:T(8,128)S(1)}, u32[]{:S(2)}) copy-start(f32[4096,128]{1,0:T(8,128)S(1)} %get-tuple-element.18.conv_ref) | copy-start | bytes 6291460
  81.7 5.7 %copy-start.1 = (bf16[4096,128]{1,0:T(8,128)(2,1)S(1)}, bf16[4096,128]{1,0:T(8,128)(2,1)}, u32[]{:S(2)}) copy-start(bf16[4096,128]{1,0:T(8,128)(2,1)} %go_ref.1) | copy-start | bytes 3145732
  81.7 5.7 %copy-start.13 = (bf16[4096,128]{1,0:T(8,128)(2,1)S(1)}, bf16[4096,128]{1,0:T(8,128)(2,1)}, u32[]{:S(2)}) copy-start(bf16[4096,128]{1,0:T(8,128)(2,1)} %param.13) | copy-start | bytes 3145732
  82.1 6.7 %copy-start.14 = (f32[128,16]{0,1:T(8,128)S(1)}, f32[128,16]{0,1:T(8,128)}, u32[]{:S(2)}) copy-start(f32[128,16]{0,1:T(8,128)} %param.16) | copy-start | bytes 24580
  82.1 6.8 %copy-start.16 = (f32[128,16]{0,1:T(8,128)S(1)}, f32[128,16]{0,1:T(8,128)}, u32[]{:S(2)}) copy-start(f32[128,16]{0,1:T(8,128)} %get-tuple-element.114) | copy-start | bytes 24580
  82.1 7.0 %copy-start.15 = (f32[128,16]{0,1:T(8,128)S(1)}, f32[128,16]{0,1:T(8,128)}, u32[]{:S(2)}) copy-start(f32[128,16]{0,1:T(8,128)} %get-tuple-element.110) | copy-start | bytes 24580
  82.2 10.5 %copy-start.3 = (bf16[4096,128]{1,0:T(8,128)(2,1)S(1)}, bf16[4096,128]{1,0:T(8,128)(2,1)}, u32[]{:S(2)}) copy-start(bf16[4096,128]{1,0:T(8,128)(2,1)} %k_ref.3) | copy-start | bytes 3145732
  82.2 10.5 %copy-start.6 = (s32[32,128]{1,0:T(8,128)S(1)}, s32[32,128]{1,0:T(8,128)}, u32[]{:S(2)}) copy-start(s32[32,128]{1,0:T(8,128)} %shard_map.136) | copy-start | bytes 49156
  82.2 1.3 %collective-permute-start.6 = (f32[4,16,128]{2,1,0:T(8,128)S(1)}, f32[4,16,128]{2,1,0:T(8,128)S(1)}, u32[]{:S(2)}, u32[]{:S(2)}) collective-permute-start(f32[4,16,128]{2,1,0:T(8,128)S(1)} %shard_map.140), channel_id=1, source_target_pairs={{0,1},{1,0},{2,3},{3,2},{4,5},{5,4},{6,7},{7,6},{8,9},{9,8},{10,11... | collective-permute-start | bytes 98312 | tf_op jit(solution)/shard_map/ppermute | solution.py:235
  83.5 3.9 %collective-permute-start.7 = (f32[4,16,128]{2,1,0:T(8,128)S(1)}, f32[4,16,128]{2,1,0:T(8,128)S(1)}, u32[]{:S(2)}, u32[]{:S(2)}) collective-permute-start(f32[4,16,128]{2,1,0:T(8,128)S(1)} %add.217), channel_id=1, source_target_pairs={{0,2},{1,3},{2,0},{3,1},{4,6},{5,7},{6,4},{7,5},{8,10},{9,11},{10,... | collective-permute-start | bytes 98312 | tf_op jit(solution)/shard_map/ppermute | solution.py:235
  87.4 3.9 %collective-permute-start.8 = (f32[4,16,128]{2,1,0:T(8,128)S(1)}, f32[4,16,128]{2,1,0:T(8,128)S(1)}, u32[]{:S(2)}, u32[]{:S(2)}) collective-permute-start(f32[4,16,128]{2,1,0:T(8,128)S(1)} %add.218), channel_id=1, source_target_pairs={{0,4},{1,5},{2,6},{3,7},{4,0},{5,1},{6,2},{7,3},{8,12},{9,13},{10,... | collective-permute-start | bytes 98312 | tf_op jit(solution)/shard_map/ppermute | solution.py:235
  91.3 15.7 %collective-permute-start.9 = (f32[4,16,128]{2,1,0:T(8,128)S(1)}, f32[4,16,128]{2,1,0:T(8,128)S(1)}, u32[]{:S(2)}, u32[]{:S(2)}) collective-permute-start(f32[4,16,128]{2,1,0:T(8,128)S(1)} %add.219), channel_id=1, source_target_pairs={{0,8},{1,9},{2,10},{3,11},{4,12},{5,13},{6,14},{7,15},{8,0},{9,1},... | collective-permute-start | bytes 98312 | tf_op jit(solution)/shard_map/ppermute | solution.py:235
  92.6 1.2 %copy-start.4 = (bf16[4096,128]{1,0:T(8,128)(2,1)S(1)}, bf16[4096,128]{1,0:T(8,128)(2,1)}, u32[]{:S(2)}) copy-start(bf16[4096,128]{1,0:T(8,128)(2,1)} %v_ref.3) | copy-start | bytes 3145732
  93.9 1.6 %copy-start.12 = (f32[4096,128]{1,0:T(8,128)S(1)}, f32[4096,128]{1,0:T(8,128)}, u32[]{:S(2)}) copy-start(f32[4096,128]{1,0:T(8,128)} %copy-done.11) | copy-start | bytes 6291460

commit v2 on v1

v2 whole, which is shorter than its diff:
```python
import functools

import jax
import jax.numpy as jnp
from jax import lax
from jax.experimental import pallas as pl
from jax.experimental.pallas import tpu as pltpu
from jax.sharding import PartitionSpec as P

F32 = jnp.float32
BF16 = jnp.bfloat16
LANES = 128


def complex_product(a_real, a_imag, b_real, b_imag):
    return (a_real * b_real - a_imag * b_imag, a_real * b_imag + a_imag * b_real)


def split(x):
    hi = x.astype(BF16)
    return hi, (x - hi.astype(F32)).astype(BF16)


def dot(lhs, rhs, contract):
    return lax.dot_general(lhs, rhs, (contract, ((), ())), preferred_element_type=F32)


NN = ((1,), (0,))
NT = ((1,), (1,))
TN = ((0,), (0,))


def place(per_filter, filter_ref, pos_ref):
    rows = lax.broadcasted_iota(jnp.int32, (LANES, LANES), 0)
    cols = lax.broadcasted_iota(jnp.int32, (LANES, LANES), 1)
    before = (rows < cols).astype(F32).astype(BF16)
    ones = jnp.ones((LANES, LANES), BF16)
    pair = jnp.concatenate([before, ones], axis=1)
    seen = (rows * per_filter).astype(F32)
    for block in range(filter_ref.shape[0]):
        hot = rows == filter_ref[block : block + 1, :]
        counts = dot(hot.astype(F32).astype(BF16), pair, NN)
        spot = jnp.where(hot, counts[:, :LANES] + seen, 0.0)
        pos_ref[block : block + 1, :] = jnp.sum(spot, axis=0, keepdims=True).astype(jnp.int32)
        seen = seen + counts[:, LANES:]


def three(x):
    hi = x.astype(BF16)
    rest = x - hi.astype(F32)
    mid = rest.astype(BF16)
    return hi, mid, (rest - mid.astype(F32)).astype(BF16)


def block_picks(groups, per, modes):
    filters = groups * per
    group = lax.broadcasted_iota(jnp.int32, (groups, filters), 0)
    owner = lax.broadcasted_iota(jnp.int32, (groups, filters), 1) // per
    lane = lax.broadcasted_iota(jnp.int32, (per * modes, filters), 0) // modes
    inside = lax.broadcasted_iota(jnp.int32, (per * modes, filters), 1) % per
    return (group == owner).astype(F32).astype(BF16), lane == inside


def to_groups(values, picks, per):
    pick, inside = picks
    tiled = jnp.where(inside, jnp.concatenate([values] * per, axis=0), 0.0)
    return sum(dot(pick, part, NT) for part in three(tiled))


def from_groups(values, picks, per):
    pick, inside = picks
    spread = sum(dot(part, pick, TN) for part in three(values))
    spread = jnp.where(inside, spread, 0.0)
    modes = spread.shape[0] // per
    return sum(spread[f * modes : (f + 1) * modes] for f in range(per))


def mode_rates(decay_rate, twist, length):
    rho = decay_rate / length
    return rho, twist * rho, jnp.sqrt(1.0 - jnp.exp(-2.0 * rho))


def power_of(rho, angle, steps):
    mag = jnp.exp(-rho * steps)
    return mag * jnp.cos(angle * steps), mag * jnp.sin(angle * steps)


def factor_blocks(me, count):
    blocks = [1, 2]
    bit = 4
    while bit < count:
        upper = (me // bit) % 2
        inside = me % bit // 4
        blocks += [(upper * inside + (1 - upper) * (bit // 4 - 1 - inside)) * 4, bit]
        bit *= 2
    return blocks


def setup(per, count, me, rate_ref, twist_ref, res_ref, re_ref, im_ref, factor_ref):
    modes, filters = rate_ref.shape
    length = float(LANES * count)
    picks = block_picks(filters // per, per, modes)
    rho, angle, scale = mode_rates(rate_ref[...], twist_ref[...], length)
    rho, angle, rr, ri = (
        to_groups(part, picks, per)
        for part in (rho, angle, res_ref[0] * scale, res_ref[1] * scale)
    )
    re_ref[:, 32, :], im_ref[:, 32, :] = rr, ri
    for step in [0, *range(1, 9), *range(16, 128, 8)]:
        re, im = power_of(rho, angle, float(step))
        rows = []
        if step < 8:
            rows.append(step)
        if 0 < step <= 8:
            rows.append(16 - step)
        if step % 8 == 0:
            rows.append(16 + step // 8)
        for row in rows:
            re_ref[:, row, :], im_ref[:, row, :] = re, im
    for i, blocks in enumerate(factor_blocks(me, count)):
        steps = jnp.asarray(blocks, jnp.int32).astype(F32) * float(LANES)
        factor_ref[i, 0], factor_ref[i, 1] = power_of(rho, angle, steps)


def powers(re_ref, im_ref, group, backward):
    low = slice(8, 16) if backward else slice(0, 8)
    low_re, low_im = re_ref[group, low, :], im_ref[group, low, :]
    real, imag = [], []
    for a in range(16):
        row = 16 + (15 - a if backward else a)
        high_re, high_im = re_ref[group, row : row + 1, :], im_ref[group, row : row + 1, :]
        r, i = complex_product(high_re, high_im, low_re, low_im)
        real.append(r)
        imag.append(i)
    return jnp.concatenate(real, axis=0), jnp.concatenate(imag, axis=0)


def stacked(real, imag):
    hi, lo = split(jnp.concatenate([real, imag], axis=1))
    return jnp.concatenate([hi, lo], axis=0)


def own_filter(rows, lanes, members, modes):
    row = lax.broadcasted_iota(jnp.int32, (rows, lanes), 0) // members
    lane = (lax.broadcasted_iota(jnp.int32, (rows, lanes), 1) % LANES) // modes
    return row == lane


def mode_sum(data, table, members, modes):
    out = dot(jnp.concatenate([data, data], axis=1), table, NN)
    lane = (lax.broadcasted_iota(jnp.int32, (members, 2 * LANES), 1) % LANES) // modes
    total = jnp.zeros((members, 2 * LANES), F32)
    for f in range(data.shape[0] // members):
        total = jnp.where(lane == f, out[f * members : (f + 1) * members], total)
    return total


def states_kernel(
    members, modes, count, filter_hbm, rate_hbm, twist_hbm, res_hbm,
    go_hbm, q_hbm, k_hbm, v_hbm,
    gate_ref, mixed_ref, y_lo, y_hi, x_lo, x_hi, ahead_ref, pos_ref, re_hbm, im_hbm, factor_ref,
    go_ref, k_ref, v_ref,
    filter_ref, rate_ref, twist_ref, res_ref, q_ref,
    natural_g, natural_m, grouped_g, grouped_m, re_ref, im_ref, spot_ref, sems, load_sems,
):
    channels = go_ref.shape[0]
    loads = [
        pltpu.make_async_copy(source, target, load_sems.at[i])
        for i, (source, target) in enumerate(
            (
                (filter_hbm, filter_ref), (rate_hbm, rate_ref), (twist_hbm, twist_ref),
                (res_hbm, res_ref), (go_hbm, go_ref), (q_hbm, q_ref), (k_hbm, k_ref),
                (v_hbm, v_ref),
            )
        )
    ]
    for load in loads:
        load.start()
    for load in loads[:4]:
        load.wait()
    place(members, filter_ref, pos_ref)
    spots = pltpu.make_async_copy(pos_ref, spot_ref, sems.at[0])
    spots.start()
    me = lax.axis_index("seq")
    setup(LANES // modes, count, me, rate_ref, twist_ref, res_ref, re_ref, im_ref, factor_ref)
    tables = [
        pltpu.make_async_copy(re_ref, re_hbm, sems.at[1]),
        pltpu.make_async_copy(im_ref, im_hbm, sems.at[2]),
    ]
    for table in tables:
        table.start()
    tile = 256
    for load in loads[4:]:
        load.wait()

    @pl.loop(0, channels // tile)
    def _(i):
        at = pl.ds(pl.multiple_of(i * tile, tile), tile)
        gate = (go_ref[at, :].astype(F32) * q_ref[at, :].astype(F32)).astype(BF16)
        mixed = (k_ref[at, :].astype(F32) * v_ref[at, :].astype(F32)).astype(BF16)
        natural_g[at, :] = gate.astype(F32)
        natural_m[at, :] = mixed.astype(F32)

    spots.wait()

    @pl.loop(0, channels // LANES)
    def _(i):
        base = pl.multiple_of(i * LANES, LANES)
        for u in range(LANES):
            to = spot_ref[i, u]
            grouped_g[pl.ds(to, 1), :] = natural_g[pl.ds(base + u, 1), :]
            grouped_m[pl.ds(to, 1), :] = natural_m[pl.ds(base + u, 1), :]

    size = (LANES // modes) * members
    half = y_lo.shape[0]
    upper = me % 2
    for which, (y_ref, x_ref) in enumerate(((y_lo, x_lo), (y_hi, x_hi))):

        @pl.loop(0, half, unroll=4)
        def _(i, which=which, y_ref=y_ref, x_ref=x_ref):
            g = which * half + i
            at = pl.ds(pl.multiple_of(g * size, size), size)
            gate = grouped_g[at, :].astype(BF16)
            mixed = grouped_m[at, :].astype(BF16)
            gate_ref[at, :] = gate
            mixed_ref[at, :] = mixed
            y = mode_sum(gate, stacked(*powers(re_ref, im_ref, g, False)), members, modes)
            x = mode_sum(mixed, stacked(*powers(re_ref, im_ref, g, True)), members, modes)
            y_ref[i, 0], y_ref[i, 1] = y[:, :LANES], y[:, LANES:]
            x_ref[i, 0], x_ref[i, 1] = x[:, :LANES], x[:, LANES:]

    @pl.loop(0, half)
    def _(i):
        ahead_ref[i] = jnp.where(upper == 1, y_lo[i], y_hi[i])
        ahead_ref[half + i] = jnp.where(upper == 1, x_lo[i], x_hi[i])

    for table in tables:
        table.wait()


def rates_kernel(
    members, modes, gate_ref, mixed_ref, re_ref, im_ref, v_lo, v_hi, w_lo, w_hi, ahead_ref
):
    size = (LANES // modes) * members
    half = v_lo.shape[0]
    upper = lax.axis_index("seq") % 2
    step = lax.broadcasted_iota(jnp.int32, (LANES, LANES), 0).astype(F32)
    left = float(LANES) - step
    for which, (v_ref, w_ref) in enumerate(((v_lo, w_lo), (v_hi, w_hi))):

        @pl.loop(0, half, unroll=4)
        def _(i, which=which, v_ref=v_ref, w_ref=w_ref):
            g = which * half + i
            at = pl.ds(pl.multiple_of(g * size, size), size)
            head_re, head_im = powers(re_ref, im_ref, g, False)
            back_re, back_im = powers(re_ref, im_ref, g, True)
            v = mode_sum(gate_ref[at, :], stacked(step * head_re, step * head_im), members, modes)
            w = mode_sum(mixed_ref[at, :], stacked(left * back_re, left * back_im), members, modes)
            v_ref[i, 0], v_ref[i, 1] = v[:, :LANES], v[:, LANES:]
            w_ref[i, 0], w_ref[i, 1] = w[:, :LANES], w[:, LANES:]

    @pl.loop(0, half)
    def _(i):
        ahead_ref[i] = jnp.where(upper == 1, v_lo[i], v_hi[i])
        ahead_ref[half + i] = jnp.where(upper == 1, w_lo[i], w_hi[i])


def pair(ref, i):
    return [ref[i, 0], ref[i, 1]]


def pick(flag, yes, no):
    return [jnp.where(flag, a, b) for a, b in zip(yes, no)]


def plus(a, b):
    return [p + q for p, q in zip(a, b)]


def scaled(span, a):
    return [span * p for p in a]


def place_of(level):
    me = lax.axis_index("seq")
    low, high = me % 2, (me // 2) % 2
    return (low, high, 8 * low) if level == 0 else (high, None, 8 * low + 4 * high)


def merge_kernel(level, lo1, hi1, lo2, hi2, got_ref, factor_ref, *outs):
    upper, following, base = place_of(level)
    is_up = upper == 1
    n = lo1.shape[0]
    for i in range(n):
        p = (factor_ref[level, 0, pl.ds(base + i, 1), :], factor_ref[level, 1, pl.ds(base + i, 1), :])
        y, x = pick(is_up, pair(hi1, i), pair(lo1, i)), pick(is_up, pair(hi2, i), pair(lo2, i))
        got_y, got_x = pair(got_ref, i), pair(got_ref, n + i)
        t_y = plus(pick(is_up, got_y, y), complex_product(*p, *pick(is_up, y, got_y)))
        t_x = plus(pick(is_up, x, got_x), complex_product(*p, *pick(is_up, got_x, x)))
        if level == 0:
            which, at = divmod(i, n // 2)
            for ref, t in ((outs[which], t_y), (outs[2 + which], t_x)):
                ref[at, 0], ref[at, 1] = t
        else:
            for kind, t in enumerate((t_y, t_x)):
                outs[0][kind, i, 0], outs[0][kind, i, 1] = t
    if level == 0:
        y_lo, y_hi, x_lo, x_hi, ahead = outs
        for i in range(n // 2):
            ahead[i] = jnp.where(following == 1, y_lo[i], y_hi[i])
            ahead[n // 2 + i] = jnp.where(following == 1, x_lo[i], x_hi[i])


def rows_of(pair_):
    return [jnp.sum(part, axis=0, keepdims=True) for part in pair_]


def rate_merge_kernel(
    level, y_lo, y_hi, x_lo, x_hi, got_ref, v_lo, v_hi, w_lo, w_hi, more_ref, factor_ref, *outs
):
    upper, following, base = place_of(level)
    is_up = upper == 1
    span = float(LANES << level)
    n = y_lo.shape[0]
    sums_ref = outs[-1]
    for i in range(n):
        p = (factor_ref[level, 0, pl.ds(base + i, 1), :], factor_ref[level, 1, pl.ds(base + i, 1), :])
        own = [
            pick(is_up, pair(hi, i), pair(lo, i))
            for lo, hi in ((y_lo, y_hi), (x_lo, x_hi), (v_lo, v_hi), (w_lo, w_hi))
        ]
        got = [pair(got_ref, i), pair(got_ref, n + i), pair(more_ref, i), pair(more_ref, n + i)]
        y_up, v_up = pick(is_up, own[0], got[0]), pick(is_up, own[2], got[2])
        x_low, w_low = pick(is_up, got[1], own[1]), pick(is_up, got[3], own[3])
        v_low, w_up = pick(is_up, got[2], own[2]), pick(is_up, own[3], got[3])
        t_v = plus(v_low, complex_product(*p, *plus(v_up, scaled(span, y_up))))
        t_w = plus(w_up, complex_product(*p, *plus(w_low, scaled(span, x_low))))
        a = rows_of(complex_product(*x_low, *y_up))
        w = rows_of(plus(complex_product(*w_low, *y_up), complex_product(*x_low, *v_up)))
        for kind, row in enumerate((*a, *w)):
            sums_ref[kind, i : i + 1, :] = row
        if level == 0:
            which, at = divmod(i, n // 2)
            for ref, t in ((outs[which], t_v), (outs[2 + which], t_w)):
                ref[at, 0], ref[at, 1] = t
        else:
            for kind, t in enumerate((t_v, t_w)):
                outs[0][kind, i, 0], outs[0][kind, i, 1] = t
    if level == 0:
        ahead = outs[4]
        for i in range(n // 2):
            ahead[i] = jnp.where(following == 1, outs[0][i], outs[1][i])
            ahead[n // 2 + i] = jnp.where(following == 1, outs[2][i], outs[3][i])


def total_kernel(
    calls, yx_ref, vw_ref, into_y, into_x, factor_ref, sums0_ref, sums1_ref, *refs
):
    lags, out_ref = refs[:calls], refs[-1]
    _, _, base = place_of(1)
    half = place_of(0)[2]
    span = float(LANES << 2)
    g = 0
    for lag in lags:
        for i in range(lag.shape[0]):
            for kind in range(4):
                out_ref[kind, g : g + 1, :] = lag[i, kind : kind + 1, :]
            g += 1
    for i in range(sums0_ref.shape[1]):
        for kind in range(4):
            out_ref[kind, pl.ds(half + i, 1), :] += sums0_ref[kind, i : i + 1, :]
    for i in range(into_y.shape[0]):
        p = (factor_ref[3, 0, pl.ds(base + i, 1), :], factor_ref[3, 1, pl.ds(base + i, 1), :])
        y, x = pair(into_y, i), pair(into_x, i)
        own = [(yx_ref[1, i, 0], yx_ref[1, i, 1])] + [
            (vw_ref[kind, i, 0], vw_ref[kind, i, 1]) for kind in range(2)
        ]
        a = rows_of(complex_product(*own[0], *y))
        w = rows_of(plus(complex_product(*own[2], *y), complex_product(*own[1], *x)))
        far = complex_product(*p, *rows_of(complex_product(*x, *y)))
        w = plus(w, scaled(span, far))
        for kind, row in enumerate((*a, *w)):
            out_ref[kind, pl.ds(base + i, 1), :] += row + sums1_ref[kind, i : i + 1, :]


def scan_kernel(first, last, next_last, bit, at, total_ref, got_ref, factor_ref, *refs):
    me = lax.axis_index("seq")
    is_up = (me // bit) % 2 == 1
    before, outs = (None, refs) if first else (refs[:2], refs[2:])
    _, _, base = place_of(1)
    for i in range(total_ref.shape[1]):

        def factor(which):
            return tuple(factor_ref[which, c, pl.ds(base + i, 1), :] for c in range(2))

        got_y, got_x = pair(got_ref.at[0], i), pair(got_ref.at[got_ref.shape[0] - 1], i)
        y, x = pair(total_ref.at[0], i), pair(total_ref.at[1], i)
        far_y, far_x = got_y, got_x
        if not first:
            far_y, far_x = complex_product(*factor(at), *got_y), complex_product(*factor(at), *got_x)
        none = [jnp.zeros_like(part) for part in got_y]
        into = [pick(is_up, none, far_y), pick(is_up, far_x, none)]
        for kind in range(2):
            value = into[kind] if first else plus(pair(before[kind], i), into[kind])
            outs[kind][i, 0], outs[kind][i, 1] = value
        if last:
            continue
        t_y = plus(pick(is_up, got_y, y), complex_product(*factor(at + 1), *pick(is_up, y, got_y)))
        t_x = plus(pick(is_up, x, got_x), complex_product(*factor(at + 1), *pick(is_up, got_x, x)))
        for kind, t in enumerate((t_y, t_x)):
            outs[2][kind, i, 0], outs[2][kind, i, 1] = t
        if next_last:
            outs[3][0, i, 0], outs[3][0, i, 1] = pick((me // (2 * bit)) % 2 == 1, t_y, t_x)


def down_kernel(into_ref, other_ref, got_ref, later_ref, factor_ref, out_ref):
    low, high, base = place_of(0)
    is_up = high == 1
    n = into_ref.shape[0]
    for i in range(2 * n):
        k = i % n
        mine, other = pair(into_ref, k), pair(other_ref, k)
        into = pick(is_up, other, mine) if i < n else pick(is_up, mine, other)
        own = pair(got_ref, k) if i < n else pair(later_ref, k)
        p = tuple(factor_ref[1, c, pl.ds(base + i, 1), :] for c in range(2))
        out_ref[i, 0], out_ref[i, 1] = pick(is_up, into, plus(own, complex_product(*p, *into)))


def add_kernel(a_ref, b_ref, out_ref):
    out_ref[...] = a_ref[...] + b_ref[...]


def conv_kernel(
    members, modes, gate_ref, mixed_ref, re_ref, im_ref,
    conv_ref, sums_ref, lag,
):
    per = LANES // modes
    head_re, head_im = powers(re_ref, im_ref, 0, False)
    step = lax.broadcasted_iota(jnp.int32, (LANES, LANES), 0).astype(F32)
    gate, mixed = gate_ref[...], mixed_ref[...]
    der = stacked(step * head_re, step * head_im)
    head = stacked(head_re, head_im)
    head_hi, head_lo = head[:LANES], head[LANES:]
    own8 = own_filter(per, 2 * LANES, 1, modes)
    res = jnp.concatenate([re_ref[0, 32:33, :], -im_ref[0, 32:33, :]], axis=1)
    res_hi, res_lo = split(jnp.where(own8, res, 0.0))
    filt = dot(res_hi, head_hi, NT) + dot(res_lo, head_hi, NT) + dot(res_hi, head_lo, NT)
    row = lax.broadcasted_iota(jnp.int32, (LANES, LANES), 0)
    col = lax.broadcasted_iota(jnp.int32, (LANES, LANES), 1)
    causal = col >= row
    mirror = (row + col == LANES - 1).astype(F32).astype(BF16)
    mirrored = dot(mixed, mirror, NN).astype(BF16)
    for f in range(per):
        at = slice(f * members, (f + 1) * members)
        wide = jnp.broadcast_to(filt[f : f + 1, :], (LANES, LANES))
        shifted = pltpu.roll(wide, 0, 1, stride=1, stride_axis=0)
        hi, lo = split(jnp.where(causal, shifted, 0.0))
        gate_f = gate[at]
        conv_ref[at, :] = dot(gate_f, hi, NT) + dot(gate_f, lo, NT)
        corr = jnp.where(row + col >= LANES - 1, dot(mirrored[at], gate_f, TN), 0.0)
        aligned = pltpu.roll(corr, 1, 1, stride=1, stride_axis=0)
        lag[f : f + 1, :] = jnp.sum(aligned, axis=0, keepdims=True)
    lag_hi, lag_lo = split(lag[...])
    for which, table in enumerate((head, der)):
        hi, lo = table[:LANES], table[LANES:]
        out = dot(lag_hi, hi, NN) + dot(lag_lo, hi, NN) + dot(lag_hi, lo, NN)
        out = jnp.sum(jnp.where(own8, out, 0.0), axis=0, keepdims=True)
        sums_ref[0, 2 * which : 2 * which + 1, :] = out[:, :LANES]
        sums_ref[0, 2 * which + 1 : 2 * which + 2, :] = out[:, LANES:]


def cross_kernel(
    members, modes, calls, mine_ref, other_ref, near_ref, later_ref, factor_ref, re_ref, im_ref,
    *refs,
):
    convs, out_ref = refs[:calls], refs[calls]
    per = LANES // modes
    size = per * members
    half = mine_ref.shape[0]
    is_up = lax.axis_index("seq") % 2 == 1
    lane = (lax.broadcasted_iota(jnp.int32, (members, 2 * LANES), 1) % LANES) // modes
    first = 0
    for conv_ref in convs:
        for i in range(conv_ref.shape[0] // size):
            g = first + i
            back_re, back_im = powers(re_ref, im_ref, g, True)
            rr, ri = re_ref[g, 32:33, :], im_ref[g, 32:33, :]
            coef_re, coef_im = complex_product(rr, ri, back_re, back_im)
            coef_hi, coef_lo = split(jnp.concatenate([coef_re, -coef_im], axis=1))
            k = g % half
            mine, other = pair(mine_ref, k), pair(other_ref, k)
            into = pick(is_up, other, mine) if g < half else pick(is_up, mine, other)
            own = pair(near_ref if g < half else later_ref, k)
            p = (factor_ref[0, 0, g : g + 1, :], factor_ref[0, 1, g : g + 1, :])
            yin = pick(is_up, into, plus(own, complex_product(*p, *into)))
            yin = jnp.concatenate(yin, axis=1)
            wide = jnp.concatenate([jnp.where(lane == f, yin, 0.0) for f in range(per)], axis=0)
            hi, lo = split(wide)
            total = dot(hi, coef_hi, NT) + dot(lo, coef_hi, NT) + dot(hi, coef_lo, NT)
            out_ref[g * size : (g + 1) * size, :] = conv_ref[i * size : (i + 1) * size, :] + total
        first += conv_ref.shape[0] // size


def finish_kernel(pos_ref, grouped, k_ref, v_ref, gk_hbm, gv_hbm, natural, gk_ref, gv_ref, sems):
    channels = k_ref.shape[0]
    tile = 256

    @pl.loop(0, channels // tile)
    def _(i):
        for part in range(tile // LANES):
            block = i * (tile // LANES) + part
            base = pl.multiple_of(block * LANES, LANES)
            for u in range(LANES):
                natural[pl.ds(base + u, 1), :] = grouped[pl.ds(pos_ref[block, u], 1), :]
        at = pl.ds(pl.multiple_of(i * tile, tile), tile)
        conv = natural[at, :]
        gk_ref[at, :] = (conv * v_ref[at, :].astype(F32)).astype(BF16)
        gv_ref[at, :] = (conv * k_ref[at, :].astype(F32)).astype(BF16)
        pltpu.make_async_copy(gk_ref.at[at, :], gk_hbm.at[at, :], sems.at[0]).start()
        pltpu.make_async_copy(gv_ref.at[at, :], gv_hbm.at[at, :], sems.at[1]).start()

    pltpu.make_async_copy(gk_ref, gk_hbm, sems.at[0]).wait()
    pltpu.make_async_copy(gv_ref, gv_hbm, sems.at[1]).wait()


def product_kernel(a_ref, b_hbm, out_hbm, b_ref, out_ref, sems):
    rows = a_ref.shape[0] // 4
    parts = [pl.ds(i * rows, rows) for i in range(4)]
    loads = [
        pltpu.make_async_copy(b_hbm.at[at, :], b_ref.at[at, :], sems.at[i])
        for i, at in enumerate(parts)
    ]
    for load in loads:
        load.start()
    stores = []
    for i, at in enumerate(parts):
        loads[i].wait()
        out_ref[at, :] = (a_ref[at, :].astype(F32) * b_ref[at, :].astype(F32)).astype(BF16)
        stores.append(
            pltpu.make_async_copy(out_ref.at[at, :], out_hbm.at[at, :], sems.at[4 + i])
        )
        stores[-1].start()
    for store in stores:
        store.wait()


def params_kernel(
    per, length, total_ref, last_ref, rate_ref, twist_ref, res_ref, log_rate_ref, grad_twist_ref, grad_res_ref
):
    modes, filters = rate_ref.shape
    picks = block_picks(filters // per, per, modes)
    rate, twist = rate_ref[...], twist_ref[...]
    rho, angle, scale = mode_rates(rate, twist, length)
    a_re, a_im, w_re, w_im = (
        from_groups(total_ref[i] + last_ref[i], picks, per) for i in range(4)
    )
    r0, r1 = res_ref[0], res_ref[1]
    b_re, b_im = complex_product(r0 * scale, r1 * scale, w_re, w_im)
    slope = rho * jnp.exp(-2.0 * rho) / scale
    log_rate_ref[...] = (r0 * a_re - r1 * a_im) * slope - b_re * rho - b_im * angle
    grad_twist_ref[...] = -b_im * rho
    grad_res_ref[0] = scale * a_re
    grad_res_ref[1] = -scale * a_im


def vmem(n):
    return [pl.BlockSpec(memory_space=pltpu.VMEM)] * n


SMEM = pl.BlockSpec(memory_space=pltpu.SMEM)


def params(mebibytes):
    return pltpu.CompilerParams(vmem_limit_bytes=mebibytes << 20)


def pinned(value):
    return pltpu.with_memory_space_constraint(value, pltpu.HBM)


def swap(value, bit):
    count = lax.axis_size("seq")
    return lax.ppermute(value, "seq", [(i, i ^ bit) for i in range(count)])


def lower_only(value, bit):
    count = lax.axis_size("seq")
    return lax.ppermute(value, "seq", [(i, i ^ bit) for i in range(count) if i & bit])


def together(*values):
    return lax.optimization_barrier(values)


def body(grad_out, query, key, value, conv_out, channel_filter, decay_rate, twist, residues):
    channels, positions = grad_out.shape
    filters, modes = decay_rate.shape
    members = channels // filters
    per = LANES // modes
    groups = filters // per
    count = lax.axis_size("seq")
    me = lax.axis_index("seq")
    length = positions * count
    shape = jax.ShapeDtypeStruct
    half, quarter = groups // 2, groups // 4

    def state(*lead):
        return shape((*lead, 2, members, LANES), F32)

    rates, twists = decay_rate.T, twist.T
    poles = jnp.swapaxes(residues, 1, 2)
    number = len(factor_blocks(0, count))
    hbm = pl.BlockSpec(memory_space=pltpu.HBM)
    wide = (channels, positions)
    blocks = (channels // LANES, LANES)
    table_shape = (groups, 40, LANES)
    (
        gate, mixed, y_lo, y_hi, x_lo, x_hi, ahead, pos, tab_re, tab_im, factors,
        own_out, own_key, own_value,
    ) = pl.pallas_call(
        functools.partial(states_kernel, members, modes, count),
        out_shape=(
            shape(wide, BF16), shape(wide, BF16), *[state(half)] * 4, state(groups),
            shape(blocks, jnp.int32), shape(table_shape, F32), shape(table_shape, F32),
            shape((number, 2, groups, LANES), F32), *[shape(wide, BF16)] * 3,
        ),
        in_specs=[hbm] * 8,
        out_specs=tuple(vmem(8) + [hbm] * 2 + vmem(4)),
        scratch_shapes=[
            pltpu.VMEM(blocks, jnp.int32), pltpu.VMEM((modes, filters), F32),
            pltpu.VMEM((modes, filters), F32), pltpu.VMEM((2, modes, filters), F32),
            pltpu.VMEM(wide, BF16), *[pltpu.VMEM(wide, F32)] * 4,
            *[pltpu.VMEM(table_shape, F32)] * 2, pltpu.SMEM(blocks, jnp.int32),
            pltpu.SemaphoreType.DMA((3,)), pltpu.SemaphoreType.DMA((8,)),
        ],
        compiler_params=params(20),
    )(
        *(
            pinned(part)
            for part in (
                channel_filter.reshape(blocks), rates, twists, poles,
                grad_out, query, key, value,
            )
        )
    )

    size = per * members

    def conv_call(first, number):
        rows = pl.BlockSpec((size, positions), lambda g: (g + first, 0))
        table = pl.BlockSpec((1, 40, LANES), lambda g: (g + first, 0, 0))
        return pl.pallas_call(
            functools.partial(conv_kernel, members, modes),
            grid=(number,),
            out_shape=(shape((number * size, positions), F32), shape((number, 4, LANES), F32)),
            in_specs=[rows, rows, table, table],
            out_specs=(
                pl.BlockSpec((size, positions), lambda g: (g, 0)),
                pl.BlockSpec((1, 4, LANES), lambda g: (g, 0, 0)),
            ),
            scratch_shapes=[pltpu.VMEM((per, LANES), F32)],
            compiler_params=params(8),
            cost_estimate=pl.CostEstimate(
                flops=number * 10**9, bytes_accessed=number << 19, transcendentals=0
            ),
        )(gate, mixed, tab_re, tab_im)

    def merge(level, *args):
        n = half >> level
        if level == 0:
            outs = (*[state(n // 2)] * 4, state(n))
        else:
            outs = (state(2, n),)
        return pl.pallas_call(
            functools.partial(merge_kernel, level),
            out_shape=outs,
            in_specs=vmem(6),
            out_specs=tuple(vmem(len(outs))),
            compiler_params=params(8),
        )(*args, factors)

    def rate_merge(level, *args):
        n = half >> level
        sums = shape((4, n, LANES), F32)
        if level == 0:
            outs = (*[state(n // 2)] * 4, state(n), sums)
        else:
            outs = (state(2, n), sums)
        return pl.pallas_call(
            functools.partial(rate_merge_kernel, level),
            out_shape=outs,
            in_specs=vmem(11),
            out_specs=tuple(vmem(len(outs))),
            compiler_params=params(8),
        )(*args, factors)

    got0 = swap(ahead, 1)
    ty_lo, ty_hi, tx_lo, tx_hi, ahead1 = merge(0, y_lo, y_hi, x_lo, x_hi, got0)
    ahead1, gate, mixed = together(ahead1, gate, mixed)
    got1 = swap(ahead1, 2)
    later0 = lower_only(y_hi, 1)
    vw = pl.pallas_call(
        functools.partial(rates_kernel, members, modes),
        out_shape=(*[state(half)] * 4, state(groups)),
        in_specs=vmem(4),
        out_specs=tuple(vmem(5)),
        compiler_params=params(8),
        cost_estimate=pl.CostEstimate(flops=3 * 10**9, bytes_accessed=4 << 20, transcendentals=0),
    )(gate, mixed, tab_re, tab_im)
    vw, gate, mixed = together(vw, gate, mixed)
    more0 = swap(vw[4], 1)
    parts = [4, 6, groups - 10]
    made = [conv_call(0, parts[0])]
    got1, more0, made[0] = together(got1, more0, made[0])
    (yx,) = merge(1, ty_lo, ty_hi, tx_lo, tx_hi, got1)

    base = 4
    bit, at = base, 2
    tot, sent, into = yx, yx, ()
    while bit < count:
        last, next_last = bit * 2 >= count, bit * 4 >= count
        sent, gate, mixed = together(sent, gate, mixed)
        got = swap(sent, bit)
        if bit == base:
            rate0 = rate_merge(0, y_lo, y_hi, x_lo, x_hi, got0, *vw[:4], more0)
            more1, gate, mixed = together(rate0[4], gate, mixed)
            more1 = swap(more1, 2)
            later1 = lower_only(ty_hi, 2)
        if bit == base or last:
            first = sum(parts[: len(made)])
            conv = conv_call(first, groups - first if last else parts[len(made)])
            got, conv = together(got, conv)
            made.append(conv)
        outs = [state(quarter)] * 2
        if not last:
            outs.append(state(2, quarter))
            if next_last:
                outs.append(state(1, quarter))
        outs = pl.pallas_call(
            functools.partial(scan_kernel, bit == base, last, next_last, bit, at),
            out_shape=tuple(outs),
            in_specs=vmem(3 + len(into)),
            out_specs=tuple(vmem(len(outs))),
            compiler_params=params(4),
        )(tot, got, factors, *into)
        into = outs[:2]
        if not last:
            tot, sent = outs[2], outs[-1]
        bit *= 2
        at += 2
    into_y, into_x = into
    convs, lags = zip(*made)
    calls = len(convs)
    rate1 = rate_merge(1, ty_lo, ty_hi, tx_lo, tx_hi, got1, *rate0[:4], more1)
    total = pl.pallas_call(
        functools.partial(total_kernel, calls),
        out_shape=shape((4, groups, LANES), F32),
        in_specs=vmem(7 + calls),
        out_specs=vmem(1)[0],
        compiler_params=params(8),
    )(yx, rate1[0], into_y, into_x, factors, rate0[5], rate1[1], *lags)

    def add(a, b):
        return pl.pallas_call(
            add_kernel,
            out_shape=shape((4, groups, LANES), F32),
            in_specs=vmem(2),
            out_specs=vmem(1)[0],
            compiler_params=params(2),
        )(a, b)

    other = swap(into_y, 2)
    total = add(total, swap(total, 1))
    got = swap(total, 2)
    chip = pl.pallas_call(
        down_kernel,
        out_shape=state(half),
        in_specs=vmem(5),
        out_specs=vmem(1)[0],
        compiler_params=params(4),
    )(into_y, other, got1, later1, factors)
    grad_query = pl.pallas_call(
        product_kernel,
        out_shape=shape(wide, BF16),
        in_specs=vmem(1) + [hbm],
        out_specs=hbm,
        scratch_shapes=[pltpu.VMEM(wide, BF16)] * 2 + [pltpu.SemaphoreType.DMA((8,))],
        compiler_params=params(8),
        cost_estimate=pl.CostEstimate(flops=10**9, bytes_accessed=3 << 20, transcendentals=0),
    )(own_out, pinned(conv_out))
    total = add(total, got)
    total, chip = together(total, chip)
    got = swap(total, 4)
    chip_other = swap(chip, 1)
    cost = pl.CostEstimate(flops=4 * 10**9, bytes_accessed=4 << 20, transcendentals=0)
    grouped = pl.pallas_call(
        functools.partial(cross_kernel, members, modes, calls),
        out_shape=shape(wide, F32),
        in_specs=vmem(7 + calls),
        out_specs=vmem(1)[0],
        compiler_params=params(12),
        cost_estimate=cost,
    )(chip, chip_other, got0, later0, factors, tab_re, tab_im, *convs)
    got, grouped = together(got, grouped)
    total = add(total, got)
    bit = 8
    while bit * 2 < count:
        total = add(total, swap(total, bit))
        bit *= 2
    total, grouped = together(total, grouped)
    got = swap(total, bit)
    grad_key, grad_value = pl.pallas_call(
        finish_kernel,
        out_shape=(shape(wide, BF16), shape(wide, BF16)),
        in_specs=[SMEM] + vmem(3),
        out_specs=(hbm, hbm),
        scratch_shapes=[pltpu.VMEM(wide, F32)] + [pltpu.VMEM(wide, BF16)] * 2
        + [pltpu.SemaphoreType.DMA((2,))],
        compiler_params=params(12),
        cost_estimate=cost,
    )(pos, grouped, own_key, own_value)
    got, grad_key, grad_value = together(got, grad_key, grad_value)
    one = shape((modes, filters), F32)
    log_rate, grad_twist, grad_res = pl.pallas_call(
        functools.partial(params_kernel, per, float(length)),
        out_shape=(one, one, shape((2, modes, filters), F32)),
        in_specs=vmem(5),
        out_specs=tuple(vmem(3)),
        compiler_params=params(4),
    )(total, got, rates, twists, poles)
    return (
        grad_query, grad_key, grad_value, log_rate.T, grad_twist.T, jnp.swapaxes(grad_res, 1, 2)
    )


def solution(mesh):
    wide = P(None, ("groups", "seq"))
    return jax.shard_map(
        body,
        mesh=mesh,
        in_specs=(wide,) * 5 + (P(),) * 4,
        out_specs=(wide, wide, wide, P("groups", None), P("groups", None), P("groups", None, None)),
        check_vma=False,
    )
```

time: 110 us -> 63.6 us (0.58)
  waiting for transfers between devices: 35.2 us -> 7.39 us
  local copies, waits for them, and re-layouts: 12.6 us -> 0.01 us
  other arithmetic: 6.62 us -> 0 us
  starting transfers between devices: 10.7 us -> 15.4 us
  Pallas kernels: 43.1 us -> 39.7 us
    ppermute x10 -> x12, waiting for transfers between devices: 35.2 us -> 7.38 us  [swap(): return lax.ppermute(value, 'seq', [(i, i ^ bit) for i in range(count)])]
    unnamed x40 -> x6, local copies, waits for them, and re-layouts: 10.8 us -> 0.01 us
    pallas_call x5 -> x20, Pallas kernels: 43.1 us -> 39.7 us  [the longest x3 16.3 us: conv_call(): pl.pallas_call(functools.partial(conv_kernel, members, modes), grid=(numb...]
    ppermute x0 -> x2, starting transfers between devices: none -> 2.56 us  [lower_only(): lax.ppermute(value, 'seq', [(i, i ^ bit) for i in range(count) if i & bit])]
    ppermute x10 -> x12, starting transfers between devices: 10.7 us -> 12.8 us  [swap(): return lax.ppermute(value, 'seq', [(i, i ^ bit) for i in range(count)])]
    exp x1 -> x0, other arithmetic: 1.33 us -> none  [body(): scale = jnp.sqrt(1.0 - jnp.exp(-2.0 * rho))]
    mul x7 -> x0, other arithmetic: 1.25 us -> none  [the longest x1 1.03 us: power(): return (mag * jnp.cos(phase), mag * jnp.sin(phase))]
    convert_element_type x1 -> x0, other arithmetic: 1.24 us -> none  [body(): grad_query = (grad_out.astype(F32) * conv_out.astype(F32)).astype(BF16)]
  transfers between devices with their start and end apart: 10 -> 14, of which waited for: 8 -> 5; matrix products, arithmetic and copies ran while one was open for 2% -> 0% of each run, Pallas kernels for 26% -> 41%
where the time goes in v2:
time: 63.6 us; the launch traced here: 63.3 us
  Pallas kernels  39.7 us (62%)
  starting transfers between devices  15.4 us (24%)
  waiting for transfers between devices  7.39 us (12%)
  between operations  0.84 us (1%)
    pallas_call x3, Pallas kernels, conv_call(): pl.pallas_call(functools.partial(conv_kernel, members, modes), grid=(numb...  16.3 us
    ppermute x12, starting transfers between devices, swap(): return lax.ppermute(value, 'seq', [(i, i ^ bit) for i in range(count)])  12.8 us
    pallas_call x1, Pallas kernels, body(): pl.pallas_call(functools.partial(states_kernel, members, modes, count), o...  10.3 us
    ppermute x12, waiting for transfers between devices, swap(): return lax.ppermute(value, 'seq', [(i, i ^ bit) for i in range(count)])  7.38 us
    pallas_call x1, Pallas kernels, body(): pl.pallas_call(finish_kernel, out_shape=(shape(wide, BF16), shape(wide, B...  5.12 us
    ppermute x2, starting transfers between devices, lower_only(): lax.ppermute(value, 'seq', [(i, i ^ bit) for i in range(count) if i & bit])  2.56 us
    pallas_call x1, Pallas kernels, body(): pl.pallas_call(functools.partial(rates_kernel, members, modes), out_shape...  2.07 us
    pallas_call x1, Pallas kernels, body(): pl.pallas_call(product_kernel, out_shape=shape(wide, BF16), in_specs=vmem...  2.04 us
  transfers between devices with their start and end apart: 14, of which 5 were waited for; matrix products, arithmetic and copies ran while one was open for 0% of the time, Pallas kernels for 41%

profile of v2, /device:TPU:0, one launch (start us, length us, event | category | flops | bytes accessed | tf_op | source)
XLA Modules:
  0.0 63.3 jit_solution(14333463427025950264)
XLA Ops:
  0.6 10.3 %shard_map.136 = (bf16[4096,128]{1,0:T(8,128)(2,1)S(1)}, bf16[4096,128]{1,0:T(8,128)(2,1)S(1)}, f32[8,2,32,128]{3,2,1,0:T(8,128)S(1)}, f32[8,2,32,128]{3,2,1,0:T...) custom-call(s32[32,128]{1,0:T(8,128)} %bitcast.13, ...), custom_call_target="tpu_custom_call" | custom-call | tf_op jit(solution)/shard_map/pallas_call | solution.py:620
  10.9 0.5 collective-permute-start
  11.5 1.5 %collective-permute-done.got_ref.near_ref = f32[16,2,32,128]{3,2,1,0:T(8,128)S(1)} collective-permute-done((f32[16,2,32,128]{3,2,1,0:T(8,128)S(1)}, f32[16,2,32,128]{3,2,1,0:T(8,128)S(1)}, u32[]{:S(2)}, u32[]{:S(2)}) %collective-permute-start) | collective-permute-done | bytes 524320 | tf_op jit(solution)/shard_map/ppermute | solution.py:583
  13.0 0.1 shard_map.138
  13.1 2.1 %shard_map.139 = (f32[8,2,32,128]{3,2,1,0:T(8,128)S(1)}, f32[8,2,32,128]{3,2,1,0:T(8,128)S(1)}, f32[8,2,32,128]{3,2,1,0:T(8,128)S(1)}, f32[8,2,32,128]{3,2,1,0:T(8,128)S(1)}, f32[16,2,32,128]{3,2,1,0:T(8,128)S(1)}) custom-call(bf16[4096,128]{1,0:T(8,128)(2,1)S(1)} %get-tuple-element.146.gate_ref, bf16[4096,128]{1,0:T(8,128)(2,1)S(1)} %get-tuple-element.147.mixed_ref, ...), custom_call_target="tpu_custom_call" | custom-call | flops 3000000000 | bytes 4194304 | tf_op jit(solution)/shard_map/pallas_call | solution.py:702
  15.2 0.4 collective-permute-start.2
  15.7 2.7 %collective-permute-start.1 = (f32[8,2,32,128]{3,2,1,0:T(8,128)S(1)}, f32[8,2,32,128]{3,2,1,0:T(8,128)S(1)}, u32[]{:S(2)}, u32[]{:S(2)}) collective-permute-start(f32[8,2,32,128]{3,2,1,0:T(8,128)S(1)} %get-tuple-element.107), channel_id=1, source_target_pairs={{0,2},{1,3},{2,0},{3,1},{4,6},{5,7},{6,4},{7,5},{8,10},{9,11},{10,... | collective-permute-start | bytes 786440 | tf_op jit(solution)/shard_map/ppermute | solution.py:583
  18.3 1.3 %collective-permute-start.9 = (f32[4,2,32,128]{3,2,1,0:T(8,128)S(1)}, f32[4,2,32,128]{3,2,1,0:T(8,128)S(1)}, u32[]{:S(2)}, u32[]{:S(2)}) collective-permute-start(f32[4,2,32,128]{3,2,1,0:T(8,128)S(1)} %get-tuple-element.101.hi1.y_hi), channel_id=1, source_target_pairs={{2,0},{3,1},{6,4},{7,5},{10,8},{11,9},{14,12},{15,13},{18,16},{19,... | collective-permute-start | bytes 393224 | tf_op jit(solution)/shard_map/ppermute | solution.py:588
  19.6 4.1 %shard_map.140 = (f32[1024,128]{1,0:T(8,128)S(1)}, f32[4,4,128]{2,1,0:T(4,128)S(1)}) custom-call(bf16[4096,128]{1,0:T(8,128)(2,1)S(1)} %get-tuple-element.146.gate_ref, bf16[4096,128]{1,0:T(8,128)(2,1)S(1)} %get-tuple-element.147.mixed_ref, f32[16,40,128]{2,1,0:T(8,128)S(1)} %get-tuple-element.110.re_ref, f32[16,40,128]{2,1,0:T(8,128)S(1)} %get-tuple-element.111.im_ref), custom_call_target="tpu_custom_call" | custom-call | flops 4000000000 | bytes 2097152 | tf_op jit(solution)/shard_map/pallas_call | solution.py:652
  23.7 1.8 %collective-permute-done.1.got_ref = f32[8,2,32,128]{3,2,1,0:T(8,128)S(1)} collective-permute-done((f32[8,2,32,128]{3,2,1,0:T(8,128)S(1)}, f32[8,2,32,128]{3,2,1,0:T(8,128)S(1)}, u32[]{:S(2)}, u32[]{:S(2)}) %collective-permute-start.1) | collective-permute-done | bytes 262176 | tf_op jit(solution)/shard_map/ppermute | solution.py:583
  25.5 0.0 collective-permute-done.2.more_ref
  25.5 0.1 shard_map.141.total_ref.yx_ref
  25.5 0.3 shard_map.142
  25.9 1.5 %collective-permute-start.3 = (f32[8,2,32,128]{3,2,1,0:T(8,128)S(1)}, f32[8,2,32,128]{3,2,1,0:T(8,128)S(1)}, u32[]{:S(2)}, u32[]{:S(2)}) collective-permute-start(f32[8,2,32,128]{3,2,1,0:T(8,128)S(1)} %get-tuple-element.135), channel_id=1, source_target_pairs={{0,2},{1,3},{2,0},{3,1},{4,6},{5,7},{6,4},{7,5},{8,10},{9,11},{10,... | collective-permute-start | bytes 786440 | tf_op jit(solution)/shard_map/ppermute | solution.py:583
  27.4 1.6 %collective-permute-start.4 = (f32[2,4,2,32,128]{4,3,2,1,0:T(8,128)S(1)}, f32[2,4,2,32,128]{4,3,2,1,0:T(8,128)S(1)}, u32[]{:S(2)}, u32[]{:S(2)}) collective-permute-start(f32[2,4,2,32,128]{4,3,2,1,0:T(8,128)S(1)} %shard_map.141.total_ref.yx_ref), channel_id=1, source_target_pairs={{0,4},{1,5},{2,6},{3,7},{4,0},{5,1},{6,2},{7,3},{8,12},{9,13},{10,... | collective-permute-start | bytes 786440 | tf_op jit(solution)/shard_map/ppermute | solution.py:583
  29.0 6.1 %shard_map.144 = (f32[1536,128]{1,0:T(8,128)S(1)}, f32[6,4,128]{2,1,0:T(4,128)S(1)}) custom-call(bf16[4096,128]{1,0:T(8,128)(2,1)S(1)} %get-tuple-element.146.gate_ref, bf16[4096,128]{1,0:T(8,128)(2,1)S(1)} %get-tuple-element.147.mixed_ref, f32[16,40,128]{2,1,0:T(8,128)S(1)} %get-tuple-element.110.re_ref, f32[16,40,128]{2,1,0:T(8,128)S(1)} %get-tuple-element.111.im_ref), custom_call_target="tpu_custom_call" | custom-call | flops 6000000000 | bytes 3145728 | tf_op jit(solution)/shard_map/pallas_call | solution.py:652
  35.1 0.0 collective-permute-done.4.got_ref
  35.1 0.1 shard_map.145
  35.2 2.7 %collective-permute-start.5 = (f32[1,4,2,32,128]{4,3,2,1,0:T(8,128)S(1)}, f32[1,4,2,32,128]{4,3,2,1,0:T(8,128)S(1)}, u32[]{:S(2)}, u32[]{:S(2)}) collective-permute-start(f32[1,4,2,32,128]{4,3,2,1,0:T(8,128)S(1)} %get-tuple-element.145), channel_id=1, source_target_pairs={{0,8},{1,9},{2,10},{3,11},{4,12},{5,13},{6,14},{7,15},{8,0},{9,1},... | collective-permute-start | bytes 393224 | tf_op jit(solution)/shard_map/ppermute | solution.py:583
  37.8 6.1 %shard_map.146 = (f32[1536,128]{1,0:T(8,128)S(1)}, f32[6,4,128]{2,1,0:T(4,128)S(1)}) custom-call(bf16[4096,128]{1,0:T(8,128)(2,1)S(1)} %get-tuple-element.146.gate_ref, bf16[4096,128]{1,0:T(8,128)(2,1)S(1)} %get-tuple-element.147.mixed_ref, f32[16,40,128]{2,1,0:T(8,128)S(1)} %get-tuple-element.110.re_ref, f32[16,40,128]{2,1,0:T(8,128)S(1)} %get-tuple-element.111.im_ref), custom_call_target="tpu_custom_call" | custom-call | flops 6000000000 | bytes 3145728 | tf_op jit(solution)/shard_map/pallas_call | solution.py:652
  43.9 0.0 collective-permute-done.5.got_ref
  43.9 0.1 shard_map.147
  44.0 1.1 %collective-permute-start.8 = (f32[4,2,32,128]{3,2,1,0:T(8,128)S(1)}, f32[4,2,32,128]{3,2,1,0:T(8,128)S(1)}, u32[]{:S(2)}, u32[]{:S(2)}) collective-permute-start(f32[4,2,32,128]{3,2,1,0:T(8,128)S(1)} %get-tuple-element.153.into_y.into_ref), channel_id=1, source_target_pairs={{0,2},{1,3},{2,0},{3,1},{4,6},{5,7},{6,4},{7,5},{8,10},{9,11},{10,... | collective-permute-start | bytes 393224 | tf_op jit(solution)/shard_map/ppermute | solution.py:583
  45.1 0.0 collective-permute-done.3.more_ref
  45.1 0.2 shard_map.143
  45.3 0.1 shard_map.148.a_ref
  45.4 0.1 collective-permute-start.6
  45.5 1.2 %collective-permute-done.6.b_ref = f32[4,16,128]{2,1,0:T(8,128)S(1)} collective-permute-done((f32[4,16,128]{2,1,0:T(8,128)S(1)}, f32[4,16,128]{2,1,0:T(8,128)S(1)}, u32[]{:S(2)}, u32[]{:S(2)}) %collective-permute-start.6) | collective-permute-done | bytes 32800 | tf_op jit(solution)/shard_map/ppermute | solution.py:583
  46.7 1.0 %collective-permute-start.7 = (f32[4,16,128]{2,1,0:T(8,128)S(1)}, f32[4,16,128]{2,1,0:T(8,128)S(1)}, u32[]{:S(2)}, u32[]{:S(2)}) collective-permute-start(f32[4,16,128]{2,1,0:T(8,128)S(1)} %shard_map.149.a_ref), channel_id=1, source_target_pairs={{0,2},{1,3},{2,0},{3,1},{4,6},{5,7},{6,4},{7,5},{8,10},{9,11},{10,... | collective-permute-start | bytes 98312 | tf_op jit(solution)/shard_map/ppermute | solution.py:583
  47.7 1.3 %collective-permute-start.12 = (f32[8,2,32,128]{3,2,1,0:T(8,128)S(1)}, f32[8,2,32,128]{3,2,1,0:T(8,128)S(1)}, u32[]{:S(2)}, u32[]{:S(2)}) collective-permute-start(f32[8,2,32,128]{3,2,1,0:T(8,128)S(1)} %get-tuple-element.95.hi1.y_hi), channel_id=1, source_target_pairs={{1,0},{3,2},{5,4},{7,6},{9,8},{11,10},{13,12},{15,14},{17,16},{19,... | collective-permute-start | bytes 786440 | tf_op jit(solution)/shard_map/ppermute | solution.py:588
  49.0 1.7 %collective-permute-done.7.b_ref = f32[4,16,128]{2,1,0:T(8,128)S(1)} collective-permute-done((f32[4,16,128]{2,1,0:T(8,128)S(1)}, f32[4,16,128]{2,1,0:T(8,128)S(1)}, u32[]{:S(2)}, u32[]{:S(2)}) %collective-permute-start.7) | collective-permute-done | bytes 32800 | tf_op jit(solution)/shard_map/ppermute | solution.py:583
  50.6 0.0 collective-permute-done.9.later_ref
  50.7 0.0 collective-permute-done.8.other_ref
  50.7 0.1 shard_map.151.mine_ref
  50.7 0.1 collective-permute-start.11
  50.8 2.0 %shard_map.137 = bf16[4096,128]{1,0:T(8,128)(2,1)} custom-call(bf16[4096,128]{1,0:T(8,128)(2,1)S(1)} %get-tuple-element.93.a_ref, bf16[4096,128]{1,0:T(8,128)(2,1)} %b_hbm.1), custom_call_target="tpu_custom_call" | custom-call | flops 1000000000 | bytes 3145728 | tf_op jit(solution)/shard_map/pallas_call | solution.py:782
  52.9 0.9 %collective-permute-start.10 = (f32[4,16,128]{2,1,0:T(8,128)S(1)}, f32[4,16,128]{2,1,0:T(8,128)S(1)}, u32[]{:S(2)}, u32[]{:S(2)}) collective-permute-start(f32[4,16,128]{2,1,0:T(8,128)S(1)} %shard_map.150.a_ref), channel_id=1, source_target_pairs={{0,4},{1,5},{2,6},{3,7},{4,0},{5,1},{6,2},{7,3},{8,12},{9,13},{10,... | collective-permute-start | bytes 98312 | tf_op jit(solution)/shard_map/ppermute | solution.py:583
  53.8 0.0 collective-permute-done.12.later_ref
  53.8 0.0 collective-permute-done.11.other_ref
  53.8 1.9 %shard_map.152.grouped = f32[4096,128]{1,0:T(8,128)S(1)} custom-call(f32[8,2,32,128]{3,2,1,0:T(8,128)S(1)} %shard_map.151.mine_ref, f32[8,2,32,128]{3,2,1,0:T(8,128)S(1)} %collective-permute-done.11.other_ref, f32[16,2,32,128]{3,2,1,0:T(8,128)S(1)} %collective-permute-done.got_ref.near_ref, f32[8,2,32,128]{3,2,1,0:T(8,128)S(1)} %collective-permute-done.12.later_ref, ...), custom_call_target="tpu_custom_call" | custom-call | flops 4000000000 | bytes 4194304 | tf_op jit(solution)/shard_map/pallas_call | solution.py:796
  55.7 1.2 %collective-permute-done.10.b_ref = f32[4,16,128]{2,1,0:T(8,128)S(1)} collective-permute-done((f32[4,16,128]{2,1,0:T(8,128)S(1)}, f32[4,16,128]{2,1,0:T(8,128)S(1)}, u32[]{:S(2)}, u32[]{:S(2)}) %collective-permute-start.10) | collective-permute-done | bytes 32800 | tf_op jit(solution)/shard_map/ppermute | solution.py:583
  56.9 0.3 collective-permute-start.13
  57.2 0.0 copy-start
  57.2 0.0 copy-start.1
  57.2 0.0 copy-start.2
  57.2 5.1 %shard_map.154 = (bf16[4096,128]{1,0:T(8,128)(2,1)}, bf16[4096,128]{1,0:T(8,128)(2,1)}) custom-call(s32[32,128]{1,0:T(8,128)S(1)} %get-tuple-element.168.pos_ref, f32[4096,128]{1,0:T(8,128)S(1)} %shard_map.152.grouped, bf16[4096,128]{1,0:T(8,128)(2,1)S(1)} %get-tuple-element.170.k_ref, bf16[4096,128]{1,0:T(8,128)(2,1)S(1)} %get-tuple-element.171.v_ref), custom_call_target="tpu_custom_call" | custom-call | flops 4000000000 | bytes 4194304 | tf_op jit(solution)/shard_map/pallas_call | solution.py:812
  62.3 0.0 collective-permute-done.13.last_ref
  62.3 0.0 copy-done
  62.4 0.0 copy-done.1
  62.4 0.0 copy-done.2
  62.4 0.9 %shard_map.155 = (f32[16,128]{1,0:T(8,128)}, f32[16,128]{1,0:T(8,128)}, f32[2,16,128]{2,1,0:T(8,128)}) custom-call(f32[4,16,128]{2,1,0:T(8,128)S(1)} %shard_map.153.total_ref, f32[4,16,128]{2,1,0:T(8,128)S(1)} %collective-permute-done.13.last_ref, f32[16,128]{1,0:T(8,128)S(1)} %bitcast.10, f32[16,128]{1,0:T(8,128)S(1)} %bitcast.12, f32[2,16,128]{2,1,0:T(8,128)S(1)} %bitcast.8), custom_call_target="tpu_custom_call" | custom-call | tf_op jit(solution)/shard_map/pallas_call | solution.py:824
  (3 shorter events, 0.0 us)
Async XLA Ops:
  10.9 2.1 %collective-permute-start = (f32[16,2,32,128]{3,2,1,0:T(8,128)S(1)}, f32[16,2,32,128]{3,2,1,0:T(8,128)S(1)}, u32[]{:S(2)}, u32[]{:S(2)}) collective-permute-start(f32[16,2,32,128]{3,2,1,0:T(8,128)S(1)} %get-tuple-element.98), channel_id=1, source_target_pairs={{0,1},{1,0},{2,3},{3,2},{4,5},{5,4},{6,7},{7,6},{8,9},{9,8},{10,11... | collective-permute-start | bytes 1572872 | tf_op jit(solution)/shard_map/ppermute | solution.py:583
  15.2 10.3 %collective-permute-start.2 = (f32[16,2,32,128]{3,2,1,0:T(8,128)S(1)}, f32[16,2,32,128]{3,2,1,0:T(8,128)S(1)}, u32[]{:S(2)}, u32[]{:S(2)}) collective-permute-start(f32[16,2,32,128]{3,2,1,0:T(8,128)S(1)} %get-tuple-element.117), channel_id=1, source_target_pairs={{0,1},{1,0},{2,3},{3,2},{4,5},{5,4},{6,7},{7,6},{8,9},{9,8},{10,11... | collective-permute-start | bytes 1572872 | tf_op jit(solution)/shard_map/ppermute | solution.py:583
  15.7 9.8 %collective-permute-start.1 = (f32[8,2,32,128]{3,2,1,0:T(8,128)S(1)}, f32[8,2,32,128]{3,2,1,0:T(8,128)S(1)}, u32[]{:S(2)}, u32[]{:S(2)}) collective-permute-start(f32[8,2,32,128]{3,2,1,0:T(8,128)S(1)} %get-tuple-element.107), channel_id=1, source_target_pairs={{0,2},{1,3},{2,0},{3,1},{4,6},{5,7},{6,4},{7,5},{8,10},{9,11},{10,... | collective-permute-start | bytes 786440 | tf_op jit(solution)/shard_map/ppermute | solution.py:583
  18.3 32.3 %collective-permute-start.9 = (f32[4,2,32,128]{3,2,1,0:T(8,128)S(1)}, f32[4,2,32,128]{3,2,1,0:T(8,128)S(1)}, u32[]{:S(2)}, u32[]{:S(2)}) collective-permute-start(f32[4,2,32,128]{3,2,1,0:T(8,128)S(1)} %get-tuple-element.101.hi1.y_hi), channel_id=1, source_target_pairs={{2,0},{3,1},{6,4},{7,5},{10,8},{11,9},{14,12},{15,13},{18,16},{19,... | collective-permute-start | bytes 393224 | tf_op jit(solution)/shard_map/ppermute | solution.py:588
  25.9 19.2 %collective-permute-start.3 = (f32[8,2,32,128]{3,2,1,0:T(8,128)S(1)}, f32[8,2,32,128]{3,2,1,0:T(8,128)S(1)}, u32[]{:S(2)}, u32[]{:S(2)}) collective-permute-start(f32[8,2,32,128]{3,2,1,0:T(8,128)S(1)} %get-tuple-element.135), channel_id=1, source_target_pairs={{0,2},{1,3},{2,0},{3,1},{4,6},{5,7},{6,4},{7,5},{8,10},{9,11},{10,... | collective-permute-start | bytes 786440 | tf_op jit(solution)/shard_map/ppermute | solution.py:583
  27.4 7.7 %collective-permute-start.4 = (f32[2,4,2,32,128]{4,3,2,1,0:T(8,128)S(1)}, f32[2,4,2,32,128]{4,3,2,1,0:T(8,128)S(1)}, u32[]{:S(2)}, u32[]{:S(2)}) collective-permute-start(f32[2,4,2,32,128]{4,3,2,1,0:T(8,128)S(1)} %shard_map.141.total_ref.yx_ref), channel_id=1, source_target_pairs={{0,4},{1,5},{2,6},{3,7},{4,0},{5,1},{6,2},{7,3},{8,12},{9,13},{10,... | collective-permute-start | bytes 786440 | tf_op jit(solution)/shard_map/ppermute | solution.py:583
  35.2 8.8 %collective-permute-start.5 = (f32[1,4,2,32,128]{4,3,2,1,0:T(8,128)S(1)}, f32[1,4,2,32,128]{4,3,2,1,0:T(8,128)S(1)}, u32[]{:S(2)}, u32[]{:S(2)}) collective-permute-start(f32[1,4,2,32,128]{4,3,2,1,0:T(8,128)S(1)} %get-tuple-element.145), channel_id=1, source_target_pairs={{0,8},{1,9},{2,10},{3,11},{4,12},{5,13},{6,14},{7,15},{8,0},{9,1},... | collective-permute-start | bytes 393224 | tf_op jit(solution)/shard_map/ppermute | solution.py:583
  44.0 6.7 %collective-permute-start.8 = (f32[4,2,32,128]{3,2,1,0:T(8,128)S(1)}, f32[4,2,32,128]{3,2,1,0:T(8,128)S(1)}, u32[]{:S(2)}, u32[]{:S(2)}) collective-permute-start(f32[4,2,32,128]{3,2,1,0:T(8,128)S(1)} %get-tuple-element.153.into_y.into_ref), channel_id=1, source_target_pairs={{0,2},{1,3},{2,0},{3,1},{4,6},{5,7},{6,4},{7,5},{8,10},{9,11},{10,... | collective-permute-start | bytes 393224 | tf_op jit(solution)/shard_map/ppermute | solution.py:583
  45.4 1.3 %collective-permute-start.6 = (f32[4,16,128]{2,1,0:T(8,128)S(1)}, f32[4,16,128]{2,1,0:T(8,128)S(1)}, u32[]{:S(2)}, u32[]{:S(2)}) collective-permute-start(f32[4,16,128]{2,1,0:T(8,128)S(1)} %shard_map.148.a_ref), channel_id=1, source_target_pairs={{0,1},{1,0},{2,3},{3,2},{4,5},{5,4},{6,7},{7,6},{8,9},{9,8},{10,11... | collective-permute-start | bytes 98312 | tf_op jit(solution)/shard_map/ppermute | solution.py:583
  46.7 3.9 %collective-permute-start.7 = (f32[4,16,128]{2,1,0:T(8,128)S(1)}, f32[4,16,128]{2,1,0:T(8,128)S(1)}, u32[]{:S(2)}, u32[]{:S(2)}) collective-permute-start(f32[4,16,128]{2,1,0:T(8,128)S(1)} %shard_map.149.a_ref), channel_id=1, source_target_pairs={{0,2},{1,3},{2,0},{3,1},{4,6},{5,7},{6,4},{7,5},{8,10},{9,11},{10,... | collective-permute-start | bytes 98312 | tf_op jit(solution)/shard_map/ppermute | solution.py:583
  47.7 6.1 %collective-permute-start.12 = (f32[8,2,32,128]{3,2,1,0:T(8,128)S(1)}, f32[8,2,32,128]{3,2,1,0:T(8,128)S(1)}, u32[]{:S(2)}, u32[]{:S(2)}) collective-permute-start(f32[8,2,32,128]{3,2,1,0:T(8,128)S(1)} %get-tuple-element.95.hi1.y_hi), channel_id=1, source_target_pairs={{1,0},{3,2},{5,4},{7,6},{9,8},{11,10},{13,12},{15,14},{17,16},{19,... | collective-permute-start | bytes 786440 | tf_op jit(solution)/shard_map/ppermute | solution.py:588
  50.7 3.0 %collective-permute-start.11 = (f32[8,2,32,128]{3,2,1,0:T(8,128)S(1)}, f32[8,2,32,128]{3,2,1,0:T(8,128)S(1)}, u32[]{:S(2)}, u32[]{:S(2)}) collective-permute-start(f32[8,2,32,128]{3,2,1,0:T(8,128)S(1)} %shard_map.151.mine_ref), channel_id=1, source_target_pairs={{0,1},{1,0},{2,3},{3,2},{4,5},{5,4},{6,7},{7,6},{8,9},{9,8},{10,11... | collective-permute-start | bytes 786440 | tf_op jit(solution)/shard_map/ppermute | solution.py:583
  52.9 4.0 %collective-permute-start.10 = (f32[4,16,128]{2,1,0:T(8,128)S(1)}, f32[4,16,128]{2,1,0:T(8,128)S(1)}, u32[]{:S(2)}, u32[]{:S(2)}) collective-permute-start(f32[4,16,128]{2,1,0:T(8,128)S(1)} %shard_map.150.a_ref), channel_id=1, source_target_pairs={{0,4},{1,5},{2,6},{3,7},{4,0},{5,1},{6,2},{7,3},{8,12},{9,13},{10,... | collective-permute-start | bytes 98312 | tf_op jit(solution)/shard_map/ppermute | solution.py:583
  56.9 5.5 %collective-permute-start.13 = (f32[4,16,128]{2,1,0:T(8,128)S(1)}, f32[4,16,128]{2,1,0:T(8,128)S(1)}, u32[]{:S(2)}, u32[]{:S(2)}) collective-permute-start(f32[4,16,128]{2,1,0:T(8,128)S(1)} %shard_map.153.total_ref), channel_id=1, source_target_pairs={{0,8},{1,9},{2,10},{3,11},{4,12},{5,13},{6,14},{7,15},{8,0},{9,1},... | collective-permute-start | bytes 98312 | tf_op jit(solution)/shard_map/ppermute | solution.py:583
  57.2 5.1 %copy-start = (f32[2,128,16]{1,2,0:T(8,128)S(1)}, f32[2,128,16]{1,2,0:T(8,128)}, u32[]{:S(2)}) copy-start(f32[2,128,16]{1,2,0:T(8,128)} %param.17) | copy-start | bytes 49156
  57.2 5.2 %copy-start.1 = (f32[128,16]{0,1:T(8,128)S(1)}, f32[128,16]{0,1:T(8,128)}, u32[]{:S(2)}) copy-start(f32[128,16]{0,1:T(8,128)} %param.15) | copy-start | bytes 24580
  57.2 5.2 %copy-start.2 = (f32[128,16]{0,1:T(8,128)S(1)}, f32[128,16]{0,1:T(8,128)}, u32[]{:S(2)}) copy-start(f32[128,16]{0,1:T(8,128)} %param.16) | copy-start | bytes 24580

commit v3 on v2

--- a/solution.py
+++ b/solution.py
@@ -10,6 +10,8 @@
 F32 = jnp.float32
 BF16 = jnp.bfloat16
 LANES = 128
+COST = 10**6
+UNROLL = {4: 4, 5: 5, 6: 3}
 
 
 def complex_product(a_real, a_imag, b_real, b_imag):
@@ -106,8 +108,13 @@
         for part in (rho, angle, res_ref[0] * scale, res_ref[1] * scale)
     )
     re_ref[:, 32, :], im_ref[:, 32, :] = rr, ri
-    for step in [0, *range(1, 9), *range(16, 128, 8)]:
-        re, im = power_of(rho, angle, float(step))
+    known = {0: (jnp.ones_like(rho), jnp.zeros_like(rho))}
+    for step in [1, 2, 4, 8, 16, 32, 64]:
+        known[step] = power_of(rho, angle, float(step))
+    for step in [*range(9), *range(16, 128, 8)]:
+        top = 1 << max(step.bit_length() - 1, 0)
+        if step not in known:
+            known[step] = complex_product(*known[top], *known[step - top])
         rows = []
         if step < 8:
             rows.append(step)
@@ -116,7 +123,7 @@
         if step % 8 == 0:
             rows.append(16 + step // 8)
         for row in rows:
-            re_ref[:, row, :], im_ref[:, row, :] = re, im
+            re_ref[:, row, :], im_ref[:, row, :] = known[step]
     for i, blocks in enumerate(factor_blocks(me, count)):
         steps = jnp.asarray(blocks, jnp.int32).astype(F32) * float(LANES)
         factor_ref[i, 0], factor_ref[i, 1] = power_of(rho, angle, steps)
@@ -239,7 +246,7 @@
 
 
 def rates_kernel(
-    members, modes, gate_ref, mixed_ref, re_ref, im_ref, v_lo, v_hi, w_lo, w_hi, ahead_ref
+    members, modes, gate_ref, mixed_ref, re_ref, im_ref, more_y, v_lo, v_hi, w_lo, w_hi, ahead_ref
 ):
     size = (LANES // modes) * members
     half = v_lo.shape[0]
@@ -263,6 +270,7 @@
     def _(i):
         ahead_ref[i] = jnp.where(upper == 1, v_lo[i], v_hi[i])
         ahead_ref[half + i] = jnp.where(upper == 1, w_lo[i], w_hi[i])
+        ahead_ref[2 * half + i] = more_y[i]
 
 
 def pair(ref, i):
@@ -316,8 +324,9 @@
 
 
 def rate_merge_kernel(
-    level, y_lo, y_hi, x_lo, x_hi, got_ref, v_lo, v_hi, w_lo, w_hi, more_ref, factor_ref, *outs
+    level, y_lo, y_hi, x_lo, x_hi, got_ref, v_lo, v_hi, w_lo, w_hi, more_ref, factor_ref, *refs
 ):
+    next_y, outs = (refs[0], refs[1:]) if level == 0 else (None, refs)
     upper, following, base = place_of(level)
     is_up = upper == 1
     span = float(LANES << level)
@@ -351,6 +360,7 @@
         for i in range(n // 2):
             ahead[i] = jnp.where(following == 1, outs[0][i], outs[1][i])
             ahead[n // 2 + i] = jnp.where(following == 1, outs[2][i], outs[3][i])
+            ahead[n + i] = next_y[i]
 
 
 def total_kernel(
@@ -413,7 +423,7 @@
             outs[3][0, i, 0], outs[3][0, i, 1] = pick((me // (2 * bit)) % 2 == 1, t_y, t_x)
 
 
-def down_kernel(into_ref, other_ref, got_ref, later_ref, factor_ref, out_ref):
+def down_kernel(into_ref, other_ref, got_ref, more_ref, factor_ref, out_ref):
     low, high, base = place_of(0)
     is_up = high == 1
     n = into_ref.shape[0]
@@ -421,7 +431,7 @@
         k = i % n
         mine, other = pair(into_ref, k), pair(other_ref, k)
         into = pick(is_up, other, mine) if i < n else pick(is_up, mine, other)
-        own = pair(got_ref, k) if i < n else pair(later_ref, k)
+        own = pair(got_ref, k) if i < n else pair(more_ref, 2 * n + k)
         p = tuple(factor_ref[1, c, pl.ds(base + i, 1), :] for c in range(2))
         out_ref[i, 0], out_ref[i, 1] = pick(is_up, into, plus(own, complex_product(*p, *into)))
 
@@ -431,46 +441,62 @@
 
 
 def conv_kernel(
-    members, modes, gate_ref, mixed_ref, re_ref, im_ref,
-    conv_ref, sums_ref, lag,
+    members, modes, first, unroll, gate_ref, mixed_ref, re_ref, im_ref, conv_ref, sums_ref
 ):
     per = LANES // modes
-    head_re, head_im = powers(re_ref, im_ref, 0, False)
+    size = per * members
     step = lax.broadcasted_iota(jnp.int32, (LANES, LANES), 0).astype(F32)
-    gate, mixed = gate_ref[...], mixed_ref[...]
-    der = stacked(step * head_re, step * head_im)
-    head = stacked(head_re, head_im)
-    head_hi, head_lo = head[:LANES], head[LANES:]
-    own8 = own_filter(per, 2 * LANES, 1, modes)
-    res = jnp.concatenate([re_ref[0, 32:33, :], -im_ref[0, 32:33, :]], axis=1)
-    res_hi, res_lo = split(jnp.where(own8, res, 0.0))
-    filt = dot(res_hi, head_hi, NT) + dot(res_lo, head_hi, NT) + dot(res_hi, head_lo, NT)
+    own = own_filter(per, 2 * LANES, 1, modes)
     row = lax.broadcasted_iota(jnp.int32, (LANES, LANES), 0)
     col = lax.broadcasted_iota(jnp.int32, (LANES, LANES), 1)
-    causal = col >= row
     mirror = (row + col == LANES - 1).astype(F32).astype(BF16)
-    mirrored = dot(mixed, mirror, NN).astype(BF16)
-    for f in range(per):
-        at = slice(f * members, (f + 1) * members)
-        wide = jnp.broadcast_to(filt[f : f + 1, :], (LANES, LANES))
-        shifted = pltpu.roll(wide, 0, 1, stride=1, stride_axis=0)
-        hi, lo = split(jnp.where(causal, shifted, 0.0))
-        gate_f = gate[at]
-        conv_ref[at, :] = dot(gate_f, hi, NT) + dot(gate_f, lo, NT)
-        corr = jnp.where(row + col >= LANES - 1, dot(mirrored[at], gate_f, TN), 0.0)
-        aligned = pltpu.roll(corr, 1, 1, stride=1, stride_axis=0)
-        lag[f : f + 1, :] = jnp.sum(aligned, axis=0, keepdims=True)
-    lag_hi, lag_lo = split(lag[...])
-    for which, table in enumerate((head, der)):
-        hi, lo = table[:LANES], table[LANES:]
-        out = dot(lag_hi, hi, NN) + dot(lag_lo, hi, NN) + dot(lag_hi, lo, NN)
-        out = jnp.sum(jnp.where(own8, out, 0.0), axis=0, keepdims=True)
-        sums_ref[0, 2 * which : 2 * which + 1, :] = out[:, :LANES]
-        sums_ref[0, 2 * which + 1 : 2 * which + 2, :] = out[:, LANES:]
+    causal, mirrored_causal = row >= col, row + col >= LANES - 1
+
+    @pl.loop(0, conv_ref.shape[0] // size, unroll=unroll)
+    def _(i):
+        g = first + i
+        at = pl.ds(pl.multiple_of(g * size, size), size)
+        to = pl.multiple_of(i * size, size)
+        gate, mixed = gate_ref[at, :], mixed_ref[at, :]
+        head_re, head_im = powers(re_ref, im_ref, g, False)
+        head, der = stacked(head_re, head_im), stacked(step * head_re, step * head_im)
+        res = jnp.concatenate([re_ref[g, 32:33, :], -im_ref[g, 32:33, :]], axis=1)
+        filt = dot(jnp.concatenate(split(jnp.where(own, res, 0.0)), axis=0), head, NT)
+        filt = filt[:per, :LANES] + filt[per:, :LANES] + filt[:per, LANES:]
+        filt = dot(jnp.concatenate(split(filt), axis=0), mirror, NN)
+        filt = filt[:per] + filt[per:]
+        turned = dot(mirror, mixed, NT).astype(BF16)
+        lags = []
+        for f in range(per):
+            mine = slice(f * members, (f + 1) * members)
+            wide = jnp.broadcast_to(filt[f : f + 1, :], (LANES, LANES))
+            wide = pltpu.roll(wide, 1, 1, stride=1, stride_axis=0)
+            hi, lo = split(jnp.where(causal, wide, 0.0))
+            twice = jnp.concatenate([gate[mine], gate[mine]], axis=1)
+            conv_ref[pl.ds(to + f * members, members), :] = dot(
+                twice, jnp.concatenate([hi, lo], axis=0), NN
+            )
+            corr = jnp.where(mirrored_causal, dot(turned[:, mine], gate[mine], NN), 0.0)
+            corr = pltpu.roll(corr, 1, 1, stride=1, stride_axis=0)
+            lags.append(jnp.sum(corr, axis=0, keepdims=True))
+        lag_hi, lag_lo = split(jnp.concatenate(lags, axis=0))
+        lags = jnp.concatenate(
+            [
+                jnp.concatenate([lag_hi, lag_hi], axis=1),
+                jnp.concatenate([lag_lo, jnp.zeros_like(lag_lo)], axis=1),
+            ],
+            axis=0,
+        )
+        for which, table in enumerate((head, der)):
+            out = dot(lags, table, NN)
+            out = jnp.where(own, out[:per] + out[per:], 0.0)
+            out = jnp.sum(out, axis=0, keepdims=True)
+            sums_ref[i, 2 * which : 2 * which + 1, :] = out[:, :LANES]
+            sums_ref[i, 2 * which + 1 : 2 * which + 2, :] = out[:, LANES:]
 
 
 def cross_kernel(
-    members, modes, calls, mine_ref, other_ref, near_ref, later_ref, factor_ref, re_ref, im_ref,
+    members, modes, calls, mine_ref, other_ref, near_ref, more_ref, factor_ref, re_ref, im_ref,
     *refs,
 ):
     convs, out_ref = refs[:calls], refs[calls]
@@ -490,13 +516,17 @@
             k = g % half
             mine, other = pair(mine_ref, k), pair(other_ref, k)
             into = pick(is_up, other, mine) if g < half else pick(is_up, mine, other)
-            own = pair(near_ref if g < half else later_ref, k)
+            own = pair(near_ref, k) if g < half else pair(more_ref, 2 * half + k)
             p = (factor_ref[0, 0, g : g + 1, :], factor_ref[0, 1, g : g + 1, :])
             yin = pick(is_up, into, plus(own, complex_product(*p, *into)))
             yin = jnp.concatenate(yin, axis=1)
             wide = jnp.concatenate([jnp.where(lane == f, yin, 0.0) for f in range(per)], axis=0)
-            hi, lo = split(wide)
-            total = dot(hi, coef_hi, NT) + dot(lo, coef_hi, NT) + dot(hi, coef_lo, NT)
+            both = dot(
+                jnp.concatenate(split(wide), axis=0),
+                jnp.concatenate([coef_hi, coef_lo], axis=0),
+                NT,
+            )
+            total = both[:size, :LANES] + both[size:, :LANES] + both[:size, LANES:]
             out_ref[g * size : (g + 1) * size, :] = conv_ref[i * size : (i + 1) * size, :] + total
         first += conv_ref.shape[0] // size
 
@@ -581,11 +611,6 @@
 def swap(value, bit):
     count = lax.axis_size("seq")
     return lax.ppermute(value, "seq", [(i, i ^ bit) for i in range(count)])
-
-
-def lower_only(value, bit):
-    count = lax.axis_size("seq")
-    return lax.ppermute(value, "seq", [(i, i ^ bit) for i in range(count) if i & bit])
 
 
 def together(*values):
@@ -647,21 +672,14 @@
     size = per * members
 
     def conv_call(first, number):
-        rows = pl.BlockSpec((size, positions), lambda g: (g + first, 0))
-        table = pl.BlockSpec((1, 40, LANES), lambda g: (g + first, 0, 0))
         return pl.pallas_call(
-            functools.partial(conv_kernel, members, modes),
-            grid=(number,),
+            functools.partial(conv_kernel, members, modes, first, UNROLL.get(number, 1)),
             out_shape=(shape((number * size, positions), F32), shape((number, 4, LANES), F32)),
-            in_specs=[rows, rows, table, table],
-            out_specs=(
-                pl.BlockSpec((size, positions), lambda g: (g, 0)),
-                pl.BlockSpec((1, 4, LANES), lambda g: (g, 0, 0)),
-            ),
-            scratch_shapes=[pltpu.VMEM((per, LANES), F32)],
+            in_specs=vmem(4),
+            out_specs=tuple(vmem(2)),
             compiler_params=params(8),
             cost_estimate=pl.CostEstimate(
-                flops=number * 10**9, bytes_accessed=number << 19, transcendentals=0
+                flops=number * COST, bytes_accessed=number << 10, transcendentals=0
             ),
         )(gate, mixed, tab_re, tab_im)
 
@@ -683,35 +701,33 @@
         n = half >> level
         sums = shape((4, n, LANES), F32)
         if level == 0:
-            outs = (*[state(n // 2)] * 4, state(n), sums)
+            outs = (*[state(n // 2)] * 4, state(n + n // 2), sums)
         else:
             outs = (state(2, n), sums)
         return pl.pallas_call(
             functools.partial(rate_merge_kernel, level),
             out_shape=outs,
-            in_specs=vmem(11),
+            in_specs=vmem(len(args)),
             out_specs=tuple(vmem(len(outs))),
             compiler_params=params(8),
-        )(*args, factors)
+        )(*args)
 
     got0 = swap(ahead, 1)
     ty_lo, ty_hi, tx_lo, tx_hi, ahead1 = merge(0, y_lo, y_hi, x_lo, x_hi, got0)
     ahead1, gate, mixed = together(ahead1, gate, mixed)
     got1 = swap(ahead1, 2)
-    later0 = lower_only(y_hi, 1)
     vw = pl.pallas_call(
         functools.partial(rates_kernel, members, modes),
-        out_shape=(*[state(half)] * 4, state(groups)),
-        in_specs=vmem(4),
+        out_shape=(*[state(half)] * 4, state(groups + half)),
+        in_specs=vmem(5),
         out_specs=tuple(vmem(5)),
         compiler_params=params(8),
-        cost_estimate=pl.CostEstimate(flops=3 * 10**9, bytes_accessed=4 << 20, transcendentals=0),
-    )(gate, mixed, tab_re, tab_im)
-    vw, gate, mixed = together(vw, gate, mixed)
+        cost_estimate=pl.CostEstimate(flops=2 * COST, bytes_accessed=1 << 10, transcendentals=0),
+    )(gate, mixed, tab_re, tab_im, y_hi)
+    parts = [5, 5, groups - 10]
+    made = [conv_call(0, parts[0])]
+    got1, vw, made[0] = together(got1, vw, made[0])
     more0 = swap(vw[4], 1)
-    parts = [4, 6, groups - 10]
-    made = [conv_call(0, parts[0])]
-    got1, more0, made[0] = together(got1, more0, made[0])
     (yx,) = merge(1, ty_lo, ty_hi, tx_lo, tx_hi, got1)
 
     base = 4
@@ -722,10 +738,11 @@
         sent, gate, mixed = together(sent, gate, mixed)
         got = swap(sent, bit)
         if bit == base:
-            rate0 = rate_merge(0, y_lo, y_hi, x_lo, x_hi, got0, *vw[:4], more0)
+            rate0 = rate_merge(
+                0, y_lo, y_hi, x_lo, x_hi, got0, *vw[:4], more0, factors, ty_hi
+            )
             more1, gate, mixed = together(rate0[4], gate, mixed)
             more1 = swap(more1, 2)
-            later1 = lower_only(ty_hi, 2)
         if bit == base or last:
             first = sum(parts[: len(made)])
             conv = conv_call(first, groups - first if last else parts[len(made)])
@@ -751,7 +768,9 @@
     into_y, into_x = into
     convs, lags = zip(*made)
     calls = len(convs)
-    rate1 = rate_merge(1, ty_lo, ty_hi, tx_lo, tx_hi, got1, *rate0[:4], more1)
+    rate1 = rate_merge(
+        1, ty_lo, ty_hi, tx_lo, tx_hi, got1, *rate0[:4], more1, factors
+    )
     total = pl.pallas_call(
         functools.partial(total_kernel, calls),
         out_shape=shape((4, groups, LANES), F32),
@@ -769,16 +788,11 @@
             compiler_params=params(2),
         )(a, b)
 
+    into_y, total = together(into_y, total)
     other = swap(into_y, 2)
     total = add(total, swap(total, 1))
+    total, own_out = together(total, own_out)
     got = swap(total, 2)
-    chip = pl.pallas_call(
-        down_kernel,
-        out_shape=state(half),
-        in_specs=vmem(5),
-        out_specs=vmem(1)[0],
-        compiler_params=params(4),
-    )(into_y, other, got1, later1, factors)
     grad_query = pl.pallas_call(
         product_kernel,
         out_shape=shape(wide, BF16),
@@ -786,13 +800,21 @@
         out_specs=hbm,
         scratch_shapes=[pltpu.VMEM(wide, BF16)] * 2 + [pltpu.SemaphoreType.DMA((8,))],
         compiler_params=params(8),
-        cost_estimate=pl.CostEstimate(flops=10**9, bytes_accessed=3 << 20, transcendentals=0),
+        cost_estimate=pl.CostEstimate(flops=COST, bytes_accessed=1 << 10, transcendentals=0),
     )(own_out, pinned(conv_out))
+    other, grad_query = together(other, grad_query)
+    chip = pl.pallas_call(
+        down_kernel,
+        out_shape=state(half),
+        in_specs=vmem(5),
+        out_specs=vmem(1)[0],
+        compiler_params=params(4),
+    )(into_y, other, got1, more1, factors)
     total = add(total, got)
     total, chip = together(total, chip)
     got = swap(total, 4)
     chip_other = swap(chip, 1)
-    cost = pl.CostEstimate(flops=4 * 10**9, bytes_accessed=4 << 20, transcendentals=0)
+    cost = pl.CostEstimate(flops=COST, bytes_accessed=1 << 10, transcendentals=0)
     grouped = pl.pallas_call(
         functools.partial(cross_kernel, members, modes, calls),
         out_shape=shape(wide, F32),
@@ -800,7 +822,7 @@
         out_specs=vmem(1)[0],
         compiler_params=params(12),
         cost_estimate=cost,
-    )(chip, chip_other, got0, later0, factors, tab_re, tab_im, *convs)
+    )(chip, chip_other, got0, more0, factors, tab_re, tab_im, *convs)
     got, grouped = together(got, grouped)
     total = add(total, got)
     bit = 8

time: 63.6 us -> 60 us (0.943)
  Pallas kernels: 39.7 us -> 36 us
    pallas_call x3, Pallas kernels: 16.3 us -> 13.1 us  [conv_call(): pl.pallas_call(functools.partial(conv_kernel, members, modes, first, UNRO...]
    ppermute x2 -> x0, starting transfers between devices: 2.56 us -> none  [lower_only(): lax.ppermute(value, 'seq', [(i, i ^ bit) for i in range(count) if i & bit])]
    ppermute x12, starting transfers between devices: 12.8 us -> 15 us  [swap(): return lax.ppermute(value, 'seq', [(i, i ^ bit) for i in range(count)])]
  transfers between devices with their start and end apart: 14 -> 12, of which waited for: 5 -> 9; matrix products, arithmetic and copies ran while one was open for 0% -> 0% of each run, Pallas kernels for 41% -> 41%
where the time goes in v3:
time: 60 us; the launch traced here: 59.8 us
  Pallas kernels  36 us (60%)
  starting transfers between devices  15 us (25%)
  waiting for transfers between devices  7.94 us (13%)
  between operations  0.79 us (1%)
    ppermute x12, starting transfers between devices, swap(): return lax.ppermute(value, 'seq', [(i, i ^ bit) for i in range(count)])  15 us
    pallas_call x3, Pallas kernels, conv_call(): pl.pallas_call(functools.partial(conv_kernel, members, modes, first, UNRO...  13.1 us
    pallas_call x1, Pallas kernels, body(): pl.pallas_call(functools.partial(states_kernel, members, modes, count), o...  9.81 us
    ppermute x12, waiting for transfers between devices, swap(): return lax.ppermute(value, 'seq', [(i, i ^ bit) for i in range(count)])  7.94 us
    pallas_call x1, Pallas kernels, body(): pl.pallas_call(finish_kernel, out_shape=(shape(wide, BF16), shape(wide, B...  5.12 us
    pallas_call x1, Pallas kernels, body(): pl.pallas_call(functools.partial(rates_kernel, members, modes), out_shape...  2.09 us
    pallas_call x1, Pallas kernels, body(): pl.pallas_call(product_kernel, out_shape=shape(wide, BF16), in_specs=vmem...  2.04 us
    pallas_call x1, Pallas kernels, body(): pl.pallas_call(functools.partial(cross_kernel, members, modes, calls), ou...  1.9 us
  transfers between devices with their start and end apart: 12, of which 9 were waited for; matrix products, arithmetic and copies ran while one was open for 0% of the time, Pallas kernels for 41%

profile of v3, /device:TPU:0, one launch (start us, length us, event | category | flops | bytes accessed | tf_op | source)
XLA Modules:
  0.0 59.8 jit_solution(8266123645680123675)
XLA Ops:
  0.6 9.8 %shard_map.136 = (bf16[4096,128]{1,0:T(8,128)(2,1)S(1)}, bf16[4096,128]{1,0:T(8,128)(2,1)S(1)}, f32[8,2,32,128]{3,2,1,0:T(8,128)S(1)}, f32[8,2,32,128]{3,2,1,0:T...) custom-call(s32[32,128]{1,0:T(8,128)} %bitcast.13, ...), custom_call_target="tpu_custom_call" | custom-call | tf_op jit(solution)/shard_map/pallas_call | solution.py:645
  10.5 0.5 collective-permute-start
  11.0 1.5 %collective-permute-done.got_ref.near_ref = f32[16,2,32,128]{3,2,1,0:T(8,128)S(1)} collective-permute-done((f32[16,2,32,128]{3,2,1,0:T(8,128)S(1)}, f32[16,2,32,128]{3,2,1,0:T(8,128)S(1)}, u32[]{:S(2)}, u32[]{:S(2)}) %collective-permute-start) | collective-permute-done | bytes 524320 | tf_op jit(solution)/shard_map/ppermute | solution.py:613
  12.5 0.1 shard_map.137
  12.7 2.9 %collective-permute-start.1 = (f32[8,2,32,128]{3,2,1,0:T(8,128)S(1)}, f32[8,2,32,128]{3,2,1,0:T(8,128)S(1)}, u32[]{:S(2)}, u32[]{:S(2)}) collective-permute-start(f32[8,2,32,128]{3,2,1,0:T(8,128)S(1)} %get-tuple-element.109), channel_id=1, source_target_pairs={{0,2},{1,3},{2,0},{3,1},{4,6},{5,7},{6,4},{7,5},{8,10},{9,11},{10,... | collective-permute-start | bytes 786440 | tf_op jit(solution)/shard_map/ppermute | solution.py:613
  15.6 2.1 %shard_map.138 = (f32[8,2,32,128]{3,2,1,0:T(8,128)S(1)}, f32[8,2,32,128]{3,2,1,0:T(8,128)S(1)}, f32[8,2,32,128]{3,2,1,0:T(8,128)S(1)}, f32[8,2,32,128]{3,2,1,0:T(8,128)S(1)}, f32[24,2,32,128]{3,2,1,0:T(8,128)S(1)}) custom-call(bf16[4096,128]{1,0:T(8,128)(2,1)S(1)} %get-tuple-element.139.gate_ref, bf16[4096,128]{1,0:T(8,128)(2,1)S(1)} %get-tuple-element.140.mixed_ref, ...), custom_call_target="tpu_custom_call" | custom-call | flops 2000000 | bytes 1024 | tf_op jit(solution)/shard_map/pallas_call | solution.py:719
  17.7 4.0 %shard_map.139 = (f32[1280,128]{1,0:T(8,128)S(1)}, f32[5,4,128]{2,1,0:T(4,128)S(1)}) custom-call(bf16[4096,128]{1,0:T(8,128)(2,1)S(1)} %get-tuple-element.139.gate_ref, bf16[4096,128]{1,0:T(8,128)(2,1)S(1)} %get-tuple-element.140.mixed_ref, f32[16,40,128]{2,1,0:T(8,128)S(1)} %get-tuple-element.112.re_ref, f32[16,40,128]{2,1,0:T(8,128)S(1)} %get-tuple-element.113.im_ref), custom_call_target="tpu_custom_call" | custom-call | flops 5000000 | bytes 5120 | tf_op jit(solution)/shard_map/pallas_call | solution.py:675
  21.7 0.5 collective-permute-done.1.got_ref
  22.2 0.0 collective-permute-start.3
  22.2 0.1 shard_map.140.total_ref.yx_ref
  22.3 1.9 %collective-permute-start.2 = (f32[2,4,2,32,128]{4,3,2,1,0:T(8,128)S(1)}, f32[2,4,2,32,128]{4,3,2,1,0:T(8,128)S(1)}, u32[]{:S(2)}, u32[]{:S(2)}) collective-permute-start(f32[2,4,2,32,128]{4,3,2,1,0:T(8,128)S(1)} %shard_map.140.total_ref.yx_ref), channel_id=1, source_target_pairs={{0,4},{1,5},{2,6},{3,7},{4,0},{5,1},{6,2},{7,3},{8,12},{9,13},{10,... | collective-permute-start | bytes 786440 | tf_op jit(solution)/shard_map/ppermute | solution.py:613
  24.2 0.3 collective-permute-done.3.more_ref
  24.5 0.3 shard_map.141
  24.9 1.8 %collective-permute-start.5 = (f32[12,2,32,128]{3,2,1,0:T(8,128)S(1)}, f32[12,2,32,128]{3,2,1,0:T(8,128)S(1)}, u32[]{:S(2)}, u32[]{:S(2)}) collective-permute-start(f32[12,2,32,128]{3,2,1,0:T(8,128)S(1)} %get-tuple-element.151), channel_id=1, source_target_pairs={{0,2},{1,3},{2,0},{3,1},{4,6},{5,7},{6,4},{7,5},{8,10},{9,11},{10,... | collective-permute-start | bytes 1179656 | tf_op jit(solution)/shard_map/ppermute | solution.py:613
  26.7 4.0 %shard_map.142 = (f32[1280,128]{1,0:T(8,128)S(1)}, f32[5,4,128]{2,1,0:T(4,128)S(1)}) custom-call(bf16[4096,128]{1,0:T(8,128)(2,1)S(1)} %get-tuple-element.139.gate_ref, bf16[4096,128]{1,0:T(8,128)(2,1)S(1)} %get-tuple-element.140.mixed_ref, f32[16,40,128]{2,1,0:T(8,128)S(1)} %get-tuple-element.112.re_ref, f32[16,40,128]{2,1,0:T(8,128)S(1)} %get-tuple-element.113.im_ref), custom_call_target="tpu_custom_call" | custom-call | flops 5000000 | bytes 5120 | tf_op jit(solution)/shard_map/pallas_call | solution.py:675
  30.6 0.5 collective-permute-done.2.got_ref
  31.1 0.1 shard_map.143
  31.2 2.8 %collective-permute-start.4 = (f32[1,4,2,32,128]{4,3,2,1,0:T(8,128)S(1)}, f32[1,4,2,32,128]{4,3,2,1,0:T(8,128)S(1)}, u32[]{:S(2)}, u32[]{:S(2)}) collective-permute-start(f32[1,4,2,32,128]{4,3,2,1,0:T(8,128)S(1)} %get-tuple-element.138), channel_id=1, source_target_pairs={{0,8},{1,9},{2,10},{3,11},{4,12},{5,13},{6,14},{7,15},{8,0},{9,1},... | collective-permute-start | bytes 393224 | tf_op jit(solution)/shard_map/ppermute | solution.py:613
  34.0 5.1 %shard_map.144 = (f32[1536,128]{1,0:T(8,128)S(1)}, f32[6,4,128]{2,1,0:T(4,128)S(1)}) custom-call(bf16[4096,128]{1,0:T(8,128)(2,1)S(1)} %get-tuple-element.139.gate_ref, bf16[4096,128]{1,0:T(8,128)(2,1)S(1)} %get-tuple-element.140.mixed_ref, f32[16,40,128]{2,1,0:T(8,128)S(1)} %get-tuple-element.112.re_ref, f32[16,40,128]{2,1,0:T(8,128)S(1)} %get-tuple-element.113.im_ref), custom_call_target="tpu_custom_call" | custom-call | flops 6000000 | bytes 6144 | tf_op jit(solution)/shard_map/pallas_call | solution.py:675
  39.1 1.1 %collective-permute-done.4.got_ref = f32[1,4,2,32,128]{4,3,2,1,0:T(8,128)S(1)} collective-permute-done((f32[1,4,2,32,128]{4,3,2,1,0:T(8,128)S(1)}, f32[1,4,2,32,128]{4,3,2,1,0:T(8,128)S(1)}, u32[]{:S(2)}, u32[]{:S(2)}) %collective-permute-start.4) | collective-permute-done | bytes 131104 | tf_op jit(solution)/shard_map/ppermute | solution.py:613
  40.2 0.0 collective-permute-done.5.more_ref
  40.3 0.2 shard_map.146
  40.4 0.1 shard_map.147.a_ref
  40.6 1.6 %collective-permute-start.6 = (f32[4,2,32,128]{3,2,1,0:T(8,128)S(1)}, f32[4,2,32,128]{3,2,1,0:T(8,128)S(1)}, u32[]{:S(2)}, u32[]{:S(2)}) collective-permute-start(f32[4,2,32,128]{3,2,1,0:T(8,128)S(1)} %get-tuple-element.159.into_y.into_ref), channel_id=1, source_target_pairs={{0,2},{1,3},{2,0},{3,1},{4,6},{5,7},{6,4},{7,5},{8,10},{9,11},{10,... | collective-permute-start | bytes 393224 | tf_op jit(solution)/shard_map/ppermute | solution.py:613
  42.2 0.0 collective-permute-start.7
  42.2 1.2 %collective-permute-done.7.b_ref = f32[4,16,128]{2,1,0:T(8,128)S(1)} collective-permute-done((f32[4,16,128]{2,1,0:T(8,128)S(1)}, f32[4,16,128]{2,1,0:T(8,128)S(1)}, u32[]{:S(2)}, u32[]{:S(2)}) %collective-permute-start.7) | collective-permute-done | bytes 32800 | tf_op jit(solution)/shard_map/ppermute | solution.py:613
  43.4 0.5 collective-permute-start.8
  43.9 2.0 %shard_map.149 = bf16[4096,128]{1,0:T(8,128)(2,1)} custom-call(bf16[4096,128]{1,0:T(8,128)(2,1)S(1)} %get-tuple-element.162.a_ref, bf16[4096,128]{1,0:T(8,128)(2,1)} %b_hbm.1), custom_call_target="tpu_custom_call" | custom-call | flops 1000000 | bytes 1024 | tf_op jit(solution)/shard_map/pallas_call | solution.py:796
  45.9 1.4 %collective-permute-done.8.b_ref = f32[4,16,128]{2,1,0:T(8,128)S(1)} collective-permute-done((f32[4,16,128]{2,1,0:T(8,128)S(1)}, f32[4,16,128]{2,1,0:T(8,128)S(1)}, u32[]{:S(2)}, u32[]{:S(2)}) %collective-permute-start.8) | collective-permute-done | bytes 32800 | tf_op jit(solution)/shard_map/ppermute | solution.py:613
  47.4 0.0 collective-permute-done.6.other_ref
  47.4 0.1 shard_map.151.mine_ref
  47.5 0.1 collective-permute-start.10
  47.5 0.7 %collective-permute-start.9 = (f32[4,16,128]{2,1,0:T(8,128)S(1)}, f32[4,16,128]{2,1,0:T(8,128)S(1)}, u32[]{:S(2)}, u32[]{:S(2)}) collective-permute-start(f32[4,16,128]{2,1,0:T(8,128)S(1)} %shard_map.150.a_ref), channel_id=1, source_target_pairs={{0,4},{1,5},{2,6},{3,7},{4,0},{5,1},{6,2},{7,3},{8,12},{9,13},{10,... | collective-permute-start | bytes 98312 | tf_op jit(solution)/shard_map/ppermute | solution.py:613
  48.3 0.8 %collective-permute-done.10.other_ref = f32[8,2,32,128]{3,2,1,0:T(8,128)S(1)} collective-permute-done((f32[8,2,32,128]{3,2,1,0:T(8,128)S(1)}, f32[8,2,32,128]{3,2,1,0:T(8,128)S(1)}, u32[]{:S(2)}, u32[]{:S(2)}) %collective-permute-start.10) | collective-permute-done | bytes 262176 | tf_op jit(solution)/shard_map/ppermute | solution.py:613
  49.1 1.9 %shard_map.152.grouped = f32[4096,128]{1,0:T(8,128)S(1)} custom-call(f32[8,2,32,128]{3,2,1,0:T(8,128)S(1)} %shard_map.151.mine_ref, f32[8,2,32,128]{3,2,1,0:T(8,128)S(1)} %collective-permute-done.10.other_ref, f32[16,2,32,128]{3,2,1,0:T(8,128)S(1)} %collective-permute-done.got_ref.near_ref, f32[24,2,32,128]{3,2,1,0:T(8,128)S(1)} %collective-permute-done.3.more_ref, ...), custom_call_target="tpu_custom_call" | custom-call | flops 1000000 | bytes 1024 | tf_op jit(solution)/shard_map/pallas_call | solution.py:818
  51.0 0.6 collective-permute-done.9.b_ref
  51.5 2.1 %collective-permute-start.11 = (f32[4,16,128]{2,1,0:T(8,128)S(1)}, f32[4,16,128]{2,1,0:T(8,128)S(1)}, u32[]{:S(2)}, u32[]{:S(2)}) collective-permute-start(f32[4,16,128]{2,1,0:T(8,128)S(1)} %shard_map.153.total_ref), channel_id=1, source_target_pairs={{0,8},{1,9},{2,10},{3,11},{4,12},{5,13},{6,14},{7,15},{8,0},{9,1},... | collective-permute-start | bytes 98312 | tf_op jit(solution)/shard_map/ppermute | solution.py:613
  53.7 0.0 copy-start
  53.7 0.0 copy-start.1
  53.7 0.0 copy-start.2
  53.7 5.1 %shard_map.154 = (bf16[4096,128]{1,0:T(8,128)(2,1)}, bf16[4096,128]{1,0:T(8,128)(2,1)}) custom-call(s32[32,128]{1,0:T(8,128)S(1)} %get-tuple-element.174.pos_ref, f32[4096,128]{1,0:T(8,128)S(1)} %shard_map.152.grouped, bf16[4096,128]{1,0:T(8,128)(2,1)S(1)} %get-tuple-element.176.k_ref, bf16[4096,128]{1,0:T(8,128)(2,1)S(1)} %get-tuple-element.177.v_ref), custom_call_target="tpu_custom_call" | custom-call | flops 1000000 | bytes 1024 | tf_op jit(solution)/shard_map/pallas_call | solution.py:834
  58.8 0.0 collective-permute-done.11.last_ref
  58.8 0.0 copy-done
  58.8 0.0 copy-done.1
  58.8 0.0 copy-done.2
  58.8 0.9 %shard_map.155 = (f32[16,128]{1,0:T(8,128)}, f32[16,128]{1,0:T(8,128)}, f32[2,16,128]{2,1,0:T(8,128)}) custom-call(f32[4,16,128]{2,1,0:T(8,128)S(1)} %shard_map.153.total_ref, f32[4,16,128]{2,1,0:T(8,128)S(1)} %collective-permute-done.11.last_ref, f32[16,128]{1,0:T(8,128)S(1)} %bitcast.10, f32[16,128]{1,0:T(8,128)S(1)} %bitcast.12, f32[2,16,128]{2,1,0:T(8,128)S(1)} %bitcast.8), custom_call_target="tpu_custom_call" | custom-call | tf_op jit(solution)/shard_map/pallas_call | solution.py:846
  (4 shorter events, 0.1 us)
Async XLA Ops:
  10.5 2.1 %collective-permute-start = (f32[16,2,32,128]{3,2,1,0:T(8,128)S(1)}, f32[16,2,32,128]{3,2,1,0:T(8,128)S(1)}, u32[]{:S(2)}, u32[]{:S(2)}) collective-permute-start(f32[16,2,32,128]{3,2,1,0:T(8,128)S(1)} %get-tuple-element.100), channel_id=1, source_target_pairs={{0,1},{1,0},{2,3},{3,2},{4,5},{5,4},{6,7},{7,6},{8,9},{9,8},{10,11... | collective-permute-start | bytes 1572872 | tf_op jit(solution)/shard_map/ppermute | solution.py:613
  12.7 9.5 %collective-permute-start.1 = (f32[8,2,32,128]{3,2,1,0:T(8,128)S(1)}, f32[8,2,32,128]{3,2,1,0:T(8,128)S(1)}, u32[]{:S(2)}, u32[]{:S(2)}) collective-permute-start(f32[8,2,32,128]{3,2,1,0:T(8,128)S(1)} %get-tuple-element.109), channel_id=1, source_target_pairs={{0,2},{1,3},{2,0},{3,1},{4,6},{5,7},{6,4},{7,5},{8,10},{9,11},{10,... | collective-permute-start | bytes 786440 | tf_op jit(solution)/shard_map/ppermute | solution.py:613
  22.2 2.3 %collective-permute-start.3 = (f32[24,2,32,128]{3,2,1,0:T(8,128)S(1)}, f32[24,2,32,128]{3,2,1,0:T(8,128)S(1)}, u32[]{:S(2)}, u32[]{:S(2)}) collective-permute-start(f32[24,2,32,128]{3,2,1,0:T(8,128)S(1)} %get-tuple-element.127), channel_id=1, source_target_pairs={{0,1},{1,0},{2,3},{3,2},{4,5},{5,4},{6,7},{7,6},{8,9},{9,8},{10,11... | collective-permute-start | bytes 2359304 | tf_op jit(solution)/shard_map/ppermute | solution.py:613
  22.3 8.8 %collective-permute-start.2 = (f32[2,4,2,32,128]{4,3,2,1,0:T(8,128)S(1)}, f32[2,4,2,32,128]{4,3,2,1,0:T(8,128)S(1)}, u32[]{:S(2)}, u32[]{:S(2)}) collective-permute-start(f32[2,4,2,32,128]{4,3,2,1,0:T(8,128)S(1)} %shard_map.140.total_ref.yx_ref), channel_id=1, source_target_pairs={{0,4},{1,5},{2,6},{3,7},{4,0},{5,1},{6,2},{7,3},{8,12},{9,13},{10,... | collective-permute-start | bytes 786440 | tf_op jit(solution)/shard_map/ppermute | solution.py:613
  24.9 15.4 %collective-permute-start.5 = (f32[12,2,32,128]{3,2,1,0:T(8,128)S(1)}, f32[12,2,32,128]{3,2,1,0:T(8,128)S(1)}, u32[]{:S(2)}, u32[]{:S(2)}) collective-permute-start(f32[12,2,32,128]{3,2,1,0:T(8,128)S(1)} %get-tuple-element.151), channel_id=1, source_target_pairs={{0,2},{1,3},{2,0},{3,1},{4,6},{5,7},{6,4},{7,5},{8,10},{9,11},{10,... | collective-permute-start | bytes 1179656 | tf_op jit(solution)/shard_map/ppermute | solution.py:613
  31.2 9.0 %collective-permute-start.4 = (f32[1,4,2,32,128]{4,3,2,1,0:T(8,128)S(1)}, f32[1,4,2,32,128]{4,3,2,1,0:T(8,128)S(1)}, u32[]{:S(2)}, u32[]{:S(2)}) collective-permute-start(f32[1,4,2,32,128]{4,3,2,1,0:T(8,128)S(1)} %get-tuple-element.138), channel_id=1, source_target_pairs={{0,8},{1,9},{2,10},{3,11},{4,12},{5,13},{6,14},{7,15},{8,0},{9,1},... | collective-permute-start | bytes 393224 | tf_op jit(solution)/shard_map/ppermute | solution.py:613
  40.6 6.8 %collective-permute-start.6 = (f32[4,2,32,128]{3,2,1,0:T(8,128)S(1)}, f32[4,2,32,128]{3,2,1,0:T(8,128)S(1)}, u32[]{:S(2)}, u32[]{:S(2)}) collective-permute-start(f32[4,2,32,128]{3,2,1,0:T(8,128)S(1)} %get-tuple-element.159.into_y.into_ref), channel_id=1, source_target_pairs={{0,2},{1,3},{2,0},{3,1},{4,6},{5,7},{6,4},{7,5},{8,10},{9,11},{10,... | collective-permute-start | bytes 393224 | tf_op jit(solution)/shard_map/ppermute | solution.py:613
  42.2 1.2 %collective-permute-start.7 = (f32[4,16,128]{2,1,0:T(8,128)S(1)}, f32[4,16,128]{2,1,0:T(8,128)S(1)}, u32[]{:S(2)}, u32[]{:S(2)}) collective-permute-start(f32[4,16,128]{2,1,0:T(8,128)S(1)} %shard_map.147.a_ref), channel_id=1, source_target_pairs={{0,1},{1,0},{2,3},{3,2},{4,5},{5,4},{6,7},{7,6},{8,9},{9,8},{10,11... | collective-permute-start | bytes 98312 | tf_op jit(solution)/shard_map/ppermute | solution.py:613
  43.4 3.9 %collective-permute-start.8 = (f32[4,16,128]{2,1,0:T(8,128)S(1)}, f32[4,16,128]{2,1,0:T(8,128)S(1)}, u32[]{:S(2)}, u32[]{:S(2)}) collective-permute-start(f32[4,16,128]{2,1,0:T(8,128)S(1)} %shard_map.148.a_ref), channel_id=1, source_target_pairs={{0,2},{1,3},{2,0},{3,1},{4,6},{5,7},{6,4},{7,5},{8,10},{9,11},{10,... | collective-permute-start | bytes 98312 | tf_op jit(solution)/shard_map/ppermute | solution.py:613
  47.5 1.6 %collective-permute-start.10 = (f32[8,2,32,128]{3,2,1,0:T(8,128)S(1)}, f32[8,2,32,128]{3,2,1,0:T(8,128)S(1)}, u32[]{:S(2)}, u32[]{:S(2)}) collective-permute-start(f32[8,2,32,128]{3,2,1,0:T(8,128)S(1)} %shard_map.151.mine_ref), channel_id=1, source_target_pairs={{0,1},{1,0},{2,3},{3,2},{4,5},{5,4},{6,7},{7,6},{8,9},{9,8},{10,11... | collective-permute-start | bytes 786440 | tf_op jit(solution)/shard_map/ppermute | solution.py:613
  47.5 4.0 %collective-permute-start.9 = (f32[4,16,128]{2,1,0:T(8,128)S(1)}, f32[4,16,128]{2,1,0:T(8,128)S(1)}, u32[]{:S(2)}, u32[]{:S(2)}) collective-permute-start(f32[4,16,128]{2,1,0:T(8,128)S(1)} %shard_map.150.a_ref), channel_id=1, source_target_pairs={{0,4},{1,5},{2,6},{3,7},{4,0},{5,1},{6,2},{7,3},{8,12},{9,13},{10,... | collective-permute-start | bytes 98312 | tf_op jit(solution)/shard_map/ppermute | solution.py:613
  51.5 7.3 %collective-permute-start.11 = (f32[4,16,128]{2,1,0:T(8,128)S(1)}, f32[4,16,128]{2,1,0:T(8,128)S(1)}, u32[]{:S(2)}, u32[]{:S(2)}) collective-permute-start(f32[4,16,128]{2,1,0:T(8,128)S(1)} %shard_map.153.total_ref), channel_id=1, source_target_pairs={{0,8},{1,9},{2,10},{3,11},{4,12},{5,13},{6,14},{7,15},{8,0},{9,1},... | collective-permute-start | bytes 98312 | tf_op jit(solution)/shard_map/ppermute | solution.py:613
  53.7 5.1 %copy-start = (f32[2,128,16]{1,2,0:T(8,128)S(1)}, f32[2,128,16]{1,2,0:T(8,128)}, u32[]{:S(2)}) copy-start(f32[2,128,16]{1,2,0:T(8,128)} %param.17) | copy-start | bytes 49156
  53.7 5.2 %copy-start.1 = (f32[128,16]{0,1:T(8,128)S(1)}, f32[128,16]{0,1:T(8,128)}, u32[]{:S(2)}) copy-start(f32[128,16]{0,1:T(8,128)} %param.15) | copy-start | bytes 24580
  53.7 5.2 %copy-start.2 = (f32[128,16]{0,1:T(8,128)S(1)}, f32[128,16]{0,1:T(8,128)}, u32[]{:S(2)}) copy-start(f32[128,16]{0,1:T(8,128)} %param.16) | copy-start | bytes 24580

commit v4 on v3

--- a/solution.py
+++ b/solution.py
@@ -11,6 +11,8 @@
 BF16 = jnp.bfloat16
 LANES = 128
 COST = 10**6
+CHUNKS = 2
+BATCH = 128
 UNROLL = {4: 4, 5: 5, 6: 3}
 
 
@@ -69,12 +71,16 @@
     return sum(dot(pick, part, NT) for part in three(tiled))
 
 
-def from_groups(values, picks, per):
+def from_groups(parts, picks, per):
     pick, inside = picks
-    spread = sum(dot(part, pick, TN) for part in three(values))
-    spread = jnp.where(inside, spread, 0.0)
-    modes = spread.shape[0] // per
-    return sum(spread[f * modes : (f + 1) * modes] for f in range(per))
+    stack = jnp.concatenate(three(jnp.concatenate(parts, axis=1)), axis=0)
+    spread = dot(stack, jnp.concatenate([pick] * 3, axis=0), TN)
+    lanes, outs = inside.shape[0], []
+    modes = lanes // per
+    for i in range(len(parts)):
+        own = jnp.where(inside, spread[i * lanes : (i + 1) * lanes], 0.0)
+        outs.append(sum(own[f * modes : (f + 1) * modes] for f in range(per)))
+    return outs
 
 
 def mode_rates(decay_rate, twist, length):
@@ -168,22 +174,33 @@
     gate_ref, mixed_ref, y_lo, y_hi, x_lo, x_hi, ahead_ref, pos_ref, re_hbm, im_hbm, factor_ref,
     go_ref, k_ref, v_ref,
     filter_ref, rate_ref, twist_ref, res_ref, q_ref,
-    natural_g, natural_m, grouped_g, grouped_m, re_ref, im_ref, spot_ref, sems, load_sems,
+    grouped_g, grouped_m, re_ref, im_ref, spot_ref, sems, load_sems,
 ):
     channels = go_ref.shape[0]
-    loads = [
-        pltpu.make_async_copy(source, target, load_sems.at[i])
+    first_loads = [
+        pltpu.make_async_copy(source, target, load_sems.at[i, 0])
         for i, (source, target) in enumerate(
-            (
-                (filter_hbm, filter_ref), (rate_hbm, rate_ref), (twist_hbm, twist_ref),
-                (res_hbm, res_ref), (go_hbm, go_ref), (q_hbm, q_ref), (k_hbm, k_ref),
-                (v_hbm, v_ref),
-            )
+            ((filter_hbm, filter_ref), (rate_hbm, rate_ref), (twist_hbm, twist_ref),
+             (res_hbm, res_ref))
         )
     ]
-    for load in loads:
+    rows = channels // CHUNKS
+
+    def loads(chunk):
+        at = pl.ds(chunk * rows, rows)
+        return [
+            pltpu.make_async_copy(source.at[at, :], target.at[at, :], load_sems.at[i, 1 + chunk])
+            for i, (source, target) in enumerate(
+                ((go_hbm, go_ref), (q_hbm, q_ref), (k_hbm, k_ref), (v_hbm, v_ref))
+            )
+        ]
+
+    for load in first_loads:
         load.start()
-    for load in loads[:4]:
+    for chunk in range(CHUNKS):
+        for load in loads(chunk):
+            load.start()
+    for load in first_loads:
         load.wait()
     place(members, filter_ref, pos_ref)
     spots = pltpu.make_async_copy(pos_ref, spot_ref, sems.at[0])
@@ -196,27 +213,22 @@
     ]
     for table in tables:
         table.start()
-    tile = 256
-    for load in loads[4:]:
-        load.wait()
-
-    @pl.loop(0, channels // tile)
-    def _(i):
-        at = pl.ds(pl.multiple_of(i * tile, tile), tile)
-        gate = (go_ref[at, :].astype(F32) * q_ref[at, :].astype(F32)).astype(BF16)
-        mixed = (k_ref[at, :].astype(F32) * v_ref[at, :].astype(F32)).astype(BF16)
-        natural_g[at, :] = gate.astype(F32)
-        natural_m[at, :] = mixed.astype(F32)
-
     spots.wait()
-
-    @pl.loop(0, channels // LANES)
-    def _(i):
-        base = pl.multiple_of(i * LANES, LANES)
-        for u in range(LANES):
-            to = spot_ref[i, u]
-            grouped_g[pl.ds(to, 1), :] = natural_g[pl.ds(base + u, 1), :]
-            grouped_m[pl.ds(to, 1), :] = natural_m[pl.ds(base + u, 1), :]
+    for chunk in range(CHUNKS):
+        for load in loads(chunk):
+            load.wait()
+
+        @pl.loop(chunk * rows // BATCH, (chunk + 1) * rows // BATCH)
+        def _(i):
+            base = pl.multiple_of(i * BATCH, BATCH)
+            at = pl.ds(base, BATCH)
+            gate = (go_ref[at, :].astype(F32) * q_ref[at, :].astype(F32)).astype(BF16)
+            mixed = (k_ref[at, :].astype(F32) * v_ref[at, :].astype(F32)).astype(BF16)
+            gate, mixed = gate.astype(F32), mixed.astype(F32)
+            for u in range(BATCH):
+                to = spot_ref[i * BATCH // LANES + u // LANES, u % LANES]
+                grouped_g[pl.ds(to, 1), :] = gate[u : u + 1]
+                grouped_m[pl.ds(to, 1), :] = mixed[u : u + 1]
 
     size = (LANES // modes) * members
     half = y_lo.shape[0]
@@ -581,8 +593,8 @@
     picks = block_picks(filters // per, per, modes)
     rate, twist = rate_ref[...], twist_ref[...]
     rho, angle, scale = mode_rates(rate, twist, length)
-    a_re, a_im, w_re, w_im = (
-        from_groups(total_ref[i] + last_ref[i], picks, per) for i in range(4)
+    a_re, a_im, w_re, w_im = from_groups(
+        [total_ref[i] + last_ref[i] for i in range(4)], picks, per
     )
     r0, r1 = res_ref[0], res_ref[1]
     b_re, b_im = complex_product(r0 * scale, r1 * scale, w_re, w_im)
@@ -654,9 +666,9 @@
         scratch_shapes=[
             pltpu.VMEM(blocks, jnp.int32), pltpu.VMEM((modes, filters), F32),
             pltpu.VMEM((modes, filters), F32), pltpu.VMEM((2, modes, filters), F32),
-            pltpu.VMEM(wide, BF16), *[pltpu.VMEM(wide, F32)] * 4,
+            pltpu.VMEM(wide, BF16), *[pltpu.VMEM(wide, F32)] * 2,
             *[pltpu.VMEM(table_shape, F32)] * 2, pltpu.SMEM(blocks, jnp.int32),
-            pltpu.SemaphoreType.DMA((3,)), pltpu.SemaphoreType.DMA((8,)),
+            pltpu.SemaphoreType.DMA((3,)), pltpu.SemaphoreType.DMA((4, 1 + CHUNKS)),
         ],
         compiler_params=params(20),
     )(

time: 60 us -> 59.5 us (level)
  transfers between devices with their start and end apart: 12 -> 12, of which waited for: 9 -> 9; matrix products, arithmetic and copies ran while one was open for 0% -> 0% of each run, Pallas kernels for 41% -> 42%
where the time goes in v4:
time: 59.5 us; the launch traced here: 59.2 us
  Pallas kernels  35.5 us (60%)
  starting transfers between devices  15 us (25%)
  waiting for transfers between devices  7.95 us (13%)
  between operations  0.79 us (1%)
    ppermute x12, starting transfers between devices, swap(): return lax.ppermute(value, 'seq', [(i, i ^ bit) for i in range(count)])  15 us
    pallas_call x3, Pallas kernels, conv_call(): pl.pallas_call(functools.partial(conv_kernel, members, modes, first, UNRO...  13.1 us
    pallas_call x1, Pallas kernels, body(): pl.pallas_call(functools.partial(states_kernel, members, modes, count), o...  9.36 us
    ppermute x12, waiting for transfers between devices, swap(): return lax.ppermute(value, 'seq', [(i, i ^ bit) for i in range(count)])  7.95 us
    pallas_call x1, Pallas kernels, body(): pl.pallas_call(finish_kernel, out_shape=(shape(wide, BF16), shape(wide, B...  5.12 us
    pallas_call x1, Pallas kernels, body(): pl.pallas_call(functools.partial(rates_kernel, members, modes), out_shape...  2.08 us
    pallas_call x1, Pallas kernels, body(): pl.pallas_call(product_kernel, out_shape=shape(wide, BF16), in_specs=vmem...  2.04 us
    pallas_call x1, Pallas kernels, body(): pl.pallas_call(functools.partial(cross_kernel, members, modes, calls), ou...  1.89 us
  transfers between devices with their start and end apart: 12, of which 9 were waited for; matrix products, arithmetic and copies ran while one was open for 0% of the time, Pallas kernels for 42%

profile of v4, /device:TPU:0, one launch (start us, length us, event | category | flops | bytes accessed | tf_op | source)
XLA Modules:
  0.0 59.2 jit_solution(14077249264943147947)
XLA Ops:
  0.6 9.4 %shard_map.136 = (bf16[4096,128]{1,0:T(8,128)(2,1)S(1)}, bf16[4096,128]{1,0:T(8,128)(2,1)S(1)}, f32[8,2,32,128]{3,2,1,0:T(8,128)S(1)}, f32[8,2,32,128]{3,2,1,0:T...) custom-call(s32[32,128]{1,0:T(8,128)} %bitcast.13, ...), custom_call_target="tpu_custom_call" | custom-call | tf_op jit(solution)/shard_map/pallas_call | solution.py:657
  10.0 0.5 collective-permute-start
  10.6 1.5 %collective-permute-done.got_ref.near_ref = f32[16,2,32,128]{3,2,1,0:T(8,128)S(1)} collective-permute-done((f32[16,2,32,128]{3,2,1,0:T(8,128)S(1)}, f32[16,2,32,128]{3,2,1,0:T(8,128)S(1)}, u32[]{:S(2)}, u32[]{:S(2)}) %collective-permute-start) | collective-permute-done | bytes 524320 | tf_op jit(solution)/shard_map/ppermute | solution.py:625
  12.1 0.1 shard_map.137
  12.2 2.9 %collective-permute-start.1 = (f32[8,2,32,128]{3,2,1,0:T(8,128)S(1)}, f32[8,2,32,128]{3,2,1,0:T(8,128)S(1)}, u32[]{:S(2)}, u32[]{:S(2)}) collective-permute-start(f32[8,2,32,128]{3,2,1,0:T(8,128)S(1)} %get-tuple-element.109), channel_id=1, source_target_pairs={{0,2},{1,3},{2,0},{3,1},{4,6},{5,7},{6,4},{7,5},{8,10},{9,11},{10,... | collective-permute-start | bytes 786440 | tf_op jit(solution)/shard_map/ppermute | solution.py:625
  15.2 2.1 %shard_map.138 = (f32[8,2,32,128]{3,2,1,0:T(8,128)S(1)}, f32[8,2,32,128]{3,2,1,0:T(8,128)S(1)}, f32[8,2,32,128]{3,2,1,0:T(8,128)S(1)}, f32[8,2,32,128]{3,2,1,0:T(8,128)S(1)}, f32[24,2,32,128]{3,2,1,0:T(8,128)S(1)}) custom-call(bf16[4096,128]{1,0:T(8,128)(2,1)S(1)} %get-tuple-element.139.gate_ref, bf16[4096,128]{1,0:T(8,128)(2,1)S(1)} %get-tuple-element.140.mixed_ref, ...), custom_call_target="tpu_custom_call" | custom-call | flops 2000000 | bytes 1024 | tf_op jit(solution)/shard_map/pallas_call | solution.py:731
  17.2 4.0 %shard_map.139 = (f32[1280,128]{1,0:T(8,128)S(1)}, f32[5,4,128]{2,1,0:T(4,128)S(1)}) custom-call(bf16[4096,128]{1,0:T(8,128)(2,1)S(1)} %get-tuple-element.139.gate_ref, bf16[4096,128]{1,0:T(8,128)(2,1)S(1)} %get-tuple-element.140.mixed_ref, f32[16,40,128]{2,1,0:T(8,128)S(1)} %get-tuple-element.112.re_ref, f32[16,40,128]{2,1,0:T(8,128)S(1)} %get-tuple-element.113.im_ref), custom_call_target="tpu_custom_call" | custom-call | flops 5000000 | bytes 5120 | tf_op jit(solution)/shard_map/pallas_call | solution.py:687
  21.2 0.5 collective-permute-done.1.got_ref
  21.8 0.0 collective-permute-start.3
  21.8 0.1 shard_map.140.total_ref.yx_ref
  21.8 1.9 %collective-permute-start.2 = (f32[2,4,2,32,128]{4,3,2,1,0:T(8,128)S(1)}, f32[2,4,2,32,128]{4,3,2,1,0:T(8,128)S(1)}, u32[]{:S(2)}, u32[]{:S(2)}) collective-permute-start(f32[2,4,2,32,128]{4,3,2,1,0:T(8,128)S(1)} %shard_map.140.total_ref.yx_ref), channel_id=1, source_target_pairs={{0,4},{1,5},{2,6},{3,7},{4,0},{5,1},{6,2},{7,3},{8,12},{9,13},{10,... | collective-permute-start | bytes 786440 | tf_op jit(solution)/shard_map/ppermute | solution.py:625
  23.7 0.3 collective-permute-done.3.more_ref
  24.1 0.3 shard_map.141
  24.4 1.8 %collective-permute-start.5 = (f32[12,2,32,128]{3,2,1,0:T(8,128)S(1)}, f32[12,2,32,128]{3,2,1,0:T(8,128)S(1)}, u32[]{:S(2)}, u32[]{:S(2)}) collective-permute-start(f32[12,2,32,128]{3,2,1,0:T(8,128)S(1)} %get-tuple-element.151), channel_id=1, source_target_pairs={{0,2},{1,3},{2,0},{3,1},{4,6},{5,7},{6,4},{7,5},{8,10},{9,11},{10,... | collective-permute-start | bytes 1179656 | tf_op jit(solution)/shard_map/ppermute | solution.py:625
  26.2 4.0 %shard_map.142 = (f32[1280,128]{1,0:T(8,128)S(1)}, f32[5,4,128]{2,1,0:T(4,128)S(1)}) custom-call(bf16[4096,128]{1,0:T(8,128)(2,1)S(1)} %get-tuple-element.139.gate_ref, bf16[4096,128]{1,0:T(8,128)(2,1)S(1)} %get-tuple-element.140.mixed_ref, f32[16,40,128]{2,1,0:T(8,128)S(1)} %get-tuple-element.112.re_ref, f32[16,40,128]{2,1,0:T(8,128)S(1)} %get-tuple-element.113.im_ref), custom_call_target="tpu_custom_call" | custom-call | flops 5000000 | bytes 5120 | tf_op jit(solution)/shard_map/pallas_call | solution.py:687
  30.2 0.5 collective-permute-done.2.got_ref
  30.7 0.1 shard_map.143
  30.8 2.8 %collective-permute-start.4 = (f32[1,4,2,32,128]{4,3,2,1,0:T(8,128)S(1)}, f32[1,4,2,32,128]{4,3,2,1,0:T(8,128)S(1)}, u32[]{:S(2)}, u32[]{:S(2)}) collective-permute-start(f32[1,4,2,32,128]{4,3,2,1,0:T(8,128)S(1)} %get-tuple-element.138), channel_id=1, source_target_pairs={{0,8},{1,9},{2,10},{3,11},{4,12},{5,13},{6,14},{7,15},{8,0},{9,1},... | collective-permute-start | bytes 393224 | tf_op jit(solution)/shard_map/ppermute | solution.py:625
  33.6 5.1 %shard_map.144 = (f32[1536,128]{1,0:T(8,128)S(1)}, f32[6,4,128]{2,1,0:T(4,128)S(1)}) custom-call(bf16[4096,128]{1,0:T(8,128)(2,1)S(1)} %get-tuple-element.139.gate_ref, bf16[4096,128]{1,0:T(8,128)(2,1)S(1)} %get-tuple-element.140.mixed_ref, f32[16,40,128]{2,1,0:T(8,128)S(1)} %get-tuple-element.112.re_ref, f32[16,40,128]{2,1,0:T(8,128)S(1)} %get-tuple-element.113.im_ref), custom_call_target="tpu_custom_call" | custom-call | flops 6000000 | bytes 6144 | tf_op jit(solution)/shard_map/pallas_call | solution.py:687
  38.7 1.1 %collective-permute-done.4.got_ref = f32[1,4,2,32,128]{4,3,2,1,0:T(8,128)S(1)} collective-permute-done((f32[1,4,2,32,128]{4,3,2,1,0:T(8,128)S(1)}, f32[1,4,2,32,128]{4,3,2,1,0:T(8,128)S(1)}, u32[]{:S(2)}, u32[]{:S(2)}) %collective-permute-start.4) | collective-permute-done | bytes 131104 | tf_op jit(solution)/shard_map/ppermute | solution.py:625
  39.8 0.0 collective-permute-done.5.more_ref
  39.8 0.2 shard_map.146
  40.0 0.1 shard_map.147.a_ref
  40.1 1.6 %collective-permute-start.6 = (f32[4,2,32,128]{3,2,1,0:T(8,128)S(1)}, f32[4,2,32,128]{3,2,1,0:T(8,128)S(1)}, u32[]{:S(2)}, u32[]{:S(2)}) collective-permute-start(f32[4,2,32,128]{3,2,1,0:T(8,128)S(1)} %get-tuple-element.159.into_y.into_ref), channel_id=1, source_target_pairs={{0,2},{1,3},{2,0},{3,1},{4,6},{5,7},{6,4},{7,5},{8,10},{9,11},{10,... | collective-permute-start | bytes 393224 | tf_op jit(solution)/shard_map/ppermute | solution.py:625
  41.8 0.0 collective-permute-start.7
  41.8 1.2 %collective-permute-done.7.b_ref = f32[4,16,128]{2,1,0:T(8,128)S(1)} collective-permute-done((f32[4,16,128]{2,1,0:T(8,128)S(1)}, f32[4,16,128]{2,1,0:T(8,128)S(1)}, u32[]{:S(2)}, u32[]{:S(2)}) %collective-permute-start.7) | collective-permute-done | bytes 32800 | tf_op jit(solution)/shard_map/ppermute | solution.py:625
  43.0 0.5 collective-permute-start.8
  43.4 2.0 %shard_map.149 = bf16[4096,128]{1,0:T(8,128)(2,1)} custom-call(bf16[4096,128]{1,0:T(8,128)(2,1)S(1)} %get-tuple-element.162.a_ref, bf16[4096,128]{1,0:T(8,128)(2,1)} %b_hbm.1), custom_call_target="tpu_custom_call" | custom-call | flops 1000000 | bytes 1024 | tf_op jit(solution)/shard_map/pallas_call | solution.py:808
  45.5 1.4 %collective-permute-done.8.b_ref = f32[4,16,128]{2,1,0:T(8,128)S(1)} collective-permute-done((f32[4,16,128]{2,1,0:T(8,128)S(1)}, f32[4,16,128]{2,1,0:T(8,128)S(1)}, u32[]{:S(2)}, u32[]{:S(2)}) %collective-permute-start.8) | collective-permute-done | bytes 32800 | tf_op jit(solution)/shard_map/ppermute | solution.py:625
  46.9 0.0 collective-permute-done.6.other_ref
  46.9 0.1 shard_map.151.mine_ref
  47.0 0.1 collective-permute-start.10
  47.1 0.7 %collective-permute-start.9 = (f32[4,16,128]{2,1,0:T(8,128)S(1)}, f32[4,16,128]{2,1,0:T(8,128)S(1)}, u32[]{:S(2)}, u32[]{:S(2)}) collective-permute-start(f32[4,16,128]{2,1,0:T(8,128)S(1)} %shard_map.150.a_ref), channel_id=1, source_target_pairs={{0,4},{1,5},{2,6},{3,7},{4,0},{5,1},{6,2},{7,3},{8,12},{9,13},{10,... | collective-permute-start | bytes 98312 | tf_op jit(solution)/shard_map/ppermute | solution.py:625
  47.8 0.8 %collective-permute-done.10.other_ref = f32[8,2,32,128]{3,2,1,0:T(8,128)S(1)} collective-permute-done((f32[8,2,32,128]{3,2,1,0:T(8,128)S(1)}, f32[8,2,32,128]{3,2,1,0:T(8,128)S(1)}, u32[]{:S(2)}, u32[]{:S(2)}) %collective-permute-start.10) | collective-permute-done | bytes 262176 | tf_op jit(solution)/shard_map/ppermute | solution.py:625
  48.6 1.9 %shard_map.152.grouped = f32[4096,128]{1,0:T(8,128)S(1)} custom-call(f32[8,2,32,128]{3,2,1,0:T(8,128)S(1)} %shard_map.151.mine_ref, f32[8,2,32,128]{3,2,1,0:T(8,128)S(1)} %collective-permute-done.10.other_ref, f32[16,2,32,128]{3,2,1,0:T(8,128)S(1)} %collective-permute-done.got_ref.near_ref, f32[24,2,32,128]{3,2,1,0:T(8,128)S(1)} %collective-permute-done.3.more_ref, ...), custom_call_target="tpu_custom_call" | custom-call | flops 1000000 | bytes 1024 | tf_op jit(solution)/shard_map/pallas_call | solution.py:830
  50.5 0.6 collective-permute-done.9.b_ref
  51.1 2.1 %collective-permute-start.11 = (f32[4,16,128]{2,1,0:T(8,128)S(1)}, f32[4,16,128]{2,1,0:T(8,128)S(1)}, u32[]{:S(2)}, u32[]{:S(2)}) collective-permute-start(f32[4,16,128]{2,1,0:T(8,128)S(1)} %shard_map.153.total_ref), channel_id=1, source_target_pairs={{0,8},{1,9},{2,10},{3,11},{4,12},{5,13},{6,14},{7,15},{8,0},{9,1},... | collective-permute-start | bytes 98312 | tf_op jit(solution)/shard_map/ppermute | solution.py:625
  53.2 0.0 copy-start
  53.2 0.0 copy-start.1
  53.2 0.0 copy-start.2
  53.2 5.1 %shard_map.154 = (bf16[4096,128]{1,0:T(8,128)(2,1)}, bf16[4096,128]{1,0:T(8,128)(2,1)}) custom-call(s32[32,128]{1,0:T(8,128)S(1)} %get-tuple-element.174.pos_ref, f32[4096,128]{1,0:T(8,128)S(1)} %shard_map.152.grouped, bf16[4096,128]{1,0:T(8,128)(2,1)S(1)} %get-tuple-element.176.k_ref, bf16[4096,128]{1,0:T(8,128)(2,1)S(1)} %get-tuple-element.177.v_ref), custom_call_target="tpu_custom_call" | custom-call | flops 1000000 | bytes 1024 | tf_op jit(solution)/shard_map/pallas_call | solution.py:846
  58.3 0.0 collective-permute-done.11.last_ref
  58.4 0.0 copy-done
  58.4 0.0 copy-done.1
  58.4 0.0 copy-done.2
  58.4 0.8 %shard_map.155 = (f32[16,128]{1,0:T(8,128)}, f32[16,128]{1,0:T(8,128)}, f32[2,16,128]{2,1,0:T(8,128)}) custom-call(f32[4,16,128]{2,1,0:T(8,128)S(1)} %shard_map.153.total_ref, f32[4,16,128]{2,1,0:T(8,128)S(1)} %collective-permute-done.11.last_ref, f32[16,128]{1,0:T(8,128)S(1)} %bitcast.10, f32[16,128]{1,0:T(8,128)S(1)} %bitcast.12, f32[2,16,128]{2,1,0:T(8,128)S(1)} %bitcast.8), custom_call_target="tpu_custom_call" | custom-call | tf_op jit(solution)/shard_map/pallas_call | solution.py:858
  (4 shorter events, 0.1 us)
Async XLA Ops:
  10.0 2.1 %collective-permute-start = (f32[16,2,32,128]{3,2,1,0:T(8,128)S(1)}, f32[16,2,32,128]{3,2,1,0:T(8,128)S(1)}, u32[]{:S(2)}, u32[]{:S(2)}) collective-permute-start(f32[16,2,32,128]{3,2,1,0:T(8,128)S(1)} %get-tuple-element.100), channel_id=1, source_target_pairs={{0,1},{1,0},{2,3},{3,2},{4,5},{5,4},{6,7},{7,6},{8,9},{9,8},{10,11... | collective-permute-start | bytes 1572872 | tf_op jit(solution)/shard_map/ppermute | solution.py:625
  12.2 9.5 %collective-permute-start.1 = (f32[8,2,32,128]{3,2,1,0:T(8,128)S(1)}, f32[8,2,32,128]{3,2,1,0:T(8,128)S(1)}, u32[]{:S(2)}, u32[]{:S(2)}) collective-permute-start(f32[8,2,32,128]{3,2,1,0:T(8,128)S(1)} %get-tuple-element.109), channel_id=1, source_target_pairs={{0,2},{1,3},{2,0},{3,1},{4,6},{5,7},{6,4},{7,5},{8,10},{9,11},{10,... | collective-permute-start | bytes 786440 | tf_op jit(solution)/shard_map/ppermute | solution.py:625
  21.8 2.3 %collective-permute-start.3 = (f32[24,2,32,128]{3,2,1,0:T(8,128)S(1)}, f32[24,2,32,128]{3,2,1,0:T(8,128)S(1)}, u32[]{:S(2)}, u32[]{:S(2)}) collective-permute-start(f32[24,2,32,128]{3,2,1,0:T(8,128)S(1)} %get-tuple-element.127), channel_id=1, source_target_pairs={{0,1},{1,0},{2,3},{3,2},{4,5},{5,4},{6,7},{7,6},{8,9},{9,8},{10,11... | collective-permute-start | bytes 2359304 | tf_op jit(solution)/shard_map/ppermute | solution.py:625
  21.8 8.8 %collective-permute-start.2 = (f32[2,4,2,32,128]{4,3,2,1,0:T(8,128)S(1)}, f32[2,4,2,32,128]{4,3,2,1,0:T(8,128)S(1)}, u32[]{:S(2)}, u32[]{:S(2)}) collective-permute-start(f32[2,4,2,32,128]{4,3,2,1,0:T(8,128)S(1)} %shard_map.140.total_ref.yx_ref), channel_id=1, source_target_pairs={{0,4},{1,5},{2,6},{3,7},{4,0},{5,1},{6,2},{7,3},{8,12},{9,13},{10,... | collective-permute-start | bytes 786440 | tf_op jit(solution)/shard_map/ppermute | solution.py:625
  24.4 15.4 %collective-permute-start.5 = (f32[12,2,32,128]{3,2,1,0:T(8,128)S(1)}, f32[12,2,32,128]{3,2,1,0:T(8,128)S(1)}, u32[]{:S(2)}, u32[]{:S(2)}) collective-permute-start(f32[12,2,32,128]{3,2,1,0:T(8,128)S(1)} %get-tuple-element.151), channel_id=1, source_target_pairs={{0,2},{1,3},{2,0},{3,1},{4,6},{5,7},{6,4},{7,5},{8,10},{9,11},{10,... | collective-permute-start | bytes 1179656 | tf_op jit(solution)/shard_map/ppermute | solution.py:625
  30.8 9.0 %collective-permute-start.4 = (f32[1,4,2,32,128]{4,3,2,1,0:T(8,128)S(1)}, f32[1,4,2,32,128]{4,3,2,1,0:T(8,128)S(1)}, u32[]{:S(2)}, u32[]{:S(2)}) collective-permute-start(f32[1,4,2,32,128]{4,3,2,1,0:T(8,128)S(1)} %get-tuple-element.138), channel_id=1, source_target_pairs={{0,8},{1,9},{2,10},{3,11},{4,12},{5,13},{6,14},{7,15},{8,0},{9,1},... | collective-permute-start | bytes 393224 | tf_op jit(solution)/shard_map/ppermute | solution.py:625
  40.1 6.8 %collective-permute-start.6 = (f32[4,2,32,128]{3,2,1,0:T(8,128)S(1)}, f32[4,2,32,128]{3,2,1,0:T(8,128)S(1)}, u32[]{:S(2)}, u32[]{:S(2)}) collective-permute-start(f32[4,2,32,128]{3,2,1,0:T(8,128)S(1)} %get-tuple-element.159.into_y.into_ref), channel_id=1, source_target_pairs={{0,2},{1,3},{2,0},{3,1},{4,6},{5,7},{6,4},{7,5},{8,10},{9,11},{10,... | collective-permute-start | bytes 393224 | tf_op jit(solution)/shard_map/ppermute | solution.py:625
  41.8 1.2 %collective-permute-start.7 = (f32[4,16,128]{2,1,0:T(8,128)S(1)}, f32[4,16,128]{2,1,0:T(8,128)S(1)}, u32[]{:S(2)}, u32[]{:S(2)}) collective-permute-start(f32[4,16,128]{2,1,0:T(8,128)S(1)} %shard_map.147.a_ref), channel_id=1, source_target_pairs={{0,1},{1,0},{2,3},{3,2},{4,5},{5,4},{6,7},{7,6},{8,9},{9,8},{10,11... | collective-permute-start | bytes 98312 | tf_op jit(solution)/shard_map/ppermute | solution.py:625
  43.0 3.9 %collective-permute-start.8 = (f32[4,16,128]{2,1,0:T(8,128)S(1)}, f32[4,16,128]{2,1,0:T(8,128)S(1)}, u32[]{:S(2)}, u32[]{:S(2)}) collective-permute-start(f32[4,16,128]{2,1,0:T(8,128)S(1)} %shard_map.148.a_ref), channel_id=1, source_target_pairs={{0,2},{1,3},{2,0},{3,1},{4,6},{5,7},{6,4},{7,5},{8,10},{9,11},{10,... | collective-permute-start | bytes 98312 | tf_op jit(solution)/shard_map/ppermute | solution.py:625
  47.0 1.6 %collective-permute-start.10 = (f32[8,2,32,128]{3,2,1,0:T(8,128)S(1)}, f32[8,2,32,128]{3,2,1,0:T(8,128)S(1)}, u32[]{:S(2)}, u32[]{:S(2)}) collective-permute-start(f32[8,2,32,128]{3,2,1,0:T(8,128)S(1)} %shard_map.151.mine_ref), channel_id=1, source_target_pairs={{0,1},{1,0},{2,3},{3,2},{4,5},{5,4},{6,7},{7,6},{8,9},{9,8},{10,11... | collective-permute-start | bytes 786440 | tf_op jit(solution)/shard_map/ppermute | solution.py:625
  47.1 4.0 %collective-permute-start.9 = (f32[4,16,128]{2,1,0:T(8,128)S(1)}, f32[4,16,128]{2,1,0:T(8,128)S(1)}, u32[]{:S(2)}, u32[]{:S(2)}) collective-permute-start(f32[4,16,128]{2,1,0:T(8,128)S(1)} %shard_map.150.a_ref), channel_id=1, source_target_pairs={{0,4},{1,5},{2,6},{3,7},{4,0},{5,1},{6,2},{7,3},{8,12},{9,13},{10,... | collective-permute-start | bytes 98312 | tf_op jit(solution)/shard_map/ppermute | solution.py:625
  51.1 7.3 %collective-permute-start.11 = (f32[4,16,128]{2,1,0:T(8,128)S(1)}, f32[4,16,128]{2,1,0:T(8,128)S(1)}, u32[]{:S(2)}, u32[]{:S(2)}) collective-permute-start(f32[4,16,128]{2,1,0:T(8,128)S(1)} %shard_map.153.total_ref), channel_id=1, source_target_pairs={{0,8},{1,9},{2,10},{3,11},{4,12},{5,13},{6,14},{7,15},{8,0},{9,1},... | collective-permute-start | bytes 98312 | tf_op jit(solution)/shard_map/ppermute | solution.py:625
  53.2 5.1 %copy-start = (f32[2,128,16]{1,2,0:T(8,128)S(1)}, f32[2,128,16]{1,2,0:T(8,128)}, u32[]{:S(2)}) copy-start(f32[2,128,16]{1,2,0:T(8,128)} %param.17) | copy-start | bytes 49156
  53.2 5.2 %copy-start.1 = (f32[128,16]{0,1:T(8,128)S(1)}, f32[128,16]{0,1:T(8,128)}, u32[]{:S(2)}) copy-start(f32[128,16]{0,1:T(8,128)} %param.15) | copy-start | bytes 24580
  53.2 5.2 %copy-start.2 = (f32[128,16]{0,1:T(8,128)S(1)}, f32[128,16]{0,1:T(8,128)}, u32[]{:S(2)}) copy-start(f32[128,16]{0,1:T(8,128)} %param.16) | copy-start | bytes 24580

commit v5 on v4

--- a/solution.py
+++ b/solution.py
@@ -235,7 +235,7 @@
     upper = me % 2
     for which, (y_ref, x_ref) in enumerate(((y_lo, x_lo), (y_hi, x_hi))):
 
-        @pl.loop(0, half, unroll=4)
+        @pl.loop(0, half, unroll=8)
         def _(i, which=which, y_ref=y_ref, x_ref=x_ref):
             g = which * half + i
             at = pl.ds(pl.multiple_of(g * size, size), size)
@@ -758,6 +758,11 @@
         if bit == base or last:
             first = sum(parts[: len(made)])
             conv = conv_call(first, groups - first if last else parts[len(made)])
+            if last:
+                rate1 = rate_merge(
+                    1, ty_lo, ty_hi, tx_lo, tx_hi, got1, *rate0[:4], more1, factors
+                )
+                got, rate1 = together(got, rate1)
             got, conv = together(got, conv)
             made.append(conv)
         outs = [state(quarter)] * 2
@@ -780,9 +785,6 @@
     into_y, into_x = into
     convs, lags = zip(*made)
     calls = len(convs)
-    rate1 = rate_merge(
-        1, ty_lo, ty_hi, tx_lo, tx_hi, got1, *rate0[:4], more1, factors
-    )
     total = pl.pallas_call(
         functools.partial(total_kernel, calls),
         out_shape=shape((4, groups, LANES), F32),

time: 59.5 us -> 58.8 us (0.988)
  no operation moved by 1% of the time
where the time goes in v5:
time: 58.8 us; the launch traced here: 58.6 us
  Pallas kernels  35 us (60%)
  starting transfers between devices  15 us (26%)
  waiting for transfers between devices  7.75 us (13%)
  between operations  0.8 us (1%)
    ppermute x12, starting transfers between devices, swap(): return lax.ppermute(value, 'seq', [(i, i ^ bit) for i in range(count)])  15 us
    pallas_call x3, Pallas kernels, conv_call(): pl.pallas_call(functools.partial(conv_kernel, members, modes, first, UNRO...  13.1 us
    pallas_call x1, Pallas kernels, body(): pl.pallas_call(functools.partial(states_kernel, members, modes, count), o...  8.89 us
    ppermute x12, waiting for transfers between devices, swap(): return lax.ppermute(value, 'seq', [(i, i ^ bit) for i in range(count)])  7.75 us
    pallas_call x1, Pallas kernels, body(): pl.pallas_call(finish_kernel, out_shape=(shape(wide, BF16), shape(wide, B...  5.12 us
    pallas_call x1, Pallas kernels, body(): pl.pallas_call(functools.partial(rates_kernel, members, modes), out_shape...  2.09 us
    pallas_call x1, Pallas kernels, body(): pl.pallas_call(product_kernel, out_shape=shape(wide, BF16), in_specs=vmem...  2.04 us
    pallas_call x1, Pallas kernels, body(): pl.pallas_call(functools.partial(cross_kernel, members, modes, calls), ou...  1.9 us
  transfers between devices with their start and end apart: 12, of which 9 were waited for; matrix products, arithmetic and copies ran while one was open for 0% of the time, Pallas kernels for 42%

profile of v5, /device:TPU:0, one launch (start us, length us, event | category | flops | bytes accessed | tf_op | source)
XLA Modules:
  0.0 58.6 jit_solution(17775985197583113343)
XLA Ops:
  0.6 8.9 %shard_map.136 = (bf16[4096,128]{1,0:T(8,128)(2,1)S(1)}, bf16[4096,128]{1,0:T(8,128)(2,1)S(1)}, f32[8,2,32,128]{3,2,1,0:T(8,128)S(1)}, f32[8,2,32,128]{3,2,1,0:T...) custom-call(s32[32,128]{1,0:T(8,128)} %bitcast.13, ...), custom_call_target="tpu_custom_call" | custom-call | tf_op jit(solution)/shard_map/pallas_call | solution.py:657
  9.5 0.6 collective-permute-start
  10.1 1.5 %collective-permute-done.got_ref.near_ref = f32[16,2,32,128]{3,2,1,0:T(8,128)S(1)} collective-permute-done((f32[16,2,32,128]{3,2,1,0:T(8,128)S(1)}, f32[16,2,32,128]{3,2,1,0:T(8,128)S(1)}, u32[]{:S(2)}, u32[]{:S(2)}) %collective-permute-start) | collective-permute-done | bytes 524320 | tf_op jit(solution)/shard_map/ppermute | solution.py:625
  11.6 0.1 shard_map.137
  11.8 2.9 %collective-permute-start.1 = (f32[8,2,32,128]{3,2,1,0:T(8,128)S(1)}, f32[8,2,32,128]{3,2,1,0:T(8,128)S(1)}, u32[]{:S(2)}, u32[]{:S(2)}) collective-permute-start(f32[8,2,32,128]{3,2,1,0:T(8,128)S(1)} %get-tuple-element.112), channel_id=1, source_target_pairs={{0,2},{1,3},{2,0},{3,1},{4,6},{5,7},{6,4},{7,5},{8,10},{9,11},{10,... | collective-permute-start | bytes 786440 | tf_op jit(solution)/shard_map/ppermute | solution.py:625
  14.7 2.1 %shard_map.138 = (f32[8,2,32,128]{3,2,1,0:T(8,128)S(1)}, f32[8,2,32,128]{3,2,1,0:T(8,128)S(1)}, f32[8,2,32,128]{3,2,1,0:T(8,128)S(1)}, f32[8,2,32,128]{3,2,1,0:T(8,128)S(1)}, f32[24,2,32,128]{3,2,1,0:T(8,128)S(1)}) custom-call(bf16[4096,128]{1,0:T(8,128)(2,1)S(1)} %get-tuple-element.150.gate_ref, bf16[4096,128]{1,0:T(8,128)(2,1)S(1)} %get-tuple-element.151.mixed_ref, ...), custom_call_target="tpu_custom_call" | custom-call | flops 2000000 | bytes 1024 | tf_op jit(solution)/shard_map/pallas_call | solution.py:731
  16.8 4.0 %shard_map.139 = (f32[1280,128]{1,0:T(8,128)S(1)}, f32[5,4,128]{2,1,0:T(4,128)S(1)}) custom-call(bf16[4096,128]{1,0:T(8,128)(2,1)S(1)} %get-tuple-element.150.gate_ref, bf16[4096,128]{1,0:T(8,128)(2,1)S(1)} %get-tuple-element.151.mixed_ref, f32[16,40,128]{2,1,0:T(8,128)S(1)} %get-tuple-element.115.re_ref, f32[16,40,128]{2,1,0:T(8,128)S(1)} %get-tuple-element.116.im_ref), custom_call_target="tpu_custom_call" | custom-call | flops 5000000 | bytes 5120 | tf_op jit(solution)/shard_map/pallas_call | solution.py:687
  20.8 0.5 collective-permute-done.1.got_ref
  21.3 0.0 collective-permute-start.3
  21.3 0.1 shard_map.140.total_ref.yx_ref
  21.4 1.9 %collective-permute-start.2 = (f32[2,4,2,32,128]{4,3,2,1,0:T(8,128)S(1)}, f32[2,4,2,32,128]{4,3,2,1,0:T(8,128)S(1)}, u32[]{:S(2)}, u32[]{:S(2)}) collective-permute-start(f32[2,4,2,32,128]{4,3,2,1,0:T(8,128)S(1)} %shard_map.140.total_ref.yx_ref), channel_id=1, source_target_pairs={{0,4},{1,5},{2,6},{3,7},{4,0},{5,1},{6,2},{7,3},{8,12},{9,13},{10,... | collective-permute-start | bytes 786440 | tf_op jit(solution)/shard_map/ppermute | solution.py:625
  23.2 0.3 collective-permute-done.3.more_ref
  23.6 0.3 shard_map.141
  23.9 1.8 %collective-permute-start.5 = (f32[12,2,32,128]{3,2,1,0:T(8,128)S(1)}, f32[12,2,32,128]{3,2,1,0:T(8,128)S(1)}, u32[]{:S(2)}, u32[]{:S(2)}) collective-permute-start(f32[12,2,32,128]{3,2,1,0:T(8,128)S(1)} %get-tuple-element.146), channel_id=1, source_target_pairs={{0,2},{1,3},{2,0},{3,1},{4,6},{5,7},{6,4},{7,5},{8,10},{9,11},{10,... | collective-permute-start | bytes 1179656 | tf_op jit(solution)/shard_map/ppermute | solution.py:625
  25.7 4.0 %shard_map.142 = (f32[1280,128]{1,0:T(8,128)S(1)}, f32[5,4,128]{2,1,0:T(4,128)S(1)}) custom-call(bf16[4096,128]{1,0:T(8,128)(2,1)S(1)} %get-tuple-element.150.gate_ref, bf16[4096,128]{1,0:T(8,128)(2,1)S(1)} %get-tuple-element.151.mixed_ref, f32[16,40,128]{2,1,0:T(8,128)S(1)} %get-tuple-element.115.re_ref, f32[16,40,128]{2,1,0:T(8,128)S(1)} %get-tuple-element.116.im_ref), custom_call_target="tpu_custom_call" | custom-call | flops 5000000 | bytes 5120 | tf_op jit(solution)/shard_map/pallas_call | solution.py:687
  29.7 0.5 collective-permute-done.2.got_ref
  30.2 0.1 shard_map.143
  30.3 2.8 %collective-permute-start.4 = (f32[1,4,2,32,128]{4,3,2,1,0:T(8,128)S(1)}, f32[1,4,2,32,128]{4,3,2,1,0:T(8,128)S(1)}, u32[]{:S(2)}, u32[]{:S(2)}) collective-permute-start(f32[1,4,2,32,128]{4,3,2,1,0:T(8,128)S(1)} %get-tuple-element.141), channel_id=1, source_target_pairs={{0,8},{1,9},{2,10},{3,11},{4,12},{5,13},{6,14},{7,15},{8,0},{9,1},... | collective-permute-start | bytes 393224 | tf_op jit(solution)/shard_map/ppermute | solution.py:625
  33.1 5.1 %shard_map.145 = (f32[1536,128]{1,0:T(8,128)S(1)}, f32[6,4,128]{2,1,0:T(4,128)S(1)}) custom-call(bf16[4096,128]{1,0:T(8,128)(2,1)S(1)} %get-tuple-element.150.gate_ref, bf16[4096,128]{1,0:T(8,128)(2,1)S(1)} %get-tuple-element.151.mixed_ref, f32[16,40,128]{2,1,0:T(8,128)S(1)} %get-tuple-element.115.re_ref, f32[16,40,128]{2,1,0:T(8,128)S(1)} %get-tuple-element.116.im_ref), custom_call_target="tpu_custom_call" | custom-call | flops 6000000 | bytes 6144 | tf_op jit(solution)/shard_map/pallas_call | solution.py:687
  38.2 0.0 collective-permute-done.5.more_ref
  38.2 0.2 shard_map.144
  38.4 0.9 %collective-permute-done.4.got_ref = f32[1,4,2,32,128]{4,3,2,1,0:T(8,128)S(1)} collective-permute-done((f32[1,4,2,32,128]{4,3,2,1,0:T(8,128)S(1)}, f32[1,4,2,32,128]{4,3,2,1,0:T(8,128)S(1)}, u32[]{:S(2)}, u32[]{:S(2)}) %collective-permute-start.4) | collective-permute-done | bytes 131104 | tf_op jit(solution)/shard_map/ppermute | solution.py:625
  39.3 0.1 shard_map.147.a_ref
  39.5 1.6 %collective-permute-start.6 = (f32[4,2,32,128]{3,2,1,0:T(8,128)S(1)}, f32[4,2,32,128]{3,2,1,0:T(8,128)S(1)}, u32[]{:S(2)}, u32[]{:S(2)}) collective-permute-start(f32[4,2,32,128]{3,2,1,0:T(8,128)S(1)} %get-tuple-element.165.into_y.into_ref), channel_id=1, source_target_pairs={{0,2},{1,3},{2,0},{3,1},{4,6},{5,7},{6,4},{7,5},{8,10},{9,11},{10,... | collective-permute-start | bytes 393224 | tf_op jit(solution)/shard_map/ppermute | solution.py:625
  41.1 0.0 collective-permute-start.7
  41.1 1.2 %collective-permute-done.7.b_ref = f32[4,16,128]{2,1,0:T(8,128)S(1)} collective-permute-done((f32[4,16,128]{2,1,0:T(8,128)S(1)}, f32[4,16,128]{2,1,0:T(8,128)S(1)}, u32[]{:S(2)}, u32[]{:S(2)}) %collective-permute-start.7) | collective-permute-done | bytes 32800 | tf_op jit(solution)/shard_map/ppermute | solution.py:625
  42.3 0.5 collective-permute-start.8
  42.8 2.0 %shard_map.149 = bf16[4096,128]{1,0:T(8,128)(2,1)} custom-call(bf16[4096,128]{1,0:T(8,128)(2,1)S(1)} %get-tuple-element.168.a_ref, bf16[4096,128]{1,0:T(8,128)(2,1)} %b_hbm.1), custom_call_target="tpu_custom_call" | custom-call | flops 1000000 | bytes 1024 | tf_op jit(solution)/shard_map/pallas_call | solution.py:810
  44.8 1.4 %collective-permute-done.8.b_ref = f32[4,16,128]{2,1,0:T(8,128)S(1)} collective-permute-done((f32[4,16,128]{2,1,0:T(8,128)S(1)}, f32[4,16,128]{2,1,0:T(8,128)S(1)}, u32[]{:S(2)}, u32[]{:S(2)}) %collective-permute-start.8) | collective-permute-done | bytes 32800 | tf_op jit(solution)/shard_map/ppermute | solution.py:625
  46.3 0.0 collective-permute-done.6.other_ref
  46.3 0.1 shard_map.151.mine_ref
  46.3 0.1 collective-permute-start.10
  46.4 0.7 %collective-permute-start.9 = (f32[4,16,128]{2,1,0:T(8,128)S(1)}, f32[4,16,128]{2,1,0:T(8,128)S(1)}, u32[]{:S(2)}, u32[]{:S(2)}) collective-permute-start(f32[4,16,128]{2,1,0:T(8,128)S(1)} %shard_map.150.a_ref), channel_id=1, source_target_pairs={{0,4},{1,5},{2,6},{3,7},{4,0},{5,1},{6,2},{7,3},{8,12},{9,13},{10,... | collective-permute-start | bytes 98312 | tf_op jit(solution)/shard_map/ppermute | solution.py:625
  47.2 0.8 %collective-permute-done.10.other_ref = f32[8,2,32,128]{3,2,1,0:T(8,128)S(1)} collective-permute-done((f32[8,2,32,128]{3,2,1,0:T(8,128)S(1)}, f32[8,2,32,128]{3,2,1,0:T(8,128)S(1)}, u32[]{:S(2)}, u32[]{:S(2)}) %collective-permute-start.10) | collective-permute-done | bytes 262176 | tf_op jit(solution)/shard_map/ppermute | solution.py:625
  47.9 1.9 %shard_map.152.grouped = f32[4096,128]{1,0:T(8,128)S(1)} custom-call(f32[8,2,32,128]{3,2,1,0:T(8,128)S(1)} %shard_map.151.mine_ref, f32[8,2,32,128]{3,2,1,0:T(8,128)S(1)} %collective-permute-done.10.other_ref, f32[16,2,32,128]{3,2,1,0:T(8,128)S(1)} %collective-permute-done.got_ref.near_ref, f32[24,2,32,128]{3,2,1,0:T(8,128)S(1)} %collective-permute-done.3.more_ref, ...), custom_call_target="tpu_custom_call" | custom-call | flops 1000000 | bytes 1024 | tf_op jit(solution)/shard_map/pallas_call | solution.py:832
  49.8 0.6 collective-permute-done.9.b_ref
  50.4 2.1 %collective-permute-start.11 = (f32[4,16,128]{2,1,0:T(8,128)S(1)}, f32[4,16,128]{2,1,0:T(8,128)S(1)}, u32[]{:S(2)}, u32[]{:S(2)}) collective-permute-start(f32[4,16,128]{2,1,0:T(8,128)S(1)} %shard_map.153.total_ref), channel_id=1, source_target_pairs={{0,8},{1,9},{2,10},{3,11},{4,12},{5,13},{6,14},{7,15},{8,0},{9,1},... | collective-permute-start | bytes 98312 | tf_op jit(solution)/shard_map/ppermute | solution.py:625
  52.6 0.0 copy-start
  52.6 0.0 copy-start.1
  52.6 0.0 copy-start.2
  52.6 5.1 %shard_map.154 = (bf16[4096,128]{1,0:T(8,128)(2,1)}, bf16[4096,128]{1,0:T(8,128)(2,1)}) custom-call(s32[32,128]{1,0:T(8,128)S(1)} %get-tuple-element.180.pos_ref, f32[4096,128]{1,0:T(8,128)S(1)} %shard_map.152.grouped, bf16[4096,128]{1,0:T(8,128)(2,1)S(1)} %get-tuple-element.182.k_ref, bf16[4096,128]{1,0:T(8,128)(2,1)S(1)} %get-tuple-element.183.v_ref), custom_call_target="tpu_custom_call" | custom-call | flops 1000000 | bytes 1024 | tf_op jit(solution)/shard_map/pallas_call | solution.py:848
  57.7 0.0 collective-permute-done.11.last_ref
  57.7 0.0 copy-done
  57.7 0.0 copy-done.1
  57.7 0.0 copy-done.2
  57.7 0.8 %shard_map.155 = (f32[16,128]{1,0:T(8,128)}, f32[16,128]{1,0:T(8,128)}, f32[2,16,128]{2,1,0:T(8,128)}) custom-call(f32[4,16,128]{2,1,0:T(8,128)S(1)} %shard_map.153.total_ref, f32[4,16,128]{2,1,0:T(8,128)S(1)} %collective-permute-done.11.last_ref, f32[16,128]{1,0:T(8,128)S(1)} %bitcast.10, f32[16,128]{1,0:T(8,128)S(1)} %bitcast.12, f32[2,16,128]{2,1,0:T(8,128)S(1)} %bitcast.8), custom_call_target="tpu_custom_call" | custom-call | tf_op jit(solution)/shard_map/pallas_call | solution.py:860
  (4 shorter events, 0.1 us)
Async XLA Ops:
  9.5 2.1 %collective-permute-start = (f32[16,2,32,128]{3,2,1,0:T(8,128)S(1)}, f32[16,2,32,128]{3,2,1,0:T(8,128)S(1)}, u32[]{:S(2)}, u32[]{:S(2)}) collective-permute-start(f32[16,2,32,128]{3,2,1,0:T(8,128)S(1)} %get-tuple-element.103), channel_id=1, source_target_pairs={{0,1},{1,0},{2,3},{3,2},{4,5},{5,4},{6,7},{7,6},{8,9},{9,8},{10,11... | collective-permute-start | bytes 1572872 | tf_op jit(solution)/shard_map/ppermute | solution.py:625
  11.8 9.5 %collective-permute-start.1 = (f32[8,2,32,128]{3,2,1,0:T(8,128)S(1)}, f32[8,2,32,128]{3,2,1,0:T(8,128)S(1)}, u32[]{:S(2)}, u32[]{:S(2)}) collective-permute-start(f32[8,2,32,128]{3,2,1,0:T(8,128)S(1)} %get-tuple-element.112), channel_id=1, source_target_pairs={{0,2},{1,3},{2,0},{3,1},{4,6},{5,7},{6,4},{7,5},{8,10},{9,11},{10,... | collective-permute-start | bytes 786440 | tf_op jit(solution)/shard_map/ppermute | solution.py:625
  21.3 2.3 %collective-permute-start.3 = (f32[24,2,32,128]{3,2,1,0:T(8,128)S(1)}, f32[24,2,32,128]{3,2,1,0:T(8,128)S(1)}, u32[]{:S(2)}, u32[]{:S(2)}) collective-permute-start(f32[24,2,32,128]{3,2,1,0:T(8,128)S(1)} %get-tuple-element.130), channel_id=1, source_target_pairs={{0,1},{1,0},{2,3},{3,2},{4,5},{5,4},{6,7},{7,6},{8,9},{9,8},{10,11... | collective-permute-start | bytes 2359304 | tf_op jit(solution)/shard_map/ppermute | solution.py:625
  21.4 8.8 %collective-permute-start.2 = (f32[2,4,2,32,128]{4,3,2,1,0:T(8,128)S(1)}, f32[2,4,2,32,128]{4,3,2,1,0:T(8,128)S(1)}, u32[]{:S(2)}, u32[]{:S(2)}) collective-permute-start(f32[2,4,2,32,128]{4,3,2,1,0:T(8,128)S(1)} %shard_map.140.total_ref.yx_ref), channel_id=1, source_target_pairs={{0,4},{1,5},{2,6},{3,7},{4,0},{5,1},{6,2},{7,3},{8,12},{9,13},{10,... | collective-permute-start | bytes 786440 | tf_op jit(solution)/shard_map/ppermute | solution.py:625
  23.9 14.3 %collective-permute-start.5 = (f32[12,2,32,128]{3,2,1,0:T(8,128)S(1)}, f32[12,2,32,128]{3,2,1,0:T(8,128)S(1)}, u32[]{:S(2)}, u32[]{:S(2)}) collective-permute-start(f32[12,2,32,128]{3,2,1,0:T(8,128)S(1)} %get-tuple-element.146), channel_id=1, source_target_pairs={{0,2},{1,3},{2,0},{3,1},{4,6},{5,7},{6,4},{7,5},{8,10},{9,11},{10,... | collective-permute-start | bytes 1179656 | tf_op jit(solution)/shard_map/ppermute | solution.py:625
  30.3 9.0 %collective-permute-start.4 = (f32[1,4,2,32,128]{4,3,2,1,0:T(8,128)S(1)}, f32[1,4,2,32,128]{4,3,2,1,0:T(8,128)S(1)}, u32[]{:S(2)}, u32[]{:S(2)}) collective-permute-start(f32[1,4,2,32,128]{4,3,2,1,0:T(8,128)S(1)} %get-tuple-element.141), channel_id=1, source_target_pairs={{0,8},{1,9},{2,10},{3,11},{4,12},{5,13},{6,14},{7,15},{8,0},{9,1},... | collective-permute-start | bytes 393224 | tf_op jit(solution)/shard_map/ppermute | solution.py:625
  39.5 6.8 %collective-permute-start.6 = (f32[4,2,32,128]{3,2,1,0:T(8,128)S(1)}, f32[4,2,32,128]{3,2,1,0:T(8,128)S(1)}, u32[]{:S(2)}, u32[]{:S(2)}) collective-permute-start(f32[4,2,32,128]{3,2,1,0:T(8,128)S(1)} %get-tuple-element.165.into_y.into_ref), channel_id=1, source_target_pairs={{0,2},{1,3},{2,0},{3,1},{4,6},{5,7},{6,4},{7,5},{8,10},{9,11},{10,... | collective-permute-start | bytes 393224 | tf_op jit(solution)/shard_map/ppermute | solution.py:625
  41.1 1.2 %collective-permute-start.7 = (f32[4,16,128]{2,1,0:T(8,128)S(1)}, f32[4,16,128]{2,1,0:T(8,128)S(1)}, u32[]{:S(2)}, u32[]{:S(2)}) collective-permute-start(f32[4,16,128]{2,1,0:T(8,128)S(1)} %shard_map.147.a_ref), channel_id=1, source_target_pairs={{0,1},{1,0},{2,3},{3,2},{4,5},{5,4},{6,7},{7,6},{8,9},{9,8},{10,11... | collective-permute-start | bytes 98312 | tf_op jit(solution)/shard_map/ppermute | solution.py:625
  42.3 3.9 %collective-permute-start.8 = (f32[4,16,128]{2,1,0:T(8,128)S(1)}, f32[4,16,128]{2,1,0:T(8,128)S(1)}, u32[]{:S(2)}, u32[]{:S(2)}) collective-permute-start(f32[4,16,128]{2,1,0:T(8,128)S(1)} %shard_map.148.a_ref), channel_id=1, source_target_pairs={{0,2},{1,3},{2,0},{3,1},{4,6},{5,7},{6,4},{7,5},{8,10},{9,11},{10,... | collective-permute-start | bytes 98312 | tf_op jit(solution)/shard_map/ppermute | solution.py:625
  46.3 1.6 %collective-permute-start.10 = (f32[8,2,32,128]{3,2,1,0:T(8,128)S(1)}, f32[8,2,32,128]{3,2,1,0:T(8,128)S(1)}, u32[]{:S(2)}, u32[]{:S(2)}) collective-permute-start(f32[8,2,32,128]{3,2,1,0:T(8,128)S(1)} %shard_map.151.mine_ref), channel_id=1, source_target_pairs={{0,1},{1,0},{2,3},{3,2},{4,5},{5,4},{6,7},{7,6},{8,9},{9,8},{10,11... | collective-permute-start | bytes 786440 | tf_op jit(solution)/shard_map/ppermute | solution.py:625
  46.4 4.0 %collective-permute-start.9 = (f32[4,16,128]{2,1,0:T(8,128)S(1)}, f32[4,16,128]{2,1,0:T(8,128)S(1)}, u32[]{:S(2)}, u32[]{:S(2)}) collective-permute-start(f32[4,16,128]{2,1,0:T(8,128)S(1)} %shard_map.150.a_ref), channel_id=1, source_target_pairs={{0,4},{1,5},{2,6},{3,7},{4,0},{5,1},{6,2},{7,3},{8,12},{9,13},{10,... | collective-permute-start | bytes 98312 | tf_op jit(solution)/shard_map/ppermute | solution.py:625
  50.4 7.3 %collective-permute-start.11 = (f32[4,16,128]{2,1,0:T(8,128)S(1)}, f32[4,16,128]{2,1,0:T(8,128)S(1)}, u32[]{:S(2)}, u32[]{:S(2)}) collective-permute-start(f32[4,16,128]{2,1,0:T(8,128)S(1)} %shard_map.153.total_ref), channel_id=1, source_target_pairs={{0,8},{1,9},{2,10},{3,11},{4,12},{5,13},{6,14},{7,15},{8,0},{9,1},... | collective-permute-start | bytes 98312 | tf_op jit(solution)/shard_map/ppermute | solution.py:625
  52.6 5.1 %copy-start = (f32[2,128,16]{1,2,0:T(8,128)S(1)}, f32[2,128,16]{1,2,0:T(8,128)}, u32[]{:S(2)}) copy-start(f32[2,128,16]{1,2,0:T(8,128)} %param.17) | copy-start | bytes 49156
  52.6 5.2 %copy-start.1 = (f32[128,16]{0,1:T(8,128)S(1)}, f32[128,16]{0,1:T(8,128)}, u32[]{:S(2)}) copy-start(f32[128,16]{0,1:T(8,128)} %param.15) | copy-start | bytes 24580
  52.6 5.2 %copy-start.2 = (f32[128,16]{0,1:T(8,128)S(1)}, f32[128,16]{0,1:T(8,128)}, u32[]{:S(2)}) copy-start(f32[128,16]{0,1:T(8,128)} %param.16) | copy-start | bytes 24580
